TPU v7x, 768 devices: a whole 4x8x12 slice. The times are simulated.
768 devices in a mesh: ctx: 96 (over y, z), head: 8 (over x, core).
Axes of the slice: x: 4, y: 8, z: 12, core: 2. Of those that a mesh axis runs over, the one named last changes fastest.
Arguments:
- lin_q: bfloat16 [12288, 4096], P('ctx', 'head'), may hold values from -5 to 5
- lin_k: bfloat16 [12288, 4096], P('ctx', 'head'), may hold values from -5 to 5
- lin_v: bfloat16 [12288, 4096], P('ctx', 'head'), may hold values from -13 to 13
- win_q: bfloat16 [12288, 4096], P('ctx', 'head'), may hold values from -5 to 5
- win_k: bfloat16 [12288, 4096], P('ctx', 'head'), may hold values from -5 to 5
- win_v: bfloat16 [12288, 4096], P('ctx', 'head'), may hold values from -5 to 5
- grad_out: bfloat16 [12288, 4096], P('ctx', 'head'), may hold values from -5 to 5
Outputs:
- mixed: bfloat16 [12288, 4096], P('ctx', 'head')
- grad_lin_q: bfloat16 [12288, 4096], P('ctx', 'head')
- grad_lin_k: bfloat16 [12288, 4096], P('ctx', 'head')
- grad_lin_v: bfloat16 [12288, 4096], P('ctx', 'head')
- grad_win_q: bfloat16 [12288, 4096], P('ctx', 'head')
- grad_win_k: bfloat16 [12288, 4096], P('ctx', 'head')
- grad_win_v: bfloat16 [12288, 4096], P('ctx', 'head')
All inputs are finite; a program needn't handle non-finite values.
Results may differ from a plain program's by a relative error of at most 0.0084.
Values may be sent and summed in bfloat16 or wider, within the bound.
No kernel may reach another device: no remote copies, remote signals or barrier semaphores. Data moves between devices by JAX's collectives and lax.ppermute only.
A program may use at most 64 MiB of HBM per device.

v0:
```python
from functools import partial
import math

import jax
import jax.numpy as jnp
from jax import lax
from jax.sharding import PartitionSpec as P

HD = 128
WIN = 512


PRECISE = lax.Precision.HIGHEST
NORM_EPS = 1e-05


def prefix_2(value, axis, combine, identity, reverse):
    count, mine = (lax.axis_size(axis), lax.axis_index(axis))
    everything = lax.all_gather(value, axis)
    start = jnp.broadcast_to(jnp.asarray(identity, value.dtype), value.shape)

    def lap(k, before):
        at = count - 1 - k if reverse else k
        reached = at > mine if reverse else at < mine
        new = combine(before, everything[at])
        return jnp.where(reached, new, before)

    return lax.fori_loop(0, count, lap, start)


def passed_along(block, axis, distance):
    devices = range(lax.axis_size(axis))
    route = [(i - distance, i) for i in devices if i - distance in devices]
    return lax.ppermute(block, axis, route)


def shortened(value):
    return jax.tree.map(lambda a: a.astype(jnp.bfloat16) if a.dtype == jnp.float32 else a, value)


def add_states(earlier, later):
    return earlier + later


def causal_rows(block_rows):
    positions = jnp.arange(block_rows, dtype=jnp.int32)
    return positions[:, None] >= positions[None, :]


def heads_first(array):
    return jnp.moveaxis(array, 1, 0)


def heads_second(array):
    return jnp.moveaxis(array, 0, 1)


def linear_forward(query, keys, values, before):
    causal = causal_rows(query.shape[0])
    scores = jnp.einsum("thd,shd->hts", query, keys, preferred_element_type=jnp.float32)
    scores = jnp.where(causal[None], scores, 0.0)
    inner = jnp.einsum("hts,shd->thd", scores, values.astype(jnp.float32), precision=PRECISE)
    result = inner + jnp.einsum(
        "thd,hde->the", query.astype(jnp.float32), before, precision=PRECISE
    )
    return (result, scores)


def linear_backward(query, keys, values, cotangent, scores, before, after):
    causal = causal_rows(query.shape[0])
    cotangent_f = cotangent.astype(jnp.float32)
    dprobs = jnp.einsum("the,she->hts", cotangent, values, preferred_element_type=jnp.float32)
    dprobs = jnp.where(causal[None], dprobs, 0.0)
    query_grad = jnp.einsum("hts,shd->thd", dprobs, keys.astype(jnp.float32), precision=PRECISE)
    query_grad = query_grad + jnp.einsum("the,hde->thd", cotangent_f, before, precision=PRECISE)
    key_grad = jnp.einsum("hts,thd->shd", dprobs, query.astype(jnp.float32), precision=PRECISE)
    key_grad = key_grad + jnp.einsum(
        "she,hde->shd", values.astype(jnp.float32), after, precision=PRECISE
    )
    value_grad = jnp.einsum("hts,the->she", scores, cotangent_f, precision=PRECISE)
    value_grad = value_grad + jnp.einsum(
        "shd,hde->she", keys.astype(jnp.float32), after, precision=PRECISE
    )
    return (query_grad, key_grad, value_grad)


def query_head(pieces, first_pos):
    query, keys, values, upstream = pieces
    row_count = query.shape[0]
    ext_count = keys.shape[0]
    window = ext_count - row_count
    score_scale = 1.0 / math.sqrt(query.shape[1])
    scores = jnp.einsum("td,sd->ts", query, keys, preferred_element_type=jnp.float32) * score_scale
    query_pos = first_pos + jnp.arange(row_count, dtype=jnp.int32)
    key_pos = first_pos - window + jnp.arange(ext_count, dtype=jnp.int32)
    allowed = (
        (key_pos[None, :] >= 0)
        & (key_pos[None, :] <= query_pos[:, None])
        & (key_pos[None, :] > query_pos[:, None] - window)
    )
    scores = jnp.where(allowed, scores, -jnp.inf)
    row_max = jnp.max(scores, axis=1, keepdims=True)
    log_total = row_max[:, 0] + jnp.log(jnp.sum(jnp.exp(scores - row_max), axis=1))
    probs = jnp.exp(scores - log_total[:, None])
    weights_low = probs.astype(jnp.bfloat16)
    output = jnp.einsum("ts,sd->td", weights_low, values, preferred_element_type=jnp.float32)
    dprobs = jnp.einsum("td,sd->ts", upstream, values, preferred_element_type=jnp.float32)
    row_dot = jnp.sum(probs * dprobs, axis=1)
    dscores = (probs * (dprobs - row_dot[:, None]) * score_scale).astype(jnp.bfloat16)
    query_grad = jnp.einsum("ts,sd->td", dscores, keys, preferred_element_type=jnp.float32)
    return (output, query_grad, log_total, row_dot)


def key_head(pieces, first_pos, total_rows):
    query, upstream, totals, dots, keys, values = pieces
    row_count = keys.shape[0]
    ext_count = query.shape[0]
    window = ext_count - row_count
    score_scale = 1.0 / math.sqrt(query.shape[1])
    scores = jnp.einsum("td,sd->ts", query, keys, preferred_element_type=jnp.float32) * score_scale
    query_pos = first_pos + jnp.arange(ext_count, dtype=jnp.int32)
    key_pos = first_pos + jnp.arange(row_count, dtype=jnp.int32)
    allowed = (
        (query_pos[:, None] < total_rows)
        & (key_pos[None, :] <= query_pos[:, None])
        & (key_pos[None, :] > query_pos[:, None] - window)
    )
    probs = jnp.where(allowed, jnp.exp(scores - totals[:, None]), 0.0)
    weights_low = probs.astype(jnp.bfloat16)
    dprobs = jnp.einsum("td,sd->ts", upstream, values, preferred_element_type=jnp.float32)
    dscores = (probs * (dprobs - dots[:, None]) * score_scale).astype(jnp.bfloat16)
    key_grad = jnp.einsum("ts,td->sd", dscores, query, preferred_element_type=jnp.float32)
    value_grad = jnp.einsum("ts,td->sd", weights_low, upstream, preferred_element_type=jnp.float32)
    return (key_grad, value_grad)


def shards(lin_q, lin_k, lin_v, win_q, win_k, win_v, grad_out):
    row_count = lin_q.shape[0]
    head_count = lin_q.shape[1] // HD
    shaped = (row_count, head_count, HD)
    flat = (row_count, head_count * HD)
    span = WIN // row_count
    total_rows = row_count * lax.axis_size("ctx")
    first_pos = lax.axis_index("ctx") * row_count
    lin_query = lin_q.reshape(shaped)
    lin_key = lin_k.reshape(shaped)
    lin_value = lin_v.reshape(shaped)
    zero_state = jnp.zeros((head_count, HD, HD), jnp.float32)
    key_state = jnp.einsum("shd,she->hde", lin_key, lin_value, preferred_element_type=jnp.float32)
    prefix = prefix_2(key_state, "ctx", add_states, zero_state, False)
    lin_out, lin_scores = linear_forward(lin_query, lin_key, lin_value, prefix)
    upstream = grad_out.reshape(shaped).astype(jnp.float32)
    square_sum, cross_sum = lax.psum(
        (jnp.sum(lin_out * lin_out, axis=(1, 2)), jnp.sum(upstream * lin_out, axis=(1, 2))), "head"
    )
    features = head_count * HD * lax.axis_size("head")
    inv_rms = lax.rsqrt(square_sum / features + NORM_EPS)
    lin_dout = (
        inv_rms[:, None, None] * upstream
        - lin_out * (inv_rms**3 * cross_sum / features)[:, None, None]
    ).astype(jnp.bfloat16)
    query_state = jnp.einsum(
        "thd,the->hde", lin_query, lin_dout, preferred_element_type=jnp.float32
    )
    suffix = prefix_2(query_state, "ctx", add_states, zero_state, True)
    grad_q, grad_k, grad_v = linear_backward(
        lin_query, lin_key, lin_value, lin_dout, lin_scores, prefix, suffix
    )
    win_query = win_q.reshape(shaped)
    win_key = win_k.reshape(shaped)
    win_value = win_v.reshape(shaped)
    cotangent = grad_out.reshape(shaped)
    reach_rows = span * row_count

    def relay_keys(passed, unused):
        moved = passed_along((passed[0], passed[1]), "ctx", 1)
        return (moved, moved)

    last_pair, stacked = lax.scan(relay_keys, (win_key, win_value), None, length=span)
    earlier_key = stacked[0][::-1].reshape((reach_rows, head_count, HD))
    earlier_value = stacked[1][::-1].reshape((reach_rows, head_count, HD))
    key_ext = jnp.concatenate([earlier_key, win_key], axis=0)
    value_ext = jnp.concatenate([earlier_value, win_value], axis=0)
    win_out, win_dq, log_total, row_dot = lax.map(
        partial(query_head, first_pos=first_pos),
        (
            heads_first(win_query),
            heads_first(key_ext),
            heads_first(value_ext),
            heads_first(cotangent),
        ),
    )

    def relay_rows(passed, unused):
        moved_rows = passed_along(shortened(passed[0]), "ctx", -1)
        moved_stats = passed_along(passed[1], "ctx", -1)
        return ((moved_rows, moved_stats), (moved_rows, moved_stats))

    last_state, stacked_back = lax.scan(
        relay_rows, ((win_query, cotangent), (log_total, row_dot)), None, length=span
    )
    later_query = stacked_back[0][0].reshape((reach_rows, head_count, HD))
    later_upstream = stacked_back[0][1].reshape((reach_rows, head_count, HD))
    later_total = jnp.moveaxis(stacked_back[1][0], 0, 1).reshape((head_count, reach_rows))
    later_dot = jnp.moveaxis(stacked_back[1][1], 0, 1).reshape((head_count, reach_rows))
    query_ext = jnp.concatenate([win_query, later_query], axis=0)
    upstream_ext = jnp.concatenate([cotangent, later_upstream], axis=0)
    total_ext = jnp.concatenate([log_total, later_total], axis=1)
    dot_ext = jnp.concatenate([row_dot, later_dot], axis=1)
    win_dk, win_dv = lax.map(
        partial(key_head, first_pos=first_pos, total_rows=total_rows),
        (
            heads_first(query_ext),
            heads_first(upstream_ext),
            total_ext,
            dot_ext,
            heads_first(win_key),
            heads_first(win_value),
        ),
    )
    mixed = (
        (lin_out * inv_rms[:, None, None] + heads_second(win_out))
        .astype(jnp.bfloat16)
        .reshape(flat)
    )
    return (
        mixed,
        grad_q.astype(jnp.bfloat16).reshape(flat),
        grad_k.astype(jnp.bfloat16).reshape(flat),
        grad_v.astype(jnp.bfloat16).reshape(flat),
        heads_second(win_dq).astype(jnp.bfloat16).reshape(flat),
        heads_second(win_dk).astype(jnp.bfloat16).reshape(flat),
        heads_second(win_dv).astype(jnp.bfloat16).reshape(flat),
    )


def solution(mesh):
    return jax.shard_map(
        shards,
        mesh=mesh,
        in_specs=(
            P("ctx", "head"),
            P("ctx", "head"),
            P("ctx", "head"),
            P("ctx", "head"),
            P("ctx", "head"),
            P("ctx", "head"),
            P("ctx", "head"),
        ),
        out_specs=(
            P("ctx", "head"),
            P("ctx", "head"),
            P("ctx", "head"),
            P("ctx", "head"),
            P("ctx", "head"),
            P("ctx", "head"),
            P("ctx", "head"),
        ),
        check_vma=False,
    )
```

profile of v0, /device:TPU:6, one launch (start us, length us, event | category | flops | bytes accessed | tf_op | source)
XLA Modules:
  0.0 677.1 jit_solution(7796649743466684802)
XLA Ops:
  8.3 1.8 fusion.76
  13.2 50.1 %while.103 = (s32[]{:T(128)}, bf16[128,4,128]{2,1,0:T(4,128)(2,1)S(1)}, bf16[128,4,128]{2,1,0:T(4,128)(2,1)S(1)}, bf16[4,128,4,128]{3,2,1,0:T(4,128)(2,1)S(1)}, bf16[4,128,4,128]{3,2,1,0:T(4,128)(2,1)S(1)}, /*index=5*/s32[]{:T(128)}) while((s32[]{:T(128)}, bf16[128,4,128]{2,1,0:T(4,128)(2,1)S(1)}, bf16[128,4,128]{2,1,0:T(4,128)(2,1)S(1)}, ...), condition=%wide.region_5.6_spmd, body=%wide.region_4.5_spmd.sunk | while | flops 2 | bytes 2097317 | solution.py:179
  13.2 4.3 collective-permute-start
  17.5 4.3 collective-permute-start.1
  21.9 2.4 collective-permute-done.1
  24.4 4.4 collective-permute-start
  28.8 5.4 collective-permute-start.1
  34.3 3.7 collective-permute-done.1
  38.2 4.4 collective-permute-start
  42.6 4.1 collective-permute-start.1
  46.8 3.9 collective-permute-done.1
  50.9 4.4 collective-permute-start
  55.3 4.5 collective-permute-start.1
  61.1 2.1 collective-permute-done.1
  67.5 9.0 %while.104 = (s32[]{:T(128)}, f32[4,128,128]{1,2,0:T(8,128)}, bf16[4,128,128]{2,1,0:T(8,128)(2,1)S(1)}, f32[4,128]{1,0:T(4,128)S(1)}, f32[4,128]{1,0:T(4,128)S(1...) while((s32[]{:T(128)}, f32[4,128,128]{1,2,0:T(8,128)}, ...), condition=%wide.region_10.11_spmd, body=%wide.region_6.10_spmd.sunk | while | flops 85444480 | bytes 3168017 | solution.py:184
  76.5 159.5 %all-gather.5.cloned.1.call-done = f32[384,128,128]{2,1,0:T(8,128)} async-done(((f32[4,128,128]{2,1,0:T(8,128)}), f32[384,128,128]{2,1,0:T(8,128)}) %all-gather.5.cloned.1.call-update) | async-done | bytes 25165840 | tf_op jit(solution)/shard_map/all_gather | solution.py:19
  236.0 102.2 %while.107 = (s32[]{:T(128)}, f32[4,128,128]{2,1,0:T(8,128)S(1)}, s32[]{:T(128)}, f32[96,4,128,128]{3,2,1,0:T(8,128)}, s32[]{:T(128)}, /*index=5*/s32[]{:T(128)}) while((s32[]{:T(128)}, f32[4,128,128]{2,1,0:T(8,128)S(1)}, s32[]{:T(128)}, f32[96,4,128,128]{3,2,1,0:T(8,128)}, s32[]{:T(128)}, /*index=5*/s32[]{:T(128)}) %tuple.205), condition=%wide.region_1.2_spmd.clone, body=%wide.region_0.1_spmd.clone.sunk | while | flops 196612 | bytes 786525 | solution.py:28
  338.6 10.0 %all-reduce = (f32[128]{0:T(128)S(1)}, f32[128]{0:T(128)S(1)}) all-reduce(f32[128]{0:T(128)S(1)} %get-tuple-element.731, f32[128]{0:T(128)S(1)} %get-tuple-element.730), channel_id=1, replica_groups=mesh['ctx'=96,'head'=8] {'head'}, use_global_device_ids=true, to_apply=%region_3.4 | all-reduce | flops 256 | bytes 2048 | tf_op jit(solution)/shard_map/psum | solution.py:153
  351.0 58.2 %while.105 = (s32[]{:T(128)}, bf16[128,4,128]{2,1,0:T(4,128)(2,1)S(1)}, bf16[128,4,128]{2,1,0:T(4,128)(2,1)S(1)}, f32[4,128]{1,0:T(4,128)S(1)}, f32[4,128]{1,0:T...) while((s32[]{:T(128)}, ...), condition=%wide.region_16.17_spmd, body=%wide.region_15.16_spmd.sunk | while | flops 2 | bytes 2130205 | solution.py:199
  351.1 1.3 collective-permute-start.4
  352.4 1.3 collective-permute-start.2
  353.7 1.3 collective-permute-start.3
  355.0 1.3 collective-permute-start.5
  356.5 7.2 %collective-permute-done.5 = f32[4,128]{1,0:T(4,128)S(1)} collective-permute-done((f32[4,128]{1,0:T(4,128)S(1)}, f32[4,128]{1,0:T(4,128)S(1)}, u32[]{:S(2)}, u32[]{:S(2)}) %collective-permute-start.5) | collective-permute-done | bytes 2080 | tf_op jit(solution)/shard_map/while/body/eval_jaxpr/ppermute | solution.py:34
  364.6 1.3 collective-permute-start.4
  365.9 1.3 collective-permute-start.2
  370.1 9.8 %collective-permute-done.5 = f32[4,128]{1,0:T(4,128)S(1)} collective-permute-done((f32[4,128]{1,0:T(4,128)S(1)}, f32[4,128]{1,0:T(4,128)S(1)}, u32[]{:S(2)}, u32[]{:S(2)}) %collective-permute-start.5) | collective-permute-done | bytes 2080 | tf_op jit(solution)/shard_map/while/body/eval_jaxpr/ppermute | solution.py:34
  386.3 9.2 %collective-permute-done.5 = f32[4,128]{1,0:T(4,128)S(1)} collective-permute-done((f32[4,128]{1,0:T(4,128)S(1)}, f32[4,128]{1,0:T(4,128)S(1)}, u32[]{:S(2)}, u32[]{:S(2)}) %collective-permute-start.5) | collective-permute-done | bytes 2080 | tf_op jit(solution)/shard_map/while/body/eval_jaxpr/ppermute | solution.py:34
  401.9 6.5 collective-permute-done.5
  410.4 7.9 %while.106 = (s32[]{:T(128)}, bf16[4,128,128]{2,1,0:T(8,128)(2,1)S(1)}, bf16[4,128,128]{2,1,0:T(8,128)(2,1)S(1)}, s32[]{:T(128)}, bf16[4,640,128]{2,1,0:T(8,128)...) while((s32[]{:T(128)}, ...), condition=%wide.region_18.19_spmd, body=%wide.region_17.18_spmd.sunk | while | flops 84871808 | bytes 1873661 | solution.py:210
  423.4 141.7 %all-gather.7.cloned.1.call-done = f32[384,128,128]{2,1,0:T(8,128)} async-done(((f32[4,128,128]{2,1,0:T(8,128)}), f32[384,128,128]{2,1,0:T(8,128)}) %all-gather.7.cloned.1.call-update) | async-done | bytes 25165840 | tf_op jit(solution)/shard_map/all_gather | solution.py:19
  565.1 102.8 %while.108 = (s32[]{:T(128)}, f32[4,128,128]{2,1,0:T(8,128)S(1)}, s32[]{:T(128)}, f32[96,4,128,128]{3,2,1,0:T(8,128)}, s32[]{:T(128)}, /*index=5*/s32[]{:T(128)}, s32[]{:T(128)}, s32[]{:T(128)}) while((s32[]{:T(128)}, f32[4,128,128]{2,1,0:T(8,128)S(1)}, s32[]{:T(128)}, f32[96,4,128,128]{3,2,1,0:T(8,128)}, s32[]{:T(128)}, ...), condition=%wide.region_14.15_spmd.clone, body=%wide.region_13.14_spmd.clone.sunk | while | flops 196616 | bytes 786587 | solution.py:28
  (434 shorter events, 255.3 us)
Async XLA Ops:
  7.2 59.4 %copy-start = (bf16[128,512]{1,0:T(8,128)(2,1)S(1)}, bf16[128,512]{1,0:T(8,128)(2,1)}, u32[]{:S(2)}) copy-start(bf16[128,512]{1,0:T(8,128)(2,1)} %param.19) | copy-start | bytes 393220
  7.2 5.0 copy-start.11
  7.2 228.8 %all-gather.5.cloned.1.call-start = ((), (), s32[]{:S(2)}) async-start(), calls=%async_computation | async-start | bytes 25427968 | tf_op jit(solution)/shard_map/all_gather | solution.py:19
  10.1 555.0 %all-gather.7.cloned.1.call-start = ((), (), s32[]{:S(2)}) async-start(), calls=%async_computation.1 | async-start | bytes 25427968 | tf_op jit(solution)/shard_map/all_gather | solution.py:19
  13.2 8.6 %collective-permute-start = (bf16[128,4,128]{2,1,0:T(4,128)(2,1)S(1)}, bf16[128,4,128]{2,1,0:T(4,128)(2,1)S(1)}, u32[]{:S(2)}, u32[]{:S(2)}) collective-permute-start(bf16[128,4,128]{2,1,0:T(4,128)(2,1)S(1)} %get-tuple-element.1146), channel_id=1, source_target_pairs={{0,8},{8,16},{16,24},{24,32},{32,40},{40,48},{48,56},{56,64},{64,7... | collective-permute-start | bytes 393224 | tf_op jit(solution)/shard_map/while/body/eval_jaxpr/ppermute | solution.py:34
  17.5 6.8 %collective-permute-start.1 = (bf16[128,4,128]{2,1,0:T(4,128)(2,1)S(1)}, bf16[128,4,128]{2,1,0:T(4,128)(2,1)S(1)}, u32[]{:S(2)}, u32[]{:S(2)}) collective-permute-start(bf16[128,4,128]{2,1,0:T(4,128)(2,1)S(1)} %get-tuple-element.1147), channel_id=1, source_target_pairs={{0,8},{8,16},{16,24},{24,32},{32,40},{40,48},{48,56},{56,64},{64,7... | collective-permute-start | bytes 393224 | tf_op jit(solution)/shard_map/while/body/eval_jaxpr/ppermute | solution.py:34
  24.4 9.8 %collective-permute-start = (bf16[128,4,128]{2,1,0:T(4,128)(2,1)S(1)}, bf16[128,4,128]{2,1,0:T(4,128)(2,1)S(1)}, u32[]{:S(2)}, u32[]{:S(2)}) collective-permute-start(bf16[128,4,128]{2,1,0:T(4,128)(2,1)S(1)} %get-tuple-element.1146), channel_id=1, source_target_pairs={{0,8},{8,16},{16,24},{24,32},{32,40},{40,48},{48,56},{56,64},{64,7... | collective-permute-start | bytes 393224 | tf_op jit(solution)/shard_map/while/body/eval_jaxpr/ppermute | solution.py:34
  28.8 9.3 %collective-permute-start.1 = (bf16[128,4,128]{2,1,0:T(4,128)(2,1)S(1)}, bf16[128,4,128]{2,1,0:T(4,128)(2,1)S(1)}, u32[]{:S(2)}, u32[]{:S(2)}) collective-permute-start(bf16[128,4,128]{2,1,0:T(4,128)(2,1)S(1)} %get-tuple-element.1147), channel_id=1, source_target_pairs={{0,8},{8,16},{16,24},{24,32},{32,40},{40,48},{48,56},{56,64},{64,7... | collective-permute-start | bytes 393224 | tf_op jit(solution)/shard_map/while/body/eval_jaxpr/ppermute | solution.py:34
  38.2 8.5 %collective-permute-start = (bf16[128,4,128]{2,1,0:T(4,128)(2,1)S(1)}, bf16[128,4,128]{2,1,0:T(4,128)(2,1)S(1)}, u32[]{:S(2)}, u32[]{:S(2)}) collective-permute-start(bf16[128,4,128]{2,1,0:T(4,128)(2,1)S(1)} %get-tuple-element.1146), channel_id=1, source_target_pairs={{0,8},{8,16},{16,24},{24,32},{32,40},{40,48},{48,56},{56,64},{64,7... | collective-permute-start | bytes 393224 | tf_op jit(solution)/shard_map/while/body/eval_jaxpr/ppermute | solution.py:34
  42.6 8.2 %collective-permute-start.1 = (bf16[128,4,128]{2,1,0:T(4,128)(2,1)S(1)}, bf16[128,4,128]{2,1,0:T(4,128)(2,1)S(1)}, u32[]{:S(2)}, u32[]{:S(2)}) collective-permute-start(bf16[128,4,128]{2,1,0:T(4,128)(2,1)S(1)} %get-tuple-element.1147), channel_id=1, source_target_pairs={{0,8},{8,16},{16,24},{24,32},{32,40},{40,48},{48,56},{56,64},{64,7... | collective-permute-start | bytes 393224 | tf_op jit(solution)/shard_map/while/body/eval_jaxpr/ppermute | solution.py:34
  50.9 10.0 %collective-permute-start = (bf16[128,4,128]{2,1,0:T(4,128)(2,1)S(1)}, bf16[128,4,128]{2,1,0:T(4,128)(2,1)S(1)}, u32[]{:S(2)}, u32[]{:S(2)}) collective-permute-start(bf16[128,4,128]{2,1,0:T(4,128)(2,1)S(1)} %get-tuple-element.1146), channel_id=1, source_target_pairs={{0,8},{8,16},{16,24},{24,32},{32,40},{40,48},{48,56},{56,64},{64,7... | collective-permute-start | bytes 393224 | tf_op jit(solution)/shard_map/while/body/eval_jaxpr/ppermute | solution.py:34
  55.3 7.9 %collective-permute-start.1 = (bf16[128,4,128]{2,1,0:T(4,128)(2,1)S(1)}, bf16[128,4,128]{2,1,0:T(4,128)(2,1)S(1)}, u32[]{:S(2)}, u32[]{:S(2)}) collective-permute-start(bf16[128,4,128]{2,1,0:T(4,128)(2,1)S(1)} %get-tuple-element.1147), channel_id=1, source_target_pairs={{0,8},{8,16},{16,24},{24,32},{32,40},{40,48},{48,56},{56,64},{64,7... | collective-permute-start | bytes 393224 | tf_op jit(solution)/shard_map/while/body/eval_jaxpr/ppermute | solution.py:34
  76.5 159.5 %copy-start.7 = (bf16[4,128,128]{2,1,0:T(8,128)(2,1)}, bf16[4,128,128]{2,1,0:T(8,128)(2,1)S(1)}, u32[]{:S(2)}) copy-start(bf16[4,128,128]{2,1,0:T(8,128)(2,1)S(1)} %get-tuple-element.567) | copy-start | bytes 393220
  236.0 112.7 %copy-start.10 = (f32[4,128,128]{1,2,0:T(8,128)S(1)}, f32[4,128,128]{1,2,0:T(8,128)}, u32[]{:S(2)}) copy-start(f32[4,128,128]{1,2,0:T(8,128)} %get-tuple-element.565) | copy-start | bytes 786436
  351.1 5.5 collective-permute-start.4
  352.4 11.4 %collective-permute-start.2 = (bf16[128,4,128]{2,1,0:T(4,128)(2,1)S(1)}, bf16[128,4,128]{2,1,0:T(4,128)(2,1)S(1)}, u32[]{:S(2)}, u32[]{:S(2)}) collective-permute-start(bf16[128,4,128]{2,1,0:T(4,128)(2,1)S(1)} %get-tuple-element.1231), channel_id=1, source_target_pairs={{8,0},{16,8},{24,16},{32,24},{40,32},{48,40},{56,48},{64,56},{72,6... | collective-permute-start | bytes 393224 | tf_op jit(solution)/shard_map/while/body/eval_jaxpr/ppermute | solution.py:34
  353.7 10.8 %collective-permute-start.3 = (bf16[128,4,128]{2,1,0:T(4,128)(2,1)S(1)}, bf16[128,4,128]{2,1,0:T(4,128)(2,1)S(1)}, u32[]{:S(2)}, u32[]{:S(2)}) collective-permute-start(bf16[128,4,128]{2,1,0:T(4,128)(2,1)S(1)} %get-tuple-element.1232), channel_id=1, source_target_pairs={{8,0},{16,8},{24,16},{32,24},{40,32},{48,40},{56,48},{64,56},{72,6... | collective-permute-start | bytes 393224 | tf_op jit(solution)/shard_map/while/body/eval_jaxpr/ppermute | solution.py:34
  355.0 8.8 %collective-permute-start.5 = (f32[4,128]{1,0:T(4,128)S(1)}, f32[4,128]{1,0:T(4,128)S(1)}, u32[]{:S(2)}, u32[]{:S(2)}) collective-permute-start(f32[4,128]{1,0:T(4,128)S(1)} %get-tuple-element.1234), channel_id=1, source_target_pairs={{8,0},{16,8},{24,16},{32,24},{40,32},{48,40},{56,48},{64,56},{72,6... | collective-permute-start | bytes 6152 | tf_op jit(solution)/shard_map/while/body/eval_jaxpr/ppermute | solution.py:34
  364.6 5.5 collective-permute-start.4
  365.9 14.0 %collective-permute-start.2 = (bf16[128,4,128]{2,1,0:T(4,128)(2,1)S(1)}, bf16[128,4,128]{2,1,0:T(4,128)(2,1)S(1)}, u32[]{:S(2)}, u32[]{:S(2)}) collective-permute-start(bf16[128,4,128]{2,1,0:T(4,128)(2,1)S(1)} %get-tuple-element.1231), channel_id=1, source_target_pairs={{8,0},{16,8},{24,16},{32,24},{40,32},{48,40},{56,48},{64,56},{72,6... | collective-permute-start | bytes 393224 | tf_op jit(solution)/shard_map/while/body/eval_jaxpr/ppermute | solution.py:34
  367.2 13.4 %collective-permute-start.3 = (bf16[128,4,128]{2,1,0:T(4,128)(2,1)S(1)}, bf16[128,4,128]{2,1,0:T(4,128)(2,1)S(1)}, u32[]{:S(2)}, u32[]{:S(2)}) collective-permute-start(bf16[128,4,128]{2,1,0:T(4,128)(2,1)S(1)} %get-tuple-element.1232), channel_id=1, source_target_pairs={{8,0},{16,8},{24,16},{32,24},{40,32},{48,40},{56,48},{64,56},{72,6... | collective-permute-start | bytes 393224 | tf_op jit(solution)/shard_map/while/body/eval_jaxpr/ppermute | solution.py:34
  368.5 11.4 %collective-permute-start.5 = (f32[4,128]{1,0:T(4,128)S(1)}, f32[4,128]{1,0:T(4,128)S(1)}, u32[]{:S(2)}, u32[]{:S(2)}) collective-permute-start(f32[4,128]{1,0:T(4,128)S(1)} %get-tuple-element.1234), channel_id=1, source_target_pairs={{8,0},{16,8},{24,16},{32,24},{40,32},{48,40},{56,48},{64,56},{72,6... | collective-permute-start | bytes 6152 | tf_op jit(solution)/shard_map/while/body/eval_jaxpr/ppermute | solution.py:34
  380.8 5.5 collective-permute-start.4
  382.1 13.4 %collective-permute-start.2 = (bf16[128,4,128]{2,1,0:T(4,128)(2,1)S(1)}, bf16[128,4,128]{2,1,0:T(4,128)(2,1)S(1)}, u32[]{:S(2)}, u32[]{:S(2)}) collective-permute-start(bf16[128,4,128]{2,1,0:T(4,128)(2,1)S(1)} %get-tuple-element.1231), channel_id=1, source_target_pairs={{8,0},{16,8},{24,16},{32,24},{40,32},{48,40},{56,48},{64,56},{72,6... | collective-permute-start | bytes 393224 | tf_op jit(solution)/shard_map/while/body/eval_jaxpr/ppermute | solution.py:34
  383.4 12.8 %collective-permute-start.3 = (bf16[128,4,128]{2,1,0:T(4,128)(2,1)S(1)}, bf16[128,4,128]{2,1,0:T(4,128)(2,1)S(1)}, u32[]{:S(2)}, u32[]{:S(2)}) collective-permute-start(bf16[128,4,128]{2,1,0:T(4,128)(2,1)S(1)} %get-tuple-element.1232), channel_id=1, source_target_pairs={{8,0},{16,8},{24,16},{32,24},{40,32},{48,40},{56,48},{64,56},{72,6... | collective-permute-start | bytes 393224 | tf_op jit(solution)/shard_map/while/body/eval_jaxpr/ppermute | solution.py:34
  384.7 10.8 %collective-permute-start.5 = (f32[4,128]{1,0:T(4,128)S(1)}, f32[4,128]{1,0:T(4,128)S(1)}, u32[]{:S(2)}, u32[]{:S(2)}) collective-permute-start(f32[4,128]{1,0:T(4,128)S(1)} %get-tuple-element.1234), channel_id=1, source_target_pairs={{8,0},{16,8},{24,16},{32,24},{40,32},{48,40},{56,48},{64,56},{72,6... | collective-permute-start | bytes 6152 | tf_op jit(solution)/shard_map/while/body/eval_jaxpr/ppermute | solution.py:34
  396.4 5.5 collective-permute-start.4
  397.7 10.7 %collective-permute-start.2 = (bf16[128,4,128]{2,1,0:T(4,128)(2,1)S(1)}, bf16[128,4,128]{2,1,0:T(4,128)(2,1)S(1)}, u32[]{:S(2)}, u32[]{:S(2)}) collective-permute-start(bf16[128,4,128]{2,1,0:T(4,128)(2,1)S(1)} %get-tuple-element.1231), channel_id=1, source_target_pairs={{8,0},{16,8},{24,16},{32,24},{40,32},{48,40},{56,48},{64,56},{72,6... | collective-permute-start | bytes 393224 | tf_op jit(solution)/shard_map/while/body/eval_jaxpr/ppermute | solution.py:34
  399.0 10.1 %collective-permute-start.3 = (bf16[128,4,128]{2,1,0:T(4,128)(2,1)S(1)}, bf16[128,4,128]{2,1,0:T(4,128)(2,1)S(1)}, u32[]{:S(2)}, u32[]{:S(2)}) collective-permute-start(bf16[128,4,128]{2,1,0:T(4,128)(2,1)S(1)} %get-tuple-element.1232), channel_id=1, source_target_pairs={{8,0},{16,8},{24,16},{32,24},{40,32},{48,40},{56,48},{64,56},{72,6... | collective-permute-start | bytes 393224 | tf_op jit(solution)/shard_map/while/body/eval_jaxpr/ppermute | solution.py:34
  400.3 8.1 %collective-permute-start.5 = (f32[4,128]{1,0:T(4,128)S(1)}, f32[4,128]{1,0:T(4,128)S(1)}, u32[]{:S(2)}, u32[]{:S(2)}) collective-permute-start(f32[4,128]{1,0:T(4,128)S(1)} %get-tuple-element.1234), channel_id=1, source_target_pairs={{8,0},{16,8},{24,16},{32,24},{40,32},{48,40},{56,48},{64,56},{72,6... | collective-permute-start | bytes 6152 | tf_op jit(solution)/shard_map/while/body/eval_jaxpr/ppermute | solution.py:34
  410.4 9.3 %copy-start.8 = (bf16[4,128,128]{2,1,0:T(8,128)(2,1)S(1)}, bf16[4,128,128]{2,1,0:T(8,128)(2,1)}, u32[]{:S(2)}) copy-start(bf16[4,128,128]{2,1,0:T(8,128)(2,1)} %copy-done.7) | copy-start | bytes 393220
  565.1 102.8 %copy-start.5 = (bf16[128,512]{1,0:T(8,128)(2,1)S(1)}, bf16[128,512]{1,0:T(8,128)(2,1)}, u32[]{:S(2)}) copy-start(bf16[128,512]{1,0:T(8,128)(2,1)} %param.20) | copy-start | bytes 393220
  (10 other events, 12.6 us)
Sparse Core Ops, SparseCore 0:
  11.7 224.1 all-gather.4
  350.5 214.5 all-gather.6
where the time goes:
time: 684 us; the launch traced here: 677 us
  waiting for transfers between devices  348 us (51%)
  other arithmetic  203 us (30%)
  starting transfers between devices  56.4 us (8%)
  matrix products  20.3 us (3%)
  local copies, waits for them, and re-layouts  18.6 us (3%)
  between operations  14.5 us (2%)
  blocking collectives  10 us (1%)
    all_gather x2, waiting for transfers between devices, prefix_2(): everything = lax.all_gather(value, axis)  301 us
    select_n x192, other arithmetic, lap(): return jnp.where(reached, new, before)  200 us
    ppermute x24, starting transfers between devices, passed_along(): return lax.ppermute(block, axis, route)  56.3 us
    ppermute x24, waiting for transfers between devices, passed_along(): return lax.ppermute(block, axis, route)  47.2 us
  transfers between devices with their start and end apart: 26, of which 15 were waited for; matrix products, arithmetic and copies ran while one was open for 5% of the time, Pallas kernels for 0%

commit v1 on v0

v1 whole, which is shorter than its diff:
```python
import math

import jax
import jax.numpy as jnp
from jax import lax
from jax.sharding import PartitionSpec as P

HD = 128
WIN = 512
LANES = 128


PRECISE = lax.Precision.HIGHEST
NORM_EPS = 1e-05


def scan_states(state, axis, reverse):
    count = lax.axis_size(axis)
    flat = state.reshape(-1, LANES)
    rows = flat.shape[0]
    per = -(-rows // count)
    flat = jnp.pad(flat, ((0, per * count - rows), (0, 0)))
    pieces = flat.reshape(count, per * LANES)
    gathered = lax.all_to_all(pieces, axis, 0, 0, tiled=True)
    index = jnp.arange(count, dtype=jnp.int32)
    if reverse:
        mask = index[None, :] > index[:, None]
    else:
        mask = index[None, :] < index[:, None]
    sums = jnp.einsum(
        "ij,jf->if", mask.astype(jnp.float32), gathered, precision=PRECISE
    )
    returned = lax.all_to_all(sums, axis, 0, 0, tiled=True)
    return returned.reshape(count * per, LANES)[:rows].reshape(state.shape)


def passed_along(block, axis, distance):
    devices = range(lax.axis_size(axis))
    route = [(i - distance, i) for i in devices if i - distance in devices]
    return lax.ppermute(block, axis, route)


def causal_rows(block_rows):
    positions = jnp.arange(block_rows, dtype=jnp.int32)
    return positions[:, None] >= positions[None, :]


def linear_forward(query, keys, values, before):
    causal = causal_rows(query.shape[0])
    scores = jnp.einsum("thd,shd->hts", query, keys, preferred_element_type=jnp.float32)
    scores = jnp.where(causal[None], scores, 0.0)
    inner = jnp.einsum("hts,shd->thd", scores, values.astype(jnp.float32), precision=PRECISE)
    result = inner + jnp.einsum(
        "thd,hde->the", query.astype(jnp.float32), before, precision=PRECISE
    )
    return (result, scores)


def linear_backward(query, keys, values, cotangent, scores, before, after):
    causal = causal_rows(query.shape[0])
    cotangent_f = cotangent.astype(jnp.float32)
    dprobs = jnp.einsum("the,she->hts", cotangent, values, preferred_element_type=jnp.float32)
    dprobs = jnp.where(causal[None], dprobs, 0.0)
    query_grad = jnp.einsum("hts,shd->thd", dprobs, keys.astype(jnp.float32), precision=PRECISE)
    query_grad = query_grad + jnp.einsum("the,hde->thd", cotangent_f, before, precision=PRECISE)
    key_grad = jnp.einsum("hts,thd->shd", dprobs, query.astype(jnp.float32), precision=PRECISE)
    key_grad = key_grad + jnp.einsum(
        "she,hde->shd", values.astype(jnp.float32), after, precision=PRECISE
    )
    value_grad = jnp.einsum("hts,the->she", scores, cotangent_f, precision=PRECISE)
    value_grad = value_grad + jnp.einsum(
        "shd,hde->she", keys.astype(jnp.float32), after, precision=PRECISE
    )
    return (query_grad, key_grad, value_grad)


def query_head(query, keys, values, upstream, first_pos):
    row_count = query.shape[0]
    ext_count = keys.shape[0]
    window = ext_count - row_count
    score_scale = 1.0 / math.sqrt(query.shape[2])
    scores = jnp.einsum("thd,shd->hts", query, keys, preferred_element_type=jnp.float32) * score_scale
    query_pos = first_pos + jnp.arange(row_count, dtype=jnp.int32)
    key_pos = first_pos - window + jnp.arange(ext_count, dtype=jnp.int32)
    allowed = (
        (key_pos[None, :] >= 0)
        & (key_pos[None, :] <= query_pos[:, None])
        & (key_pos[None, :] > query_pos[:, None] - window)
    )
    scores = jnp.where(allowed[None], scores, -jnp.inf)
    row_max = jnp.max(scores, axis=2, keepdims=True)
    log_total = row_max[:, :, 0] + jnp.log(jnp.sum(jnp.exp(scores - row_max), axis=2))
    probs = jnp.exp(scores - log_total[:, :, None])
    weights_low = probs.astype(jnp.bfloat16)
    output = jnp.einsum("hts,shd->thd", weights_low, values, preferred_element_type=jnp.float32)
    dprobs = jnp.einsum("thd,shd->hts", upstream, values, preferred_element_type=jnp.float32)
    row_dot = jnp.sum(probs * dprobs, axis=2)
    dscores = (probs * (dprobs - row_dot[:, :, None]) * score_scale).astype(jnp.bfloat16)
    query_grad = jnp.einsum("hts,shd->thd", dscores, keys, preferred_element_type=jnp.float32)
    return (output, query_grad, log_total, row_dot)


def key_head(query, upstream, totals, dots, keys, values, first_pos, total_rows):
    row_count = keys.shape[0]
    ext_count = query.shape[0]
    window = ext_count - row_count
    score_scale = 1.0 / math.sqrt(query.shape[2])
    scores = jnp.einsum("thd,shd->hts", query, keys, preferred_element_type=jnp.float32) * score_scale
    query_pos = first_pos + jnp.arange(ext_count, dtype=jnp.int32)
    key_pos = first_pos + jnp.arange(row_count, dtype=jnp.int32)
    allowed = (
        (query_pos[:, None] < total_rows)
        & (key_pos[None, :] <= query_pos[:, None])
        & (key_pos[None, :] > query_pos[:, None] - window)
    )
    probs = jnp.where(allowed[None], jnp.exp(scores - totals[:, :, None]), 0.0)
    weights_low = probs.astype(jnp.bfloat16)
    dprobs = jnp.einsum("thd,shd->hts", upstream, values, preferred_element_type=jnp.float32)
    dscores = (probs * (dprobs - dots[:, :, None]) * score_scale).astype(jnp.bfloat16)
    key_grad = jnp.einsum("hts,thd->shd", dscores, query, preferred_element_type=jnp.float32)
    value_grad = jnp.einsum("hts,thd->shd", weights_low, upstream, preferred_element_type=jnp.float32)
    return (key_grad, value_grad)


def shards(lin_q, lin_k, lin_v, win_q, win_k, win_v, grad_out):
    row_count = lin_q.shape[0]
    head_count = lin_q.shape[1] // HD
    shaped = (row_count, head_count, HD)
    flat = (row_count, head_count * HD)
    span = WIN // row_count
    total_rows = row_count * lax.axis_size("ctx")
    first_pos = lax.axis_index("ctx") * row_count
    win_query = win_q.reshape(shaped)
    win_key = win_k.reshape(shaped)
    win_value = win_v.reshape(shaped)
    cotangent = grad_out.reshape(shaped)

    earlier_keys, earlier_values = [], []
    later_queries, later_upstreams = [], []
    key_pair = (win_key, win_value)
    row_pair = (win_query, cotangent)
    for _ in range(span):
        key_pair = passed_along(key_pair, "ctx", 1)
        row_pair = passed_along(row_pair, "ctx", -1)
        earlier_keys.insert(0, key_pair[0])
        earlier_values.insert(0, key_pair[1])
        later_queries.append(row_pair[0])
        later_upstreams.append(row_pair[1])

    lin_query = lin_q.reshape(shaped)
    lin_key = lin_k.reshape(shaped)
    lin_value = lin_v.reshape(shaped)
    key_state = jnp.einsum("shd,she->hde", lin_key, lin_value, preferred_element_type=jnp.float32)
    prefix = scan_states(key_state, "ctx", False)
    lin_out, lin_scores = linear_forward(lin_query, lin_key, lin_value, prefix)
    upstream = grad_out.reshape(shaped).astype(jnp.float32)
    square_sum, cross_sum = lax.psum(
        (jnp.sum(lin_out * lin_out, axis=(1, 2)), jnp.sum(upstream * lin_out, axis=(1, 2))), "head"
    )
    features = head_count * HD * lax.axis_size("head")
    inv_rms = lax.rsqrt(square_sum / features + NORM_EPS)
    lin_dout = (
        inv_rms[:, None, None] * upstream
        - lin_out * (inv_rms**3 * cross_sum / features)[:, None, None]
    ).astype(jnp.bfloat16)
    query_state = jnp.einsum(
        "thd,the->hde", lin_query, lin_dout, preferred_element_type=jnp.float32
    )
    suffix = scan_states(query_state, "ctx", True)
    grad_q, grad_k, grad_v = linear_backward(
        lin_query, lin_key, lin_value, lin_dout, lin_scores, prefix, suffix
    )

    key_ext = jnp.concatenate(earlier_keys + [win_key], axis=0)
    value_ext = jnp.concatenate(earlier_values + [win_value], axis=0)
    win_out, win_dq, log_total, row_dot = query_head(
        win_query, key_ext, value_ext, cotangent, first_pos
    )

    later_totals, later_dots = [], []
    stat_pair = (log_total, row_dot)
    for _ in range(span):
        stat_pair = passed_along(stat_pair, "ctx", -1)
        later_totals.append(stat_pair[0])
        later_dots.append(stat_pair[1])
    query_ext = jnp.concatenate([win_query] + later_queries, axis=0)
    upstream_ext = jnp.concatenate([cotangent] + later_upstreams, axis=0)
    total_ext = jnp.concatenate([log_total] + later_totals, axis=1)
    dot_ext = jnp.concatenate([row_dot] + later_dots, axis=1)
    win_dk, win_dv = key_head(
        query_ext, upstream_ext, total_ext, dot_ext, win_key, win_value, first_pos, total_rows
    )
    mixed = (lin_out * inv_rms[:, None, None] + win_out).astype(jnp.bfloat16).reshape(flat)
    return (
        mixed,
        grad_q.astype(jnp.bfloat16).reshape(flat),
        grad_k.astype(jnp.bfloat16).reshape(flat),
        grad_v.astype(jnp.bfloat16).reshape(flat),
        win_dq.astype(jnp.bfloat16).reshape(flat),
        win_dk.astype(jnp.bfloat16).reshape(flat),
        win_dv.astype(jnp.bfloat16).reshape(flat),
    )


def solution(mesh):
    spec = P("ctx", "head")
    return jax.shard_map(
        shards,
        mesh=mesh,
        in_specs=(spec,) * 7,
        out_specs=(spec,) * 7,
        check_vma=False,
    )
```

time: 684 us -> 225 us (0.33)
  waiting for transfers between devices: 348 us -> 44.1 us
  other arithmetic: 203 us -> 2.45 us
  starting transfers between devices: 56.4 us -> 128 us
  between operations: 14.5 us -> 1.66 us
    all_gather x2 -> x0, waiting for transfers between devices: 301 us -> none  [prefix_2(): everything = lax.all_gather(value, axis)]
    select_n x192 -> x0, other arithmetic: 200 us -> none  [lap(): return jnp.where(reached, new, before)]
    all_to_all x0 -> x4, starting transfers between devices: none -> 70.4 us  [the longest x2 35.5 us: scan_states(): returned = lax.all_to_all(sums, axis, 0, 0, tiled=True)]
    ppermute x24, waiting for transfers between devices: 47.2 us -> 12.3 us  [passed_along(): return lax.ppermute(block, axis, route)]
    all_to_all x0 -> x4, waiting for transfers between devices: none -> 31.8 us  [the longest x2 20.2 us: scan_states(): returned = lax.all_to_all(sums, axis, 0, 0, tiled=True)]
    dot_general x28 -> x9, matrix products: 15.1 us -> 9.72 us  [the longest x1 2.26 us: key_head(): jnp.einsum('hts,thd->shd', dscores, query, preferred_element_type=jnp.flo...]
  transfers between devices with their start and end apart: 26 -> 28, of which waited for: 15 -> 9; matrix products, arithmetic and copies ran while one was open for 5% -> 11% of each run, Pallas kernels for 0% -> 0%
where the time goes in v1:
time: 225 us; the launch traced here: 221 us
  starting transfers between devices  128 us (57%)
  waiting for transfers between devices  44.1 us (20%)
  local copies, waits for them, and re-layouts  19.1 us (8%)
  matrix products  15.7 us (7%)
  blocking collectives  9.99 us (4%)
  other arithmetic  2.45 us (1%)
    ppermute x24, starting transfers between devices, passed_along(): return lax.ppermute(block, axis, route)  57.7 us
    all_to_all x2, starting transfers between devices, scan_states(): returned = lax.all_to_all(sums, axis, 0, 0, tiled=True)  35.5 us
    all_to_all x2, starting transfers between devices, scan_states(): gathered = lax.all_to_all(pieces, axis, 0, 0, tiled=True)  34.9 us
    all_to_all x2, waiting for transfers between devices, scan_states(): returned = lax.all_to_all(sums, axis, 0, 0, tiled=True)  20.2 us
    unnamed x76, local copies, waits for them, and re-layouts  12.5 us
    ppermute x24, waiting for transfers between devices, passed_along(): return lax.ppermute(block, axis, route)  12.3 us
    all_to_all x2, waiting for transfers between devices, scan_states(): gathered = lax.all_to_all(pieces, axis, 0, 0, tiled=True)  11.7 us
    psum x1, blocking collectives, shards(): lax.psum((jnp.sum(lin_out * lin_out, axis=(1, 2)), jnp.sum(upstream * lin...  9.99 us
  transfers between devices with their start and end apart: 28, of which 9 were waited for; matrix products, arithmetic and copies ran while one was open for 11% of the time, Pallas kernels for 0%

profile of v1, /device:TPU:6, one launch (start us, length us, event | category | flops | bytes accessed | tf_op | source)
XLA Modules:
  0.0 221.1 jit_solution(9054183050699598983)
XLA Ops:
  1.7 4.3 %collective-permute-start = (bf16[128,4,128]{0,2,1:T(8,128)(2,1)S(1)}, bf16[128,4,128]{0,2,1:T(8,128)(2,1)S(1)}, u32[]{:S(2)}, u32[]{:S(2)}) collective-permute-start(bf16[128,4,128]{0,2,1:T(8,128)(2,1)S(1)} %bitcast.153), channel_id=1, source_target_pairs={{0,8},{8,16},{16,24},{24,32},{32,40},{40,48},{48,56},{56,64},{64,7... | collective-permute-start | bytes 393224 | tf_op jit(solution)/shard_map/ppermute | solution.py:40
  7.7 4.3 %collective-permute-start.4 = (bf16[128,4,128]{2,0,1:T(8,128)(2,1)S(1)}, bf16[128,4,128]{2,0,1:T(8,128)(2,1)S(1)}, u32[]{:S(2)}, u32[]{:S(2)}) collective-permute-start(bf16[128,4,128]{2,0,1:T(8,128)(2,1)S(1)} %copy.96), channel_id=1, source_target_pairs={{0,8},{8,16},{16,24},{24,32},{32,40},{40,48},{48,56},{56,64},{64,7... | collective-permute-start | bytes 393224 | tf_op jit(solution)/shard_map/ppermute | solution.py:40
  14.0 20.2 %all-to-all-start = ((f32[96,1,768]{2,1,0:T(1,128)}), f32[96,1,768]{2,1,0:T(1,128)S(1)}, u32[]{:S(2)}, u32[]{:S(2)}) async-start(f32[96,1,768]{2,1,0:T(1,128)} %bitcast.2), calls=%async_computation | async-start | bytes 589824 | tf_op jit(solution)/shard_map/all_to_all | solution.py:24
  34.4 1.3 collective-permute-start.8
  35.9 1.3 collective-permute-start.16
  40.1 5.2 %collective-permute-start.1 = (bf16[128,4,128]{0,2,1:T(8,128)(2,1)S(1)}, bf16[128,4,128]{0,2,1:T(8,128)(2,1)S(1)}, u32[]{:S(2)}, u32[]{:S(2)}) collective-permute-start(bf16[128,4,128]{0,2,1:T(8,128)(2,1)S(1)} %collective-permute-done), channel_id=1, source_target_pairs={{0,8},{8,16},{16,24},{24,32},{32,40},{40,48},{48,56},{56,64},{64,7... | collective-permute-start | bytes 393224 | tf_op jit(solution)/shard_map/ppermute | solution.py:40
  45.3 3.9 %collective-permute-start.5 = (bf16[128,4,128]{2,0,1:T(8,128)(2,1)S(1)}, bf16[128,4,128]{2,0,1:T(8,128)(2,1)S(1)}, u32[]{:S(2)}, u32[]{:S(2)}) collective-permute-start(bf16[128,4,128]{2,0,1:T(8,128)(2,1)S(1)} %collective-permute-done.4), channel_id=1, source_target_pairs={{0,8},{8,16},{16,24},{24,32},{32,40},{40,48},{48,56},{56,64},{64,7... | collective-permute-start | bytes 393224 | tf_op jit(solution)/shard_map/ppermute | solution.py:40
  49.2 1.3 collective-permute-start.9
  50.6 1.3 collective-permute-start.17
  51.9 5.2 %collective-permute-start.2 = (bf16[128,4,128]{0,2,1:T(8,128)(2,1)S(1)}, bf16[128,4,128]{0,2,1:T(8,128)(2,1)S(1)}, u32[]{:S(2)}, u32[]{:S(2)}) collective-permute-start(bf16[128,4,128]{0,2,1:T(8,128)(2,1)S(1)} %collective-permute-done.1), channel_id=1, source_target_pairs={{0,8},{8,16},{16,24},{24,32},{32,40},{40,48},{48,56},{56,64},{64,7... | collective-permute-start | bytes 393224 | tf_op jit(solution)/shard_map/ppermute | solution.py:40
  57.1 3.9 %collective-permute-start.6 = (bf16[128,4,128]{2,0,1:T(8,128)(2,1)S(1)}, bf16[128,4,128]{2,0,1:T(8,128)(2,1)S(1)}, u32[]{:S(2)}, u32[]{:S(2)}) collective-permute-start(bf16[128,4,128]{2,0,1:T(8,128)(2,1)S(1)} %collective-permute-done.5), channel_id=1, source_target_pairs={{0,8},{8,16},{16,24},{24,32},{32,40},{40,48},{48,56},{56,64},{64,7... | collective-permute-start | bytes 393224 | tf_op jit(solution)/shard_map/ppermute | solution.py:40
  62.4 1.3 collective-permute-start.18
  63.7 5.2 %collective-permute-start.3 = (bf16[128,4,128]{0,2,1:T(8,128)(2,1)S(1)}, bf16[128,4,128]{0,2,1:T(8,128)(2,1)S(1)}, u32[]{:S(2)}, u32[]{:S(2)}) collective-permute-start(bf16[128,4,128]{0,2,1:T(8,128)(2,1)S(1)} %collective-permute-done.2), channel_id=1, source_target_pairs={{0,8},{8,16},{16,24},{24,32},{32,40},{40,48},{48,56},{56,64},{64,7... | collective-permute-start | bytes 393224 | tf_op jit(solution)/shard_map/ppermute | solution.py:40
  68.9 5.1 %collective-permute-start.7 = (bf16[128,4,128]{2,0,1:T(8,128)(2,1)S(1)}, bf16[128,4,128]{2,0,1:T(8,128)(2,1)S(1)}, u32[]{:S(2)}, u32[]{:S(2)}) collective-permute-start(bf16[128,4,128]{2,0,1:T(8,128)(2,1)S(1)} %collective-permute-done.6), channel_id=1, source_target_pairs={{0,8},{8,16},{16,24},{24,32},{32,40},{40,48},{48,56},{56,64},{64,7... | collective-permute-start | bytes 393224 | tf_op jit(solution)/shard_map/ppermute | solution.py:40
  77.7 1.3 collective-permute-start.12
  79.4 1.3 collective-permute-start.20
  81.0 2.0 collective-permute-done.19
  88.7 3.1 %collective-permute-done.13 = f32[4,128]{1,0:T(4,128)S(1)} collective-permute-done((f32[4,128]{1,0:T(4,128)S(1)}, f32[4,128]{1,0:T(4,128)S(1)}, u32[]{:S(2)}, u32[]{:S(2)}) %collective-permute-start.13) | collective-permute-done | bytes 2080 | tf_op jit(solution)/shard_map/ppermute | solution.py:40
  94.4 29.3 %all-to-all-start.1 = ((f32[96,1,768]{2,1,0:T(1,128)}), f32[96,1,768]{2,1,0:T(1,128)S(1)}, u32[]{:S(2)}, u32[]{:S(2)}) async-start(f32[96,1,768]{2,1,0:T(1,128)} %copy.91), calls=%async_computation.1 | async-start | bytes 589824 | tf_op jit(solution)/shard_map/all_to_all | solution.py:33
  126.9 3.0 %collective-permute-done.22 = f32[4,128]{1,0:T(4,128)S(1)} collective-permute-done((f32[4,128]{1,0:T(4,128)S(1)}, f32[4,128]{1,0:T(4,128)S(1)}, u32[]{:S(2)}, u32[]{:S(2)}) %collective-permute-start.22) | collective-permute-done | bytes 2080 | tf_op jit(solution)/shard_map/ppermute | solution.py:40
  131.9 3.6 %collective-permute-done.23 = f32[4,128]{1,0:T(4,128)S(1)} collective-permute-done((f32[4,128]{1,0:T(4,128)S(1)}, f32[4,128]{1,0:T(4,128)S(1)}, u32[]{:S(2)}, u32[]{:S(2)}) %collective-permute-start.23) | collective-permute-done | bytes 2080 | tf_op jit(solution)/shard_map/ppermute | solution.py:40
  136.0 1.6 fusion.4
  137.7 2.7 %all-to-all-done.1 = f32[96,1,768]{2,1,0:T(1,128)S(1)} async-done(((f32[96,1,768]{2,1,0:T(1,128)}), f32[96,1,768]{2,1,0:T(1,128)S(1)}, u32[]{:S(2)}, u32[]{:S(2)}) %all-to-all-start.1) | async-done | bytes 294944 | tf_op jit(solution)/shard_map/all_to_all | solution.py:33
  142.0 2.0 fusion.33
  144.0 10.0 %all-reduce.2 = (f32[128]{0:T(128)S(1)}, f32[128]{0:T(128)S(1)}) all-reduce(f32[128]{0:T(128)S(1)} %get-tuple-element.29, f32[128]{0:T(128)S(1)} %get-tuple-element.28), channel_id=1, replica_groups=mesh['ctx'=96,'head'=8] {'head'}, use_global_device_ids=true, to_apply=%region_1.2 | all-reduce | flops 256 | bytes 2048 | tf_op jit(solution)/shard_map/psum | solution.py:157
  156.5 14.7 %all-to-all-start.2 = ((f32[96,1,768]{2,1,0:T(1,128)}), f32[96,1,768]{2,1,0:T(1,128)}, u32[]{:S(2)}, u32[]{:S(2)}) async-start(f32[96,1,768]{2,1,0:T(1,128)} %bitcast.152), calls=%async_computation.2 | async-start | bytes 589824 | tf_op jit(solution)/shard_map/all_to_all | solution.py:24
  171.2 2.3 %fusion.17 = bf16[4,128,128]{2,1,0:T(8,128)(2,1)S(1)} fusion(bf16[640,4,128]{2,0,1:T(8,128)(2,1)} %copy-done.10, f32[4,640,128]{2,1,0:T(8,128)S(1)} %fusion.4, bf16[640,4,128]{0,2,1:T(8,128)(2,1)} %copy-done.1, bf16[128,4,128]{0,2,1:T(8,128)(2,1)S(1)} %bitcast.155, f32[4,640]{1,0:T(4,128)} %constant_dynamic-update-slice_fusion.25), kind=kOutput, calls=%fused_computation.39 | convolution fusion | flops 169148416 | bytes 2893824 | tf_op jit(solution)/shard_map/hts,thd->shd/dot_general | solution.py:120
  174.3 1.4 convolution_convert_fusion
  176.5 1.5 fusion.16
  179.0 11.7 %all-to-all-done.2 = f32[96,1,768]{2,1,0:T(1,128)} async-done(((f32[96,1,768]{2,1,0:T(1,128)}), f32[96,1,768]{2,1,0:T(1,128)}, u32[]{:S(2)}, u32[]{:S(2)}) %all-to-all-start.2) | async-done | bytes 294944 | tf_op jit(solution)/shard_map/all_to_all | solution.py:24
  193.0 6.3 %all-to-all-start.3 = ((f32[96,1,768]{2,1,0:T(1,128)}), f32[96,1,768]{2,1,0:T(1,128)S(1)}, u32[]{:S(2)}, u32[]{:S(2)}) async-start(f32[96,1,768]{2,1,0:T(1,128)} %copy.109), calls=%async_computation.3 | async-start | bytes 589824 | tf_op jit(solution)/shard_map/all_to_all | solution.py:33
  201.2 17.5 %all-to-all-done.3 = f32[96,1,768]{2,1,0:T(1,128)S(1)} async-done(((f32[96,1,768]{2,1,0:T(1,128)}), f32[96,1,768]{2,1,0:T(1,128)S(1)}, u32[]{:S(2)}, u32[]{:S(2)}) %all-to-all-start.3) | async-done | bytes 294944 | tf_op jit(solution)/shard_map/all_to_all | solution.py:33
  (151 shorter events, 40.5 us)
Async XLA Ops:
  0.6 33.5 %copy-start.12 = (bf16[128,512]{1,0:T(8,128)(2,1)S(1)}, bf16[128,512]{1,0:T(8,128)(2,1)}, u32[]{:S(2)}) copy-start(bf16[128,512]{1,0:T(8,128)(2,1)} %param.10) | copy-start | bytes 393220
  1.7 38.3 %collective-permute-start = (bf16[128,4,128]{0,2,1:T(8,128)(2,1)S(1)}, bf16[128,4,128]{0,2,1:T(8,128)(2,1)S(1)}, u32[]{:S(2)}, u32[]{:S(2)}) collective-permute-start(bf16[128,4,128]{0,2,1:T(8,128)(2,1)S(1)} %bitcast.153), channel_id=1, source_target_pairs={{0,8},{8,16},{16,24},{24,32},{32,40},{40,48},{48,56},{56,64},{64,7... | collective-permute-start | bytes 393224 | tf_op jit(solution)/shard_map/ppermute | solution.py:40
  7.1 28.7 %copy-start.13 = (bf16[128,512]{1,0:T(8,128)(2,1)S(1)}, bf16[128,512]{1,0:T(8,128)(2,1)}, u32[]{:S(2)}) copy-start(bf16[128,512]{1,0:T(8,128)(2,1)} %param.13) | copy-start | bytes 393220
  7.7 37.6 %collective-permute-start.4 = (bf16[128,4,128]{2,0,1:T(8,128)(2,1)S(1)}, bf16[128,4,128]{2,0,1:T(8,128)(2,1)S(1)}, u32[]{:S(2)}, u32[]{:S(2)}) collective-permute-start(bf16[128,4,128]{2,0,1:T(8,128)(2,1)S(1)} %copy.96), channel_id=1, source_target_pairs={{0,8},{8,16},{16,24},{24,32},{32,40},{40,48},{48,56},{56,64},{64,7... | collective-permute-start | bytes 393224 | tf_op jit(solution)/shard_map/ppermute | solution.py:40
  14.0 79.1 %all-to-all-start = ((f32[96,1,768]{2,1,0:T(1,128)}), f32[96,1,768]{2,1,0:T(1,128)S(1)}, u32[]{:S(2)}, u32[]{:S(2)}) async-start(f32[96,1,768]{2,1,0:T(1,128)} %bitcast.2), calls=%async_computation | async-start | bytes 589824 | tf_op jit(solution)/shard_map/all_to_all | solution.py:24
  34.4 14.8 %collective-permute-start.8 = (bf16[128,4,128]{2,0,1:T(8,128)(2,1)S(1)}, bf16[128,4,128]{2,0,1:T(8,128)(2,1)S(1)}, u32[]{:S(2)}, u32[]{:S(2)}) collective-permute-start(bf16[128,4,128]{2,0,1:T(8,128)(2,1)S(1)} %copy.118), channel_id=1, source_target_pairs={{8,0},{16,8},{24,16},{32,24},{40,32},{48,40},{56,48},{64,56},{72,6... | collective-permute-start | bytes 393224 | tf_op jit(solution)/shard_map/ppermute | solution.py:40
  35.9 14.7 %collective-permute-start.16 = (bf16[128,4,128]{0,2,1:T(8,128)(2,1)S(1)}, bf16[128,4,128]{0,2,1:T(8,128)(2,1)S(1)}, u32[]{:S(2)}, u32[]{:S(2)}) collective-permute-start(bf16[128,4,128]{0,2,1:T(8,128)(2,1)S(1)} %bitcast.146), channel_id=1, source_target_pairs={{8,0},{16,8},{24,16},{32,24},{40,32},{48,40},{56,48},{64,56},{72,6... | collective-permute-start | bytes 393224 | tf_op jit(solution)/shard_map/ppermute | solution.py:40
  37.7 39.0 %copy-start.3 = (f32[4,128,128]{2,1,0:T(8,128)}, f32[4,128,128]{2,1,0:T(8,128)S(1)}, u32[]{:S(2)}) copy-start(f32[4,128,128]{2,1,0:T(8,128)S(1)} %convolution_select_fusion.1) | copy-start | bytes 786436
  40.1 11.8 %collective-permute-start.1 = (bf16[128,4,128]{0,2,1:T(8,128)(2,1)S(1)}, bf16[128,4,128]{0,2,1:T(8,128)(2,1)S(1)}, u32[]{:S(2)}, u32[]{:S(2)}) collective-permute-start(bf16[128,4,128]{0,2,1:T(8,128)(2,1)S(1)} %collective-permute-done), channel_id=1, source_target_pairs={{0,8},{8,16},{16,24},{24,32},{32,40},{40,48},{48,56},{56,64},{64,7... | collective-permute-start | bytes 393224 | tf_op jit(solution)/shard_map/ppermute | solution.py:40
  45.3 11.8 %collective-permute-start.5 = (bf16[128,4,128]{2,0,1:T(8,128)(2,1)S(1)}, bf16[128,4,128]{2,0,1:T(8,128)(2,1)S(1)}, u32[]{:S(2)}, u32[]{:S(2)}) collective-permute-start(bf16[128,4,128]{2,0,1:T(8,128)(2,1)S(1)} %collective-permute-done.4), channel_id=1, source_target_pairs={{0,8},{8,16},{16,24},{24,32},{32,40},{40,48},{48,56},{56,64},{64,7... | collective-permute-start | bytes 393224 | tf_op jit(solution)/shard_map/ppermute | solution.py:40
  49.2 11.8 %collective-permute-start.9 = (bf16[128,4,128]{2,0,1:T(8,128)(2,1)S(1)}, bf16[128,4,128]{2,0,1:T(8,128)(2,1)S(1)}, u32[]{:S(2)}, u32[]{:S(2)}) collective-permute-start(bf16[128,4,128]{2,0,1:T(8,128)(2,1)S(1)} %collective-permute-done.8), channel_id=1, source_target_pairs={{8,0},{16,8},{24,16},{32,24},{40,32},{48,40},{56,48},{64,56},{72,6... | collective-permute-start | bytes 393224 | tf_op jit(solution)/shard_map/ppermute | solution.py:40
  50.6 11.8 %collective-permute-start.17 = (bf16[128,4,128]{0,2,1:T(8,128)(2,1)S(1)}, bf16[128,4,128]{0,2,1:T(8,128)(2,1)S(1)}, u32[]{:S(2)}, u32[]{:S(2)}) collective-permute-start(bf16[128,4,128]{0,2,1:T(8,128)(2,1)S(1)} %collective-permute-done.16), channel_id=1, source_target_pairs={{8,0},{16,8},{24,16},{32,24},{40,32},{48,40},{56,48},{64,56},{72,6... | collective-permute-start | bytes 393224 | tf_op jit(solution)/shard_map/ppermute | solution.py:40
  51.9 11.8 %collective-permute-start.2 = (bf16[128,4,128]{0,2,1:T(8,128)(2,1)S(1)}, bf16[128,4,128]{0,2,1:T(8,128)(2,1)S(1)}, u32[]{:S(2)}, u32[]{:S(2)}) collective-permute-start(bf16[128,4,128]{0,2,1:T(8,128)(2,1)S(1)} %collective-permute-done.1), channel_id=1, source_target_pairs={{0,8},{8,16},{16,24},{24,32},{32,40},{40,48},{48,56},{56,64},{64,7... | collective-permute-start | bytes 393224 | tf_op jit(solution)/shard_map/ppermute | solution.py:40
  57.1 11.8 %collective-permute-start.6 = (bf16[128,4,128]{2,0,1:T(8,128)(2,1)S(1)}, bf16[128,4,128]{2,0,1:T(8,128)(2,1)S(1)}, u32[]{:S(2)}, u32[]{:S(2)}) collective-permute-start(bf16[128,4,128]{2,0,1:T(8,128)(2,1)S(1)} %collective-permute-done.5), channel_id=1, source_target_pairs={{0,8},{8,16},{16,24},{24,32},{32,40},{40,48},{48,56},{56,64},{64,7... | collective-permute-start | bytes 393224 | tf_op jit(solution)/shard_map/ppermute | solution.py:40
  61.0 13.0 %collective-permute-start.10 = (bf16[128,4,128]{2,0,1:T(8,128)(2,1)S(1)}, bf16[128,4,128]{2,0,1:T(8,128)(2,1)S(1)}, u32[]{:S(2)}, u32[]{:S(2)}) collective-permute-start(bf16[128,4,128]{2,0,1:T(8,128)(2,1)S(1)} %collective-permute-done.9), channel_id=1, source_target_pairs={{8,0},{16,8},{24,16},{32,24},{40,32},{48,40},{56,48},{64,56},{72,6... | collective-permute-start | bytes 393224 | tf_op jit(solution)/shard_map/ppermute | solution.py:40
  62.4 13.0 %collective-permute-start.18 = (bf16[128,4,128]{0,2,1:T(8,128)(2,1)S(1)}, bf16[128,4,128]{0,2,1:T(8,128)(2,1)S(1)}, u32[]{:S(2)}, u32[]{:S(2)}) collective-permute-start(bf16[128,4,128]{0,2,1:T(8,128)(2,1)S(1)} %collective-permute-done.17), channel_id=1, source_target_pairs={{8,0},{16,8},{24,16},{32,24},{40,32},{48,40},{56,48},{64,56},{72,6... | collective-permute-start | bytes 393224 | tf_op jit(solution)/shard_map/ppermute | solution.py:40
  63.7 13.0 %collective-permute-start.3 = (bf16[128,4,128]{0,2,1:T(8,128)(2,1)S(1)}, bf16[128,4,128]{0,2,1:T(8,128)(2,1)S(1)}, u32[]{:S(2)}, u32[]{:S(2)}) collective-permute-start(bf16[128,4,128]{0,2,1:T(8,128)(2,1)S(1)} %collective-permute-done.2), channel_id=1, source_target_pairs={{0,8},{8,16},{16,24},{24,32},{32,40},{40,48},{48,56},{56,64},{64,7... | collective-permute-start | bytes 393224 | tf_op jit(solution)/shard_map/ppermute | solution.py:40
  68.9 8.1 %collective-permute-start.7 = (bf16[128,4,128]{2,0,1:T(8,128)(2,1)S(1)}, bf16[128,4,128]{2,0,1:T(8,128)(2,1)S(1)}, u32[]{:S(2)}, u32[]{:S(2)}) collective-permute-start(bf16[128,4,128]{2,0,1:T(8,128)(2,1)S(1)} %collective-permute-done.6), channel_id=1, source_target_pairs={{0,8},{8,16},{16,24},{24,32},{32,40},{40,48},{48,56},{56,64},{64,7... | collective-permute-start | bytes 393224 | tf_op jit(solution)/shard_map/ppermute | solution.py:40
  74.1 6.9 %collective-permute-start.11 = (bf16[128,4,128]{2,0,1:T(8,128)(2,1)S(1)}, bf16[128,4,128]{2,0,1:T(8,128)(2,1)S(1)}, u32[]{:S(2)}, u32[]{:S(2)}) collective-permute-start(bf16[128,4,128]{2,0,1:T(8,128)(2,1)S(1)} %collective-permute-done.10), channel_id=1, source_target_pairs={{8,0},{16,8},{24,16},{32,24},{40,32},{48,40},{56,48},{64,56},{72,6... | collective-permute-start | bytes 393224 | tf_op jit(solution)/shard_map/ppermute | solution.py:40
  75.4 7.5 %collective-permute-start.19 = (bf16[128,4,128]{0,2,1:T(8,128)(2,1)S(1)}, bf16[128,4,128]{0,2,1:T(8,128)(2,1)S(1)}, u32[]{:S(2)}, u32[]{:S(2)}) collective-permute-start(bf16[128,4,128]{0,2,1:T(8,128)(2,1)S(1)} %collective-permute-done.18), channel_id=1, source_target_pairs={{8,0},{16,8},{24,16},{32,24},{40,32},{48,40},{56,48},{64,56},{72,6... | collective-permute-start | bytes 393224 | tf_op jit(solution)/shard_map/ppermute | solution.py:40
  77.7 7.5 %collective-permute-start.12 = (f32[4,128]{1,0:T(4,128)S(1)}, f32[4,128]{1,0:T(4,128)S(1)}, u32[]{:S(2)}, u32[]{:S(2)}) collective-permute-start(f32[4,128]{1,0:T(4,128)S(1)} %get-tuple-element.33), channel_id=1, source_target_pairs={{8,0},{16,8},{24,16},{32,24},{40,32},{48,40},{56,48},{64,56},{72,6... | collective-permute-start | bytes 6152 | tf_op jit(solution)/shard_map/ppermute | solution.py:40
  79.4 7.4 %collective-permute-start.20 = (f32[4,128]{1,0:T(4,128)S(1)}, f32[4,128]{1,0:T(4,128)S(1)}, u32[]{:S(2)}, u32[]{:S(2)}) collective-permute-start(f32[4,128]{1,0:T(4,128)S(1)} %get-tuple-element.39), channel_id=1, source_target_pairs={{8,0},{16,8},{24,16},{32,24},{40,32},{48,40},{56,48},{64,56},{72,6... | collective-permute-start | bytes 6152 | tf_op jit(solution)/shard_map/ppermute | solution.py:40
  84.4 51.6 %copy-start.15 = (pred[640,128]{1,0:T(8,128)(4,1)S(1)}, pred[640,128]{1,0:T(8,128)(4,1)}, u32[]{:S(2)}) copy-start(pred[640,128]{1,0:T(8,128)(4,1)} %compare_and_fusion) | copy-start | bytes 245764
  85.2 6.7 %collective-permute-start.13 = (f32[4,128]{1,0:T(4,128)S(1)}, f32[4,128]{1,0:T(4,128)S(1)}, u32[]{:S(2)}, u32[]{:S(2)}) collective-permute-start(f32[4,128]{1,0:T(4,128)S(1)} %collective-permute-done.12), channel_id=1, source_target_pairs={{8,0},{16,8},{24,16},{32,24},{40,32},{48,40},{56,48},{64,56},{72,6... | collective-permute-start | bytes 6152 | tf_op jit(solution)/shard_map/ppermute | solution.py:40
  86.8 36.9 %collective-permute-start.21 = (f32[4,128]{1,0:T(4,128)S(1)}, f32[4,128]{1,0:T(4,128)S(1)}, u32[]{:S(2)}, u32[]{:S(2)}) collective-permute-start(f32[4,128]{1,0:T(4,128)S(1)} %collective-permute-done.20), channel_id=1, source_target_pairs={{8,0},{16,8},{24,16},{32,24},{40,32},{48,40},{56,48},{64,56},{72,6... | collective-permute-start | bytes 6152 | tf_op jit(solution)/shard_map/ppermute | solution.py:40
  91.8 33.8 %collective-permute-start.14 = (f32[4,128]{1,0:T(4,128)S(1)}, f32[4,128]{1,0:T(4,128)S(1)}, u32[]{:S(2)}, u32[]{:S(2)}) collective-permute-start(f32[4,128]{1,0:T(4,128)S(1)} %collective-permute-done.13), channel_id=1, source_target_pairs={{8,0},{16,8},{24,16},{32,24},{40,32},{48,40},{56,48},{64,56},{72,6... | collective-permute-start | bytes 6152 | tf_op jit(solution)/shard_map/ppermute | solution.py:40
  94.4 45.9 %all-to-all-start.1 = ((f32[96,1,768]{2,1,0:T(1,128)}), f32[96,1,768]{2,1,0:T(1,128)S(1)}, u32[]{:S(2)}, u32[]{:S(2)}) async-start(f32[96,1,768]{2,1,0:T(1,128)} %copy.91), calls=%async_computation.1 | async-start | bytes 589824 | tf_op jit(solution)/shard_map/all_to_all | solution.py:33
  123.7 6.2 %collective-permute-start.22 = (f32[4,128]{1,0:T(4,128)S(1)}, f32[4,128]{1,0:T(4,128)S(1)}, u32[]{:S(2)}, u32[]{:S(2)}) collective-permute-start(f32[4,128]{1,0:T(4,128)S(1)} %collective-permute-done.21), channel_id=1, source_target_pairs={{8,0},{16,8},{24,16},{32,24},{40,32},{48,40},{56,48},{64,56},{72,6... | collective-permute-start | bytes 6152 | tf_op jit(solution)/shard_map/ppermute | solution.py:40
  125.6 6.2 %collective-permute-start.15 = (f32[4,128]{1,0:T(4,128)S(1)}, f32[4,128]{1,0:T(4,128)S(1)}, u32[]{:S(2)}, u32[]{:S(2)}) collective-permute-start(f32[4,128]{1,0:T(4,128)S(1)} %collective-permute-done.14), channel_id=1, source_target_pairs={{8,0},{16,8},{24,16},{32,24},{40,32},{48,40},{56,48},{64,56},{72,6... | collective-permute-start | bytes 6152 | tf_op jit(solution)/shard_map/ppermute | solution.py:40
  130.0 5.5 %collective-permute-start.23 = (f32[4,128]{1,0:T(4,128)S(1)}, f32[4,128]{1,0:T(4,128)S(1)}, u32[]{:S(2)}, u32[]{:S(2)}) collective-permute-start(f32[4,128]{1,0:T(4,128)S(1)} %collective-permute-done.22), channel_id=1, source_target_pairs={{8,0},{16,8},{24,16},{32,24},{40,32},{48,40},{56,48},{64,56},{72,6... | collective-permute-start | bytes 6152 | tf_op jit(solution)/shard_map/ppermute | solution.py:40
  156.5 34.2 %all-to-all-start.2 = ((f32[96,1,768]{2,1,0:T(1,128)}), f32[96,1,768]{2,1,0:T(1,128)}, u32[]{:S(2)}, u32[]{:S(2)}) async-start(f32[96,1,768]{2,1,0:T(1,128)} %bitcast.152), calls=%async_computation.2 | async-start | bytes 589824 | tf_op jit(solution)/shard_map/all_to_all | solution.py:24
  193.0 25.8 %all-to-all-start.3 = ((f32[96,1,768]{2,1,0:T(1,128)}), f32[96,1,768]{2,1,0:T(1,128)S(1)}, u32[]{:S(2)}, u32[]{:S(2)}) async-start(f32[96,1,768]{2,1,0:T(1,128)} %copy.109), calls=%async_computation.3 | async-start | bytes 589824 | tf_op jit(solution)/shard_map/all_to_all | solution.py:33
  (17 other events, 149.6 us)

commit v2 on v1

--- a/solution.py
+++ b/solution.py
@@ -14,28 +14,43 @@
 NORM_EPS = 1e-05
 
 
-def scan_states(state, axis, reverse):
-    count = lax.axis_size(axis)
-    flat = state.reshape(-1, LANES)
-    rows = flat.shape[0]
-    per = -(-rows // count)
-    flat = jnp.pad(flat, ((0, per * count - rows), (0, 0)))
-    pieces = flat.reshape(count, per * LANES)
-    gathered = lax.all_to_all(pieces, axis, 0, 0, tiled=True)
+def exclusive_sum(gathered, reverse):
+    count = gathered.shape[0]
     index = jnp.arange(count, dtype=jnp.int32)
     if reverse:
         mask = index[None, :] > index[:, None]
     else:
         mask = index[None, :] < index[:, None]
-    sums = jnp.einsum(
-        "ij,jf->if", mask.astype(jnp.float32), gathered, precision=PRECISE
-    )
-    returned = lax.all_to_all(sums, axis, 0, 0, tiled=True)
-    return returned.reshape(count * per, LANES)[:rows].reshape(state.shape)
+    return jnp.einsum("ij,jf->if", mask.astype(jnp.float32), gathered, precision=PRECISE)
+
+
+def padded_pieces(vector, count):
+    per = -(-vector.shape[0] // count)
+    return jnp.pad(vector, (0, per * count - vector.shape[0])).reshape(count, per)
+
+
+def scan_states(state, outer, inner, reverse):
+    flat = state.reshape(-1)
+    pieces = padded_pieces(flat, lax.axis_size(inner))
+    gathered = lax.all_to_all(pieces, inner, 0, 0, tiled=True)
+    within = exclusive_sum(gathered, reverse)
+    group_total = jnp.sum(gathered, axis=0)
+    parts = padded_pieces(group_total, lax.axis_size(outer))
+    gathered_totals = lax.all_to_all(parts, outer, 0, 0, tiled=True)
+    across = lax.all_to_all(exclusive_sum(gathered_totals, reverse), outer, 0, 0, tiled=True)
+    across = across.reshape(-1)[: group_total.shape[0]]
+    returned = lax.all_to_all(within + across[None, :], inner, 0, 0, tiled=True)
+    return returned.reshape(-1)[: flat.shape[0]].reshape(state.shape)
+
+
+def head_sum(values, axis):
+    count = lax.axis_size(axis)
+    copies = jnp.broadcast_to(values[None], (count,) + values.shape)
+    return jnp.sum(lax.all_to_all(copies, axis, 0, 0, tiled=True), axis=0)
 
 
 def passed_along(block, axis, distance):
-    devices = range(lax.axis_size(axis))
+    devices = range(lax.axis_size(axis[0]) * lax.axis_size(axis[1]))
     route = [(i - distance, i) for i in devices if i - distance in devices]
     return lax.ppermute(block, axis, route)
 
@@ -122,14 +137,17 @@
     return (key_grad, value_grad)
 
 
+CTX = ("cy", "cz")
+
+
 def shards(lin_q, lin_k, lin_v, win_q, win_k, win_v, grad_out):
     row_count = lin_q.shape[0]
     head_count = lin_q.shape[1] // HD
     shaped = (row_count, head_count, HD)
     flat = (row_count, head_count * HD)
     span = WIN // row_count
-    total_rows = row_count * lax.axis_size("ctx")
-    first_pos = lax.axis_index("ctx") * row_count
+    total_rows = row_count * lax.axis_size(CTX[0]) * lax.axis_size(CTX[1])
+    first_pos = lax.axis_index(CTX) * row_count
     win_query = win_q.reshape(shaped)
     win_key = win_k.reshape(shaped)
     win_value = win_v.reshape(shaped)
@@ -137,11 +155,11 @@
 
     earlier_keys, earlier_values = [], []
     later_queries, later_upstreams = [], []
-    key_pair = (win_key, win_value)
-    row_pair = (win_query, cotangent)
+    key_pair = jnp.stack([win_key, win_value])
+    row_pair = jnp.stack([win_query, cotangent])
     for _ in range(span):
-        key_pair = passed_along(key_pair, "ctx", 1)
-        row_pair = passed_along(row_pair, "ctx", -1)
+        key_pair = passed_along(key_pair, CTX, 1)
+        row_pair = passed_along(row_pair, CTX, -1)
         earlier_keys.insert(0, key_pair[0])
         earlier_values.insert(0, key_pair[1])
         later_queries.append(row_pair[0])
@@ -151,11 +169,12 @@
     lin_key = lin_k.reshape(shaped)
     lin_value = lin_v.reshape(shaped)
     key_state = jnp.einsum("shd,she->hde", lin_key, lin_value, preferred_element_type=jnp.float32)
-    prefix = scan_states(key_state, "ctx", False)
+    prefix = scan_states(key_state, CTX[0], CTX[1], False)
     lin_out, lin_scores = linear_forward(lin_query, lin_key, lin_value, prefix)
     upstream = grad_out.reshape(shaped).astype(jnp.float32)
-    square_sum, cross_sum = lax.psum(
-        (jnp.sum(lin_out * lin_out, axis=(1, 2)), jnp.sum(upstream * lin_out, axis=(1, 2))), "head"
+    square_sum, cross_sum = head_sum(
+        jnp.stack([jnp.sum(lin_out * lin_out, axis=(1, 2)), jnp.sum(upstream * lin_out, axis=(1, 2))]),
+        "head",
     )
     features = head_count * HD * lax.axis_size("head")
     inv_rms = lax.rsqrt(square_sum / features + NORM_EPS)
@@ -166,7 +185,7 @@
     query_state = jnp.einsum(
         "thd,the->hde", lin_query, lin_dout, preferred_element_type=jnp.float32
     )
-    suffix = scan_states(query_state, "ctx", True)
+    suffix = scan_states(query_state, CTX[0], CTX[1], True)
     grad_q, grad_k, grad_v = linear_backward(
         lin_query, lin_key, lin_value, lin_dout, lin_scores, prefix, suffix
     )
@@ -178,9 +197,9 @@
     )
 
     later_totals, later_dots = [], []
-    stat_pair = (log_total, row_dot)
+    stat_pair = jnp.stack([log_total, row_dot])
     for _ in range(span):
-        stat_pair = passed_along(stat_pair, "ctx", -1)
+        stat_pair = passed_along(stat_pair, CTX, -1)
         later_totals.append(stat_pair[0])
         later_dots.append(stat_pair[1])
     query_ext = jnp.concatenate([win_query] + later_queries, axis=0)
@@ -202,11 +221,27 @@
     )
 
 
+def ctx_groups(mesh):
+    column = list(mesh.devices[:, 0])
+    count = len(column)
+    try:
+        slow = [tuple(d.coords)[1] for d in column]
+    except (AttributeError, TypeError, IndexError):
+        return 1, count
+    inner = next((i for i, y in enumerate(slow) if y != slow[0]), count)
+    if count % inner:
+        inner = count
+    return count // inner, inner
+
+
 def solution(mesh):
-    spec = P("ctx", "head")
+    outer, inner = ctx_groups(mesh)
+    heads = mesh.devices.shape[1]
+    split = jax.sharding.Mesh(mesh.devices.reshape(outer, inner, heads), CTX + ("head",))
+    spec = P(CTX, "head")
     return jax.shard_map(
         shards,
-        mesh=mesh,
+        mesh=split,
         in_specs=(spec,) * 7,
         out_specs=(spec,) * 7,
         check_vma=False,

time: 225 us -> 217 us (0.964)
  starting transfers between devices: 128 us -> 97.8 us
  waiting for transfers between devices: 44.1 us -> 69.4 us
  blocking collectives: 9.99 us -> 0 us
  local copies, waits for them, and re-layouts: 19.1 us -> 28.6 us
  matrix products: 15.7 us -> 13.4 us
    ppermute x24 -> x12, starting transfers between devices: 57.7 us -> 26.5 us  [passed_along(): return lax.ppermute(block, axis, route)]
    all_to_all x4 -> x9, waiting for transfers between devices: 31.8 us -> 47.6 us  [the longest x2 13.7 us: scan_states(): gathered_totals = lax.all_to_all(parts, outer, 0, 0, tiled=True)]
    psum x1 -> x0, blocking collectives: 9.99 us -> none  [shards(): lax.psum((jnp.sum(lin_out * lin_out, axis=(1, 2)), jnp.sum(upstream * lin...]
    ppermute x24 -> x12, waiting for transfers between devices: 12.3 us -> 21.8 us  [passed_along(): return lax.ppermute(block, axis, route)]
    all_to_all x2 -> x8, local copies, waits for them, and re-layouts: 2.03 us -> 6.8 us  [the longest x2 2.16 us: scan_states(): gathered = lax.all_to_all(pieces, inner, 0, 0, tiled=True)]
    unnamed x76 -> x74, local copies, waits for them, and re-layouts: 12.5 us -> 16.5 us
    all_to_all x4 -> x9, starting transfers between devices: 70.4 us -> 71.3 us  [the longest x2 28.3 us: scan_states(): gathered = lax.all_to_all(pieces, inner, 0, 0, tiled=True)]
  transfers between devices with their start and end apart: 28 -> 21, of which waited for: 9 -> 13; matrix products, arithmetic and copies ran while one was open for 11% -> 13% of each run, Pallas kernels for 0% -> 0%
where the time goes in v2:
time: 217 us; the launch traced here: 215 us
  starting transfers between devices  97.8 us (45%)
  waiting for transfers between devices  69.4 us (32%)
  local copies, waits for them, and re-layouts  28.6 us (13%)
  matrix products  13.4 us (6%)
  other arithmetic  4.04 us (2%)
    all_to_all x2, starting transfers between devices, scan_states(): gathered = lax.all_to_all(pieces, inner, 0, 0, tiled=True)  28.3 us
    ppermute x12, starting transfers between devices, passed_along(): return lax.ppermute(block, axis, route)  26.5 us
    all_to_all x2, starting transfers between devices, scan_states(): gathered_totals = lax.all_to_all(parts, outer, 0, 0, tiled=True)  24.5 us
    ppermute x12, waiting for transfers between devices, passed_along(): return lax.ppermute(block, axis, route)  21.8 us
    unnamed x74, local copies, waits for them, and re-layouts  16.5 us
    all_to_all x2, waiting for transfers between devices, scan_states(): gathered_totals = lax.all_to_all(parts, outer, 0, 0, tiled=True)  13.7 us
    all_to_all x2, waiting for transfers between devices, scan_states(): returned = lax.all_to_all(within + across[None, :], inner, 0, 0, tiled=True)  12.6 us
    all_to_all x2, waiting for transfers between devices, scan_states(): lax.all_to_all(exclusive_sum(gathered_totals, reverse), outer, 0, 0, tile...  10.7 us
  transfers between devices with their start and end apart: 21, of which 13 were waited for; matrix products, arithmetic and copies ran while one was open for 13% of the time, Pallas kernels for 0%

profile of v2, /device:TPU:6, one launch (start us, length us, event | category | flops | bytes accessed | tf_op | source)
XLA Modules:
  0.0 214.8 jit_solution(2837364295147511397)
XLA Ops:
  3.1 4.4 %collective-permute-start = (bf16[2,128,4,128]{3,1,2,0:T(8,128)(2,1)S(1)}, bf16[2,128,4,128]{3,1,2,0:T(8,128)(2,1)S(1)}, u32[]{:S(2)}, u32[]{:S(2)}) collective-permute-start(bf16[2,128,4,128]{3,1,2,0:T(8,128)(2,1)S(1)} %pad_maximum_fusion), channel_id=1, source_target_pairs={{0,8},{8,16},{16,24},{24,32},{32,40},{40,48},{48,56},{56,64},{64,7... | collective-permute-start | bytes 786440 | tf_op jit(solution)/shard_map/ppermute | solution.py:55
  9.0 14.2 %all-to-all-start = ((f32[12,1,5462]{2,1,0:T(1,128)}), f32[12,1,5462]{2,1,0:T(1,128)S(1)}, u32[]{:S(2)}, u32[]{:S(2)}) async-start(f32[12,1,5462]{2,1,0:T(1,128)} %all_to_all.59), calls=%async_computation | async-start | bytes 528384 | tf_op jit(solution)/shard_map/all_to_all | solution.py:35
  28.0 4.6 %collective-permute-start.1 = (bf16[2,128,4,128]{3,1,2,0:T(8,128)(2,1)S(1)}, bf16[2,128,4,128]{3,1,2,0:T(8,128)(2,1)S(1)}, u32[]{:S(2)}, u32[]{:S(2)}) collective-permute-start(bf16[2,128,4,128]{3,1,2,0:T(8,128)(2,1)S(1)} %collective-permute-done), channel_id=1, source_target_pairs={{0,8},{8,16},{16,24},{24,32},{32,40},{40,48},{48,56},{56,64},{64,7... | collective-permute-start | bytes 786440 | tf_op jit(solution)/shard_map/ppermute | solution.py:55
  32.6 6.8 %collective-permute-done.4 = bf16[2,128,4,128]{1,3,2,0:T(8,128)(2,1)S(1)} collective-permute-done((bf16[2,128,4,128]{1,3,2,0:T(8,128)(2,1)}, bf16[2,128,4,128]{1,3,2,0:T(8,128)(2,1)S(1)}, u32[]{:S(2)}, u32[]{:S(2)}) %collective-permute-start.4) | collective-permute-done | bytes 262176 | tf_op jit(solution)/shard_map/ppermute | solution.py:55
  41.9 5.2 %collective-permute-start.2 = (bf16[2,128,4,128]{3,1,2,0:T(8,128)(2,1)S(1)}, bf16[2,128,4,128]{3,1,2,0:T(8,128)(2,1)}, u32[]{:S(2)}, u32[]{:S(2)}) collective-permute-start(bf16[2,128,4,128]{3,1,2,0:T(8,128)(2,1)S(1)} %collective-permute-done.1), channel_id=1, source_target_pairs={{0,8},{8,16},{16,24},{24,32},{32,40},{40,48},{48,56},{56,64},{64,7... | collective-permute-start | bytes 786440 | tf_op jit(solution)/shard_map/ppermute | solution.py:55
  47.2 1.3 collective-permute-done.5
  50.7 15.2 %all-to-all-start.1 = ((f32[8,1,683]{2,1,0:T(1,128)}), f32[8,1,683]{2,1,0:T(1,128)S(1)}, u32[]{:S(2)}, u32[]{:S(2)}) async-start(f32[8,1,683]{2,1,0:T(1,128)} %all_to_all.62), calls=%async_computation.1 | async-start | bytes 49152 | tf_op jit(solution)/shard_map/all_to_all | solution.py:39
  65.9 1.7 fusion.49
  67.6 6.1 %all-to-all-done.1 = f32[8,1,683]{2,1,0:T(1,128)S(1)} async-done(((f32[8,1,683]{2,1,0:T(1,128)}), f32[8,1,683]{2,1,0:T(1,128)S(1)}, u32[]{:S(2)}, u32[]{:S(2)}) %all-to-all-start.1) | async-done | bytes 21888 | tf_op jit(solution)/shard_map/all_to_all | solution.py:39
  74.5 3.3 %all-to-all-start.2 = ((f32[8,1,683]{2,1,0:T(1,128)}), f32[8,1,683]{2,1,0:T(1,128)S(1)}, u32[]{:S(2)}, u32[]{:S(2)}) async-start(f32[8,1,683]{2,1,0:T(1,128)} %copy.197), calls=%async_computation.2 | async-start | bytes 49152 | tf_op jit(solution)/shard_map/all_to_all | solution.py:40
  77.8 2.0 collective-permute-start.3
  79.8 1.3 collective-permute-start.7
  81.8 4.1 %all-to-all-done.2 = f32[8,1,683]{2,1,0:T(1,128)S(1)} async-done(((f32[8,1,683]{2,1,0:T(1,128)}), f32[8,1,683]{2,1,0:T(1,128)S(1)}, u32[]{:S(2)}, u32[]{:S(2)}) %all-to-all-start.2) | async-done | bytes 21888 | tf_op jit(solution)/shard_map/all_to_all | solution.py:40
  87.3 3.5 %all-to-all-start.3 = ((f32[12,1,5462]{2,1,0:T(1,128)}), f32[12,1,5462]{2,1,0:T(1,128)S(1)}, u32[]{:S(2)}, u32[]{:S(2)}) async-start(f32[12,1,5462]{2,1,0:T(1,128)} %copy.198), calls=%async_computation.3 | async-start | bytes 528384 | tf_op jit(solution)/shard_map/all_to_all | solution.py:42
  97.3 1.7 fusion.47
  102.2 4.2 %collective-permute-done.9 = f32[2,4,128]{2,1,0:T(4,128)S(1)} collective-permute-done((f32[2,4,128]{2,1,0:T(4,128)S(1)}, f32[2,4,128]{2,1,0:T(4,128)S(1)}, u32[]{:S(2)}, u32[]{:S(2)}) %collective-permute-start.9) | collective-permute-done | bytes 4128 | tf_op jit(solution)/shard_map/ppermute | solution.py:55
  107.7 4.2 %collective-permute-done.10 = f32[2,4,128]{2,1,0:T(4,128)S(1)} collective-permute-done((f32[2,4,128]{2,1,0:T(4,128)S(1)}, f32[2,4,128]{2,1,0:T(4,128)S(1)}, u32[]{:S(2)}, u32[]{:S(2)}) %collective-permute-start.10) | collective-permute-done | bytes 4128 | tf_op jit(solution)/shard_map/ppermute | solution.py:55
  113.2 4.2 %collective-permute-done.11 = f32[2,4,128]{2,1,0:T(4,128)S(1)} collective-permute-done((f32[2,4,128]{2,1,0:T(4,128)S(1)}, f32[2,4,128]{2,1,0:T(4,128)S(1)}, u32[]{:S(2)}, u32[]{:S(2)}) %collective-permute-start.11) | collective-permute-done | bytes 4128 | tf_op jit(solution)/shard_map/ppermute | solution.py:55
  121.2 4.8 %all-to-all-start.4 = ((f32[8,2,128]{2,1,0:T(2,128)}), f32[8,2,128]{2,1,0:T(2,128)S(1)}, u32[]{:S(2)}, u32[]{:S(2)}) async-start(f32[8,2,128]{2,1,0:T(2,128)} %broadcast_in_dim.38), calls=%async_computation.4 | async-start | bytes 16384 | tf_op jit(solution)/shard_map/all_to_all | solution.py:49
  126.0 1.8 fusion.6
  127.7 1.5 all-to-all-done.4
  132.4 14.1 %all-to-all-start.5 = ((f32[12,1,5462]{2,1,0:T(1,128)}), f32[12,1,5462]{2,1,0:T(1,128)S(1)}, u32[]{:S(2)}, u32[]{:S(2)}) async-start(f32[12,1,5462]{2,1,0:T(1,128)} %all_to_all.70), calls=%async_computation.5 | async-start | bytes 528384 | tf_op jit(solution)/shard_map/all_to_all | solution.py:35
  146.5 2.1 fusion.19
  149.3 1.4 convolution_convert_fusion
  151.5 1.7 fusion.18
  153.2 9.1 %all-to-all-done.5 = f32[12,1,5462]{2,1,0:T(1,128)S(1)} async-done(((f32[12,1,5462]{2,1,0:T(1,128)}), f32[12,1,5462]{2,1,0:T(1,128)S(1)}, u32[]{:S(2)}, u32[]{:S(2)}) %all-to-all-start.5) | async-done | bytes 262208 | tf_op jit(solution)/shard_map/all_to_all | solution.py:35
  163.2 9.3 %all-to-all-start.6 = ((f32[8,1,683]{2,1,0:T(1,128)}), f32[8,1,683]{2,1,0:T(1,128)S(1)}, u32[]{:S(2)}, u32[]{:S(2)}) async-start(f32[8,1,683]{2,1,0:T(1,128)} %all_to_all.73), calls=%async_computation.6 | async-start | bytes 49152 | tf_op jit(solution)/shard_map/all_to_all | solution.py:39
  172.8 7.6 %all-to-all-done.6 = f32[8,1,683]{2,1,0:T(1,128)S(1)} async-done(((f32[8,1,683]{2,1,0:T(1,128)}), f32[8,1,683]{2,1,0:T(1,128)S(1)}, u32[]{:S(2)}, u32[]{:S(2)}) %all-to-all-start.6) | async-done | bytes 21888 | tf_op jit(solution)/shard_map/all_to_all | solution.py:39
  181.1 3.3 %all-to-all-start.7 = ((f32[8,1,683]{2,1,0:T(1,128)}), f32[8,1,683]{2,1,0:T(1,128)S(1)}, u32[]{:S(2)}, u32[]{:S(2)}) async-start(f32[8,1,683]{2,1,0:T(1,128)} %copy.222), calls=%async_computation.7 | async-start | bytes 49152 | tf_op jit(solution)/shard_map/all_to_all | solution.py:40
  185.7 6.7 %all-to-all-done.7 = f32[8,1,683]{2,1,0:T(1,128)S(1)} async-done(((f32[8,1,683]{2,1,0:T(1,128)}), f32[8,1,683]{2,1,0:T(1,128)S(1)}, u32[]{:S(2)}, u32[]{:S(2)}) %all-to-all-start.7) | async-done | bytes 21888 | tf_op jit(solution)/shard_map/all_to_all | solution.py:40
  193.8 3.5 %all-to-all-start.8 = ((f32[12,1,5462]{2,1,0:T(1,128)}), f32[12,1,5462]{2,1,0:T(1,128)S(1)}, u32[]{:S(2)}, u32[]{:S(2)}) async-start(f32[12,1,5462]{2,1,0:T(1,128)} %copy.223), calls=%async_computation.8 | async-start | bytes 528384 | tf_op jit(solution)/shard_map/all_to_all | solution.py:42
  199.0 12.6 %all-to-all-done.8 = f32[12,1,5462]{2,1,0:T(1,128)S(1)} async-done(((f32[12,1,5462]{2,1,0:T(1,128)}), f32[12,1,5462]{2,1,0:T(1,128)S(1)}, u32[]{:S(2)}, u32[]{:S(2)}) %all-to-all-start.8) | async-done | bytes 262208 | tf_op jit(solution)/shard_map/all_to_all | solution.py:42
  (161 shorter events, 45.8 us)
Async XLA Ops:
  0.6 25.7 %copy-start = (bf16[128,512]{1,0:T(8,128)(2,1)S(1)}, bf16[128,512]{1,0:T(8,128)(2,1)}, u32[]{:S(2)}) copy-start(bf16[128,512]{1,0:T(8,128)(2,1)} %param.7) | copy-start | bytes 393220
  1.8 39.2 %copy-start.8 = (bf16[128,512]{0,1:T(8,128)(2,1)}, bf16[128,512]{0,1:T(8,128)(2,1)S(1)}, u32[]{:S(2)}) copy-start(bf16[128,512]{0,1:T(8,128)(2,1)S(1)} %copy.204) | copy-start | bytes 393220
  2.9 64.7 %copy-start.14 = (bf16[128,512]{0,1:T(8,128)(2,1)}, bf16[128,512]{0,1:T(8,128)(2,1)S(1)}, u32[]{:S(2)}) copy-start(bf16[128,512]{0,1:T(8,128)(2,1)S(1)} %copy.203) | copy-start | bytes 393220
  3.1 20.2 %copy-start.18 = (bf16[128,512]{1,0:T(8,128)(2,1)S(1)}, bf16[128,512]{1,0:T(8,128)(2,1)}, u32[]{:S(2)}) copy-start(bf16[128,512]{1,0:T(8,128)(2,1)} %param.10) | copy-start | bytes 393220
  3.1 20.3 %copy-start.19 = (bf16[128,512]{1,0:T(8,128)(2,1)S(1)}, bf16[128,512]{1,0:T(8,128)(2,1)}, u32[]{:S(2)}) copy-start(bf16[128,512]{1,0:T(8,128)(2,1)} %param.13) | copy-start | bytes 393220
  3.1 24.9 %collective-permute-start = (bf16[2,128,4,128]{3,1,2,0:T(8,128)(2,1)S(1)}, bf16[2,128,4,128]{3,1,2,0:T(8,128)(2,1)S(1)}, u32[]{:S(2)}, u32[]{:S(2)}) collective-permute-start(bf16[2,128,4,128]{3,1,2,0:T(8,128)(2,1)S(1)} %pad_maximum_fusion), channel_id=1, source_target_pairs={{0,8},{8,16},{16,24},{24,32},{32,40},{40,48},{48,56},{56,64},{64,7... | collective-permute-start | bytes 786440 | tf_op jit(solution)/shard_map/ppermute | solution.py:55
  9.0 40.8 %all-to-all-start = ((f32[12,1,5462]{2,1,0:T(1,128)}), f32[12,1,5462]{2,1,0:T(1,128)S(1)}, u32[]{:S(2)}, u32[]{:S(2)}) async-start(f32[12,1,5462]{2,1,0:T(1,128)} %all_to_all.59), calls=%async_computation | async-start | bytes 528384 | tf_op jit(solution)/shard_map/all_to_all | solution.py:35
  24.3 15.1 %collective-permute-start.4 = (bf16[2,128,4,128]{1,3,2,0:T(8,128)(2,1)}, bf16[2,128,4,128]{1,3,2,0:T(8,128)(2,1)S(1)}, u32[]{:S(2)}, u32[]{:S(2)}) collective-permute-start(bf16[2,128,4,128]{1,3,2,0:T(8,128)(2,1)} %pad_maximum_fusion.1), channel_id=1, source_target_pairs={{8,0},{16,8},{24,16},{32,24},{40,32},{48,40},{56,48},{64,56},{72,6... | collective-permute-start | bytes 786440 | tf_op jit(solution)/shard_map/ppermute | solution.py:55
  28.0 13.9 %collective-permute-start.1 = (bf16[2,128,4,128]{3,1,2,0:T(8,128)(2,1)S(1)}, bf16[2,128,4,128]{3,1,2,0:T(8,128)(2,1)S(1)}, u32[]{:S(2)}, u32[]{:S(2)}) collective-permute-start(bf16[2,128,4,128]{3,1,2,0:T(8,128)(2,1)S(1)} %collective-permute-done), channel_id=1, source_target_pairs={{0,8},{8,16},{16,24},{24,32},{32,40},{40,48},{48,56},{56,64},{64,7... | collective-permute-start | bytes 786440 | tf_op jit(solution)/shard_map/ppermute | solution.py:55
  39.4 9.1 %collective-permute-start.5 = (bf16[2,128,4,128]{1,3,2,0:T(8,128)(2,1)S(1)}, bf16[2,128,4,128]{1,3,2,0:T(8,128)(2,1)}, u32[]{:S(2)}, u32[]{:S(2)}) collective-permute-start(bf16[2,128,4,128]{1,3,2,0:T(8,128)(2,1)S(1)} %collective-permute-done.4), channel_id=1, source_target_pairs={{8,0},{16,8},{24,16},{32,24},{40,32},{48,40},{56,48},{64,56},{72,6... | collective-permute-start | bytes 786440 | tf_op jit(solution)/shard_map/ppermute | solution.py:55
  41.9 45.4 %copy-start.17 = (bf16[2,128,4,128]{3,1,2,0:T(8,128)(2,1)}, bf16[2,128,4,128]{3,1,2,0:T(8,128)(2,1)S(1)}, u32[]{:S(2)}) copy-start(bf16[2,128,4,128]{3,1,2,0:T(8,128)(2,1)S(1)} %collective-permute-done.1) | copy-start | bytes 786436
  41.9 35.9 %collective-permute-start.2 = (bf16[2,128,4,128]{3,1,2,0:T(8,128)(2,1)S(1)}, bf16[2,128,4,128]{3,1,2,0:T(8,128)(2,1)}, u32[]{:S(2)}, u32[]{:S(2)}) collective-permute-start(bf16[2,128,4,128]{3,1,2,0:T(8,128)(2,1)S(1)} %collective-permute-done.1), channel_id=1, source_target_pairs={{0,8},{8,16},{16,24},{24,32},{32,40},{40,48},{48,56},{56,64},{64,7... | collective-permute-start | bytes 786440 | tf_op jit(solution)/shard_map/ppermute | solution.py:55
  48.5 31.3 %collective-permute-start.6 = (bf16[2,128,4,128]{1,3,2,0:T(8,128)(2,1)}, bf16[2,128,4,128]{1,3,2,0:T(8,128)(2,1)S(1)}, u32[]{:S(2)}, u32[]{:S(2)}) collective-permute-start(bf16[2,128,4,128]{1,3,2,0:T(8,128)(2,1)} %collective-permute-done.5), channel_id=1, source_target_pairs={{8,0},{16,8},{24,16},{32,24},{40,32},{48,40},{56,48},{64,56},{72,6... | collective-permute-start | bytes 786440 | tf_op jit(solution)/shard_map/ppermute | solution.py:55
  50.7 23.0 %all-to-all-start.1 = ((f32[8,1,683]{2,1,0:T(1,128)}), f32[8,1,683]{2,1,0:T(1,128)S(1)}, u32[]{:S(2)}, u32[]{:S(2)}) async-start(f32[8,1,683]{2,1,0:T(1,128)} %all_to_all.62), calls=%async_computation.1 | async-start | bytes 49152 | tf_op jit(solution)/shard_map/all_to_all | solution.py:39
  74.5 11.4 %all-to-all-start.2 = ((f32[8,1,683]{2,1,0:T(1,128)}), f32[8,1,683]{2,1,0:T(1,128)S(1)}, u32[]{:S(2)}, u32[]{:S(2)}) async-start(f32[8,1,683]{2,1,0:T(1,128)} %copy.197), calls=%async_computation.2 | async-start | bytes 49152 | tf_op jit(solution)/shard_map/all_to_all | solution.py:40
  77.8 13.0 %collective-permute-start.3 = (bf16[2,128,4,128]{3,1,2,0:T(8,128)(2,1)}, bf16[2,128,4,128]{3,1,2,0:T(8,128)(2,1)}, u32[]{:S(2)}, u32[]{:S(2)}) collective-permute-start(bf16[2,128,4,128]{3,1,2,0:T(8,128)(2,1)} %collective-permute-done.2), channel_id=1, source_target_pairs={{0,8},{8,16},{16,24},{24,32},{32,40},{40,48},{48,56},{56,64},{64,7... | collective-permute-start | bytes 786440 | tf_op jit(solution)/shard_map/ppermute | solution.py:55
  79.8 17.5 %collective-permute-start.7 = (bf16[2,128,4,128]{1,3,2,0:T(8,128)(2,1)S(1)}, bf16[2,128,4,128]{1,3,2,0:T(8,128)(2,1)}, u32[]{:S(2)}, u32[]{:S(2)}) collective-permute-start(bf16[2,128,4,128]{1,3,2,0:T(8,128)(2,1)S(1)} %collective-permute-done.6), channel_id=1, source_target_pairs={{8,0},{16,8},{24,16},{32,24},{40,32},{48,40},{56,48},{64,56},{72,6... | collective-permute-start | bytes 786440 | tf_op jit(solution)/shard_map/ppermute | solution.py:55
  87.3 31.3 %all-to-all-start.3 = ((f32[12,1,5462]{2,1,0:T(1,128)}), f32[12,1,5462]{2,1,0:T(1,128)S(1)}, u32[]{:S(2)}, u32[]{:S(2)}) async-start(f32[12,1,5462]{2,1,0:T(1,128)} %copy.198), calls=%async_computation.3 | async-start | bytes 528384 | tf_op jit(solution)/shard_map/all_to_all | solution.py:42
  95.4 5.5 %collective-permute-start.8 = (f32[2,4,128]{2,1,0:T(4,128)S(1)}, f32[2,4,128]{2,1,0:T(4,128)S(1)}, u32[]{:S(2)}, u32[]{:S(2)}) collective-permute-start(f32[2,4,128]{2,1,0:T(4,128)S(1)} %pad_maximum_fusion.2), channel_id=1, source_target_pairs={{8,0},{16,8},{24,16},{32,24},{40,32},{48,40},{56,48},{64,56},{72,6... | collective-permute-start | bytes 12296 | tf_op jit(solution)/shard_map/ppermute | solution.py:55
  99.0 21.6 %copy-start.1 = (bf16[640,4,128]{0,2,1:T(8,128)(2,1)}, bf16[640,4,128]{0,2,1:T(8,128)(2,1)S(1)}, u32[]{:S(2)}) copy-start(bf16[640,4,128]{0,2,1:T(8,128)(2,1)S(1)} %get-tuple-element.46) | copy-start | bytes 1966084
  100.9 5.5 %collective-permute-start.9 = (f32[2,4,128]{2,1,0:T(4,128)S(1)}, f32[2,4,128]{2,1,0:T(4,128)S(1)}, u32[]{:S(2)}, u32[]{:S(2)}) collective-permute-start(f32[2,4,128]{2,1,0:T(4,128)S(1)} %collective-permute-done.8), channel_id=1, source_target_pairs={{8,0},{16,8},{24,16},{32,24},{40,32},{48,40},{56,48},{64,56},{72,6... | collective-permute-start | bytes 12296 | tf_op jit(solution)/shard_map/ppermute | solution.py:55
  106.4 5.5 %collective-permute-start.10 = (f32[2,4,128]{2,1,0:T(4,128)S(1)}, f32[2,4,128]{2,1,0:T(4,128)S(1)}, u32[]{:S(2)}, u32[]{:S(2)}) collective-permute-start(f32[2,4,128]{2,1,0:T(4,128)S(1)} %collective-permute-done.9), channel_id=1, source_target_pairs={{8,0},{16,8},{24,16},{32,24},{40,32},{48,40},{56,48},{64,56},{72,6... | collective-permute-start | bytes 12296 | tf_op jit(solution)/shard_map/ppermute | solution.py:55
  111.9 5.5 %collective-permute-start.11 = (f32[2,4,128]{2,1,0:T(4,128)S(1)}, f32[2,4,128]{2,1,0:T(4,128)S(1)}, u32[]{:S(2)}, u32[]{:S(2)}) collective-permute-start(f32[2,4,128]{2,1,0:T(4,128)S(1)} %collective-permute-done.10), channel_id=1, source_target_pairs={{8,0},{16,8},{24,16},{32,24},{40,32},{48,40},{56,48},{64,56},{72,6... | collective-permute-start | bytes 12296 | tf_op jit(solution)/shard_map/ppermute | solution.py:55
  121.2 8.0 %all-to-all-start.4 = ((f32[8,2,128]{2,1,0:T(2,128)}), f32[8,2,128]{2,1,0:T(2,128)S(1)}, u32[]{:S(2)}, u32[]{:S(2)}) async-start(f32[8,2,128]{2,1,0:T(2,128)} %broadcast_in_dim.38), calls=%async_computation.4 | async-start | bytes 16384 | tf_op jit(solution)/shard_map/all_to_all | solution.py:49
  129.3 17.2 %copy-start.9 = (bf16[128,512]{0,1:T(8,128)(2,1)S(1)}, bf16[128,512]{0,1:T(8,128)(2,1)}, u32[]{:S(2)}) copy-start(bf16[128,512]{0,1:T(8,128)(2,1)} %copy-done.8) | copy-start | bytes 393220
  129.3 17.2 %copy-start.23 = (f32[4,640]{1,0:T(4,128)S(1)}, f32[4,640]{1,0:T(4,128)}, u32[]{:S(2)}) copy-start(f32[4,640]{1,0:T(4,128)} %copy-done.22) | copy-start | bytes 30724
  132.4 29.9 %all-to-all-start.5 = ((f32[12,1,5462]{2,1,0:T(1,128)}), f32[12,1,5462]{2,1,0:T(1,128)S(1)}, u32[]{:S(2)}, u32[]{:S(2)}) async-start(f32[12,1,5462]{2,1,0:T(1,128)} %all_to_all.70), calls=%async_computation.5 | async-start | bytes 528384 | tf_op jit(solution)/shard_map/all_to_all | solution.py:35
  151.5 21.0 %copy-start.11 = (bf16[128,512]{1,0:T(8,128)(2,1)S(1)}, bf16[128,512]{1,0:T(8,128)(2,1)}, u32[]{:S(2)}) copy-start(bf16[128,512]{1,0:T(8,128)(2,1)} %param.9) | copy-start | bytes 393220
  151.5 33.0 %copy-start.13 = (bf16[128,512]{0,1:T(8,128)(2,1)S(1)}, bf16[128,512]{0,1:T(8,128)(2,1)}, u32[]{:S(2)}) copy-start(bf16[128,512]{0,1:T(8,128)(2,1)} %copy-done.12) | copy-start | bytes 393220
  163.2 17.1 %all-to-all-start.6 = ((f32[8,1,683]{2,1,0:T(1,128)}), f32[8,1,683]{2,1,0:T(1,128)S(1)}, u32[]{:S(2)}, u32[]{:S(2)}) async-start(f32[8,1,683]{2,1,0:T(1,128)} %all_to_all.73), calls=%async_computation.6 | async-start | bytes 49152 | tf_op jit(solution)/shard_map/all_to_all | solution.py:39
  181.1 11.2 %all-to-all-start.7 = ((f32[8,1,683]{2,1,0:T(1,128)}), f32[8,1,683]{2,1,0:T(1,128)S(1)}, u32[]{:S(2)}, u32[]{:S(2)}) async-start(f32[8,1,683]{2,1,0:T(1,128)} %copy.222), calls=%async_computation.7 | async-start | bytes 49152 | tf_op jit(solution)/shard_map/all_to_all | solution.py:40
  193.8 17.8 %all-to-all-start.8 = ((f32[12,1,5462]{2,1,0:T(1,128)}), f32[12,1,5462]{2,1,0:T(1,128)S(1)}, u32[]{:S(2)}, u32[]{:S(2)}) async-start(f32[12,1,5462]{2,1,0:T(1,128)} %copy.223), calls=%async_computation.8 | async-start | bytes 528384 | tf_op jit(solution)/shard_map/all_to_all | solution.py:42
  (14 other events, 80.9 us)

commit v3 on v2

--- a/solution.py
+++ b/solution.py
@@ -35,10 +35,15 @@
     gathered = lax.all_to_all(pieces, inner, 0, 0, tiled=True)
     within = exclusive_sum(gathered, reverse)
     group_total = jnp.sum(gathered, axis=0)
-    parts = padded_pieces(group_total, lax.axis_size(outer))
-    gathered_totals = lax.all_to_all(parts, outer, 0, 0, tiled=True)
-    across = lax.all_to_all(exclusive_sum(gathered_totals, reverse), outer, 0, 0, tiled=True)
-    across = across.reshape(-1)[: group_total.shape[0]]
+    groups = lax.axis_size(outer)
+    copies = jnp.broadcast_to(group_total[None], (groups,) + group_total.shape)
+    gathered_totals = lax.all_to_all(copies, outer, 0, 0, tiled=True)
+    index = jnp.arange(groups, dtype=jnp.int32)
+    mine = lax.axis_index(outer)
+    chosen = (index > mine) if reverse else (index < mine)
+    across = jnp.einsum(
+        "j,jf->f", chosen.astype(jnp.float32), gathered_totals, precision=PRECISE
+    )
     returned = lax.all_to_all(within + across[None, :], inner, 0, 0, tiled=True)
     return returned.reshape(-1)[: flat.shape[0]].reshape(state.shape)
 
@@ -198,8 +203,8 @@
 
     later_totals, later_dots = [], []
     stat_pair = jnp.stack([log_total, row_dot])
-    for _ in range(span):
-        stat_pair = passed_along(stat_pair, CTX, -1)
+    for distance in range(1, span + 1):
+        stat_pair = passed_along(jnp.stack([log_total, row_dot]), CTX, -distance)
         later_totals.append(stat_pair[0])
         later_dots.append(stat_pair[1])
     query_ext = jnp.concatenate([win_query] + later_queries, axis=0)

time: 217 us -> 192 us (0.88)
  waiting for transfers between devices: 69.4 us -> 52.4 us
  starting transfers between devices: 97.8 us -> 91.1 us
    all_to_all x4 -> x2, waiting for transfers between devices: 24.4 us -> 11.2 us  [scan_states(): gathered_totals = lax.all_to_all(copies, outer, 0, 0, tiled=True)]
    ppermute x12, waiting for transfers between devices: 21.8 us -> 17.8 us  [passed_along(): return lax.ppermute(block, axis, route)]
    all_to_all x4 -> x2, starting transfers between devices: 31.1 us -> 27.4 us  [scan_states(): gathered_totals = lax.all_to_all(copies, outer, 0, 0, tiled=True)]
    all_to_all x2, starting transfers between devices: 28.3 us -> 25.3 us  [scan_states(): gathered = lax.all_to_all(pieces, inner, 0, 0, tiled=True)]
    all_to_all x4 -> x0, local copies, waits for them, and re-layouts: 2.7 us -> none  [the longest x2 1.42 us: scan_states(): gathered_totals = lax.all_to_all(parts, outer, 0, 0, tiled=True)]
    unnamed x74 -> x76, local copies, waits for them, and re-layouts: 16.5 us -> 17.4 us
  transfers between devices with their start and end apart: 21 -> 19, of which waited for: 13 -> 10; matrix products, arithmetic and copies ran while one was open for 13% -> 15% of each run, Pallas kernels for 0% -> 0%
where the time goes in v3:
time: 192 us; the launch traced here: 190 us
  starting transfers between devices  91.1 us (47%)
  waiting for transfers between devices  52.4 us (27%)
  local copies, waits for them, and re-layouts  28.2 us (15%)
  matrix products  13.6 us (7%)
  other arithmetic  3.21 us (2%)
    all_to_all x2, starting transfers between devices, scan_states(): gathered_totals = lax.all_to_all(copies, outer, 0, 0, tiled=True)  27.4 us
    ppermute x12, starting transfers between devices, passed_along(): return lax.ppermute(block, axis, route)  26.5 us
    all_to_all x2, starting transfers between devices, scan_states(): gathered = lax.all_to_all(pieces, inner, 0, 0, tiled=True)  25.3 us
    ppermute x12, waiting for transfers between devices, passed_along(): return lax.ppermute(block, axis, route)  17.8 us
    unnamed x76, local copies, waits for them, and re-layouts  17.4 us
    all_to_all x2, waiting for transfers between devices, scan_states(): returned = lax.all_to_all(within + across[None, :], inner, 0, 0, tiled=True)  12.9 us
    all_to_all x2, waiting for transfers between devices, scan_states(): gathered_totals = lax.all_to_all(copies, outer, 0, 0, tiled=True)  11.2 us
    all_to_all x2, waiting for transfers between devices, scan_states(): gathered = lax.all_to_all(pieces, inner, 0, 0, tiled=True)  9.13 us
  transfers between devices with their start and end apart: 19, of which 10 were waited for; matrix products, arithmetic and copies ran while one was open for 15% of the time, Pallas kernels for 0%

profile of v3, /device:TPU:6, one launch (start us, length us, event | category | flops | bytes accessed | tf_op | source)
XLA Modules:
  0.0 190.0 jit_solution(9115087412654403471)
XLA Ops:
  3.2 4.4 %collective-permute-start = (bf16[2,128,4,128]{3,1,2,0:T(8,128)(2,1)S(1)}, bf16[2,128,4,128]{3,1,2,0:T(8,128)(2,1)S(1)}, u32[]{:S(2)}, u32[]{:S(2)}) collective-permute-start(bf16[2,128,4,128]{3,1,2,0:T(8,128)(2,1)S(1)} %pad_maximum_fusion), channel_id=1, source_target_pairs={{0,8},{8,16},{16,24},{24,32},{32,40},{40,48},{48,56},{56,64},{64,7... | collective-permute-start | bytes 786440 | tf_op jit(solution)/shard_map/ppermute | solution.py:60
  9.0 14.2 %all-to-all-start = ((f32[12,1,5462]{2,1,0:T(1,128)}), f32[12,1,5462]{2,1,0:T(1,128)S(1)}, u32[]{:S(2)}, u32[]{:S(2)}) async-start(f32[12,1,5462]{2,1,0:T(1,128)} %all_to_all.43), calls=%async_computation | async-start | bytes 528384 | tf_op jit(solution)/shard_map/all_to_all | solution.py:35
  23.6 1.3 collective-permute-start.4
  26.9 4.6 %collective-permute-start.1 = (bf16[2,128,4,128]{3,1,2,0:T(8,128)(2,1)S(1)}, bf16[2,128,4,128]{3,1,2,0:T(8,128)(2,1)S(1)}, u32[]{:S(2)}, u32[]{:S(2)}) collective-permute-start(bf16[2,128,4,128]{3,1,2,0:T(8,128)(2,1)S(1)} %collective-permute-done), channel_id=1, source_target_pairs={{0,8},{8,16},{16,24},{24,32},{32,40},{40,48},{48,56},{56,64},{64,7... | collective-permute-start | bytes 786440 | tf_op jit(solution)/shard_map/ppermute | solution.py:60
  31.4 8.1 %collective-permute-done.4 = bf16[2,128,4,128]{1,3,2,0:T(8,128)(2,1)} collective-permute-done((bf16[2,128,4,128]{1,3,2,0:T(8,128)(2,1)S(1)}, bf16[2,128,4,128]{1,3,2,0:T(8,128)(2,1)}, u32[]{:S(2)}, u32[]{:S(2)}) %collective-permute-start.4) | collective-permute-done | bytes 262176 | tf_op jit(solution)/shard_map/ppermute | solution.py:60
  41.8 5.3 %collective-permute-start.2 = (bf16[2,128,4,128]{3,1,2,0:T(8,128)(2,1)S(1)}, bf16[2,128,4,128]{3,1,2,0:T(8,128)(2,1)}, u32[]{:S(2)}, u32[]{:S(2)}) collective-permute-start(bf16[2,128,4,128]{3,1,2,0:T(8,128)(2,1)S(1)} %collective-permute-done.1), channel_id=1, source_target_pairs={{0,8},{8,16},{16,24},{24,32},{32,40},{40,48},{48,56},{56,64},{64,7... | collective-permute-start | bytes 786440 | tf_op jit(solution)/shard_map/ppermute | solution.py:60
  47.0 1.8 collective-permute-done.5
  50.1 1.7 fusion.54
  52.8 15.1 %all-to-all-start.1 = ((f32[8,1,5462]{2,1,0:T(1,128)}), f32[8,1,5462]{2,1,0:T(1,128)S(1)}, u32[]{:S(2)}, u32[]{:S(2)}) async-start(f32[8,1,5462]{2,1,0:T(1,128)} %broadcast_in_dim.42), calls=%async_computation.1 | async-start | bytes 352256 | tf_op jit(solution)/shard_map/all_to_all | solution.py:40
  67.9 1.7 fusion.53
  69.6 2.0 %collective-permute-start.3 = (bf16[2,128,4,128]{3,1,2,0:T(8,128)(2,1)}, bf16[2,128,4,128]{3,1,2,0:T(8,128)(2,1)}, u32[]{:S(2)}, u32[]{:S(2)}) collective-permute-start(bf16[2,128,4,128]{3,1,2,0:T(8,128)(2,1)} %collective-permute-done.2), channel_id=1, source_target_pairs={{0,8},{8,16},{16,24},{24,32},{32,40},{40,48},{48,56},{56,64},{64,7... | collective-permute-start | bytes 786440 | tf_op jit(solution)/shard_map/ppermute | solution.py:60
  72.8 1.7 fusion.52
  74.5 3.1 %all-to-all-done.1 = f32[8,1,5462]{2,1,0:T(1,128)S(1)} async-done(((f32[8,1,5462]{2,1,0:T(1,128)}), f32[8,1,5462]{2,1,0:T(1,128)S(1)}, u32[]{:S(2)}, u32[]{:S(2)}) %all-to-all-start.1) | async-done | bytes 174816 | tf_op jit(solution)/shard_map/all_to_all | solution.py:40
  79.1 3.5 %all-to-all-start.2 = ((f32[12,1,5462]{2,1,0:T(1,128)}), f32[12,1,5462]{2,1,0:T(1,128)S(1)}, u32[]{:S(2)}, u32[]{:S(2)}) async-start(f32[12,1,5462]{2,1,0:T(1,128)} %copy.193), calls=%async_computation.2 | async-start | bytes 528384 | tf_op jit(solution)/shard_map/all_to_all | solution.py:47
  87.6 1.3 collective-permute-start.9
  88.9 1.3 collective-permute-start.10
  90.2 1.3 collective-permute-start.11
  92.1 1.7 fusion.51
  95.1 2.8 %collective-permute-done.10 = f32[2,4,128]{2,1,0:T(4,128)S(1)} collective-permute-done((f32[2,4,128]{2,1,0:T(4,128)S(1)}, f32[2,4,128]{2,1,0:T(4,128)S(1)}, u32[]{:S(2)}, u32[]{:S(2)}) %collective-permute-start.10) | collective-permute-done | bytes 4128 | tf_op jit(solution)/shard_map/ppermute | solution.py:60
  98.0 4.5 %collective-permute-done.11 = f32[2,4,128]{2,1,0:T(4,128)S(1)} collective-permute-done((f32[2,4,128]{2,1,0:T(4,128)S(1)}, f32[2,4,128]{2,1,0:T(4,128)S(1)}, u32[]{:S(2)}, u32[]{:S(2)}) %collective-permute-start.11) | collective-permute-done | bytes 4128 | tf_op jit(solution)/shard_map/ppermute | solution.py:60
  106.3 4.8 %all-to-all-start.3 = ((f32[8,2,128]{2,1,0:T(2,128)}), f32[8,2,128]{2,1,0:T(2,128)S(1)}, u32[]{:S(2)}, u32[]{:S(2)}) async-start(f32[8,2,128]{2,1,0:T(2,128)} %broadcast_in_dim.43), calls=%async_computation.3 | async-start | bytes 16384 | tf_op jit(solution)/shard_map/all_to_all | solution.py:54
  111.0 1.8 fusion.6
  112.8 1.5 all-to-all-done.3
  117.5 11.1 %all-to-all-start.4 = ((f32[12,1,5462]{2,1,0:T(1,128)}), f32[12,1,5462]{2,1,0:T(1,128)S(1)}, u32[]{:S(2)}, u32[]{:S(2)}) async-start(f32[12,1,5462]{2,1,0:T(1,128)} %all_to_all.51), calls=%async_computation.4 | async-start | bytes 528384 | tf_op jit(solution)/shard_map/all_to_all | solution.py:35
  128.6 2.1 %fusion.19 = bf16[4,128,128]{2,1,0:T(8,128)(2,1)S(1)} fusion(bf16[640,4,128]{0,2,1:T(8,128)(2,1)} %get-tuple-element.47, f32[4,640,128]{2,1,0:T(8,128)S(1)} %fusion.6, bf16[640,4,128]{0,2,1:T(8,128)(2,1)} %copy-done.1, bf16[128,4,128]{0,2,1:T(8,128)(2,1)S(1)} %bitcast.290, f32[4,640]{1,0:T(4,128)S(1)} %copy-done.24), kind=kOutput, calls=%fused_computation.42 | convolution fusion | flops 169148416 | bytes 2893824 | tf_op jit(solution)/shard_map/hts,thd->shd/dot_general | solution.py:140
  131.4 1.4 convolution_convert_fusion
  133.6 1.7 fusion.18
  135.3 9.1 %all-to-all-done.4 = f32[12,1,5462]{2,1,0:T(1,128)S(1)} async-done(((f32[12,1,5462]{2,1,0:T(1,128)}), f32[12,1,5462]{2,1,0:T(1,128)S(1)}, u32[]{:S(2)}, u32[]{:S(2)}) %all-to-all-start.4) | async-done | bytes 262208 | tf_op jit(solution)/shard_map/all_to_all | solution.py:35
  145.4 12.3 %all-to-all-start.5 = ((f32[8,1,5462]{2,1,0:T(1,128)}), f32[8,1,5462]{2,1,0:T(1,128)S(1)}, u32[]{:S(2)}, u32[]{:S(2)}) async-start(f32[8,1,5462]{2,1,0:T(1,128)} %broadcast_in_dim.50), calls=%async_computation.5 | async-start | bytes 352256 | tf_op jit(solution)/shard_map/all_to_all | solution.py:40
  159.1 8.1 %all-to-all-done.5 = f32[8,1,5462]{2,1,0:T(1,128)S(1)} async-done(((f32[8,1,5462]{2,1,0:T(1,128)}), f32[8,1,5462]{2,1,0:T(1,128)S(1)}, u32[]{:S(2)}, u32[]{:S(2)}) %all-to-all-start.5) | async-done | bytes 174816 | tf_op jit(solution)/shard_map/all_to_all | solution.py:40
  168.8 3.5 %all-to-all-start.6 = ((f32[12,1,5462]{2,1,0:T(1,128)}), f32[12,1,5462]{2,1,0:T(1,128)S(1)}, u32[]{:S(2)}, u32[]{:S(2)}) async-start(f32[12,1,5462]{2,1,0:T(1,128)} %copy.217), calls=%async_computation.6 | async-start | bytes 528384 | tf_op jit(solution)/shard_map/all_to_all | solution.py:47
  174.0 12.9 %all-to-all-done.6 = f32[12,1,5462]{2,1,0:T(1,128)S(1)} async-done(((f32[12,1,5462]{2,1,0:T(1,128)}), f32[12,1,5462]{2,1,0:T(1,128)S(1)}, u32[]{:S(2)}, u32[]{:S(2)}) %all-to-all-start.6) | async-done | bytes 262208 | tf_op jit(solution)/shard_map/all_to_all | solution.py:47
  (151 shorter events, 37.0 us)
Async XLA Ops:
  0.6 25.0 %copy-start = (bf16[128,512]{1,0:T(8,128)(2,1)S(1)}, bf16[128,512]{1,0:T(8,128)(2,1)}, u32[]{:S(2)}) copy-start(bf16[128,512]{1,0:T(8,128)(2,1)} %param.7) | copy-start | bytes 393220
  1.8 39.3 %copy-start.8 = (bf16[128,512]{0,1:T(8,128)(2,1)}, bf16[128,512]{0,1:T(8,128)(2,1)S(1)}, u32[]{:S(2)}) copy-start(bf16[128,512]{0,1:T(8,128)(2,1)S(1)} %copy.199) | copy-start | bytes 393220
  2.9 49.8 %copy-start.14 = (bf16[128,512]{0,1:T(8,128)(2,1)}, bf16[128,512]{0,1:T(8,128)(2,1)S(1)}, u32[]{:S(2)}) copy-start(bf16[128,512]{0,1:T(8,128)(2,1)S(1)} %copy.198) | copy-start | bytes 393220
  3.1 20.1 %copy-start.19 = (bf16[128,512]{1,0:T(8,128)(2,1)S(1)}, bf16[128,512]{1,0:T(8,128)(2,1)}, u32[]{:S(2)}) copy-start(bf16[128,512]{1,0:T(8,128)(2,1)} %param.10) | copy-start | bytes 393220
  3.1 20.3 %copy-start.20 = (bf16[128,512]{1,0:T(8,128)(2,1)S(1)}, bf16[128,512]{1,0:T(8,128)(2,1)}, u32[]{:S(2)}) copy-start(bf16[128,512]{1,0:T(8,128)(2,1)} %param.13) | copy-start | bytes 393220
  3.2 23.7 %collective-permute-start = (bf16[2,128,4,128]{3,1,2,0:T(8,128)(2,1)S(1)}, bf16[2,128,4,128]{3,1,2,0:T(8,128)(2,1)S(1)}, u32[]{:S(2)}, u32[]{:S(2)}) collective-permute-start(bf16[2,128,4,128]{3,1,2,0:T(8,128)(2,1)S(1)} %pad_maximum_fusion), channel_id=1, source_target_pairs={{0,8},{8,16},{16,24},{24,32},{32,40},{40,48},{48,56},{56,64},{64,7... | collective-permute-start | bytes 786440 | tf_op jit(solution)/shard_map/ppermute | solution.py:60
  7.7 15.8 %copy-start.12 = (bf16[128,512]{0,1:T(8,128)(2,1)}, bf16[128,512]{0,1:T(8,128)(2,1)S(1)}, u32[]{:S(2)}) copy-start(bf16[128,512]{0,1:T(8,128)(2,1)S(1)} %copy.317) | copy-start | bytes 393220
  9.0 42.8 %all-to-all-start = ((f32[12,1,5462]{2,1,0:T(1,128)}), f32[12,1,5462]{2,1,0:T(1,128)S(1)}, u32[]{:S(2)}, u32[]{:S(2)}) async-start(f32[12,1,5462]{2,1,0:T(1,128)} %all_to_all.43), calls=%async_computation | async-start | bytes 528384 | tf_op jit(solution)/shard_map/all_to_all | solution.py:35
  23.6 15.9 %collective-permute-start.4 = (bf16[2,128,4,128]{1,3,2,0:T(8,128)(2,1)S(1)}, bf16[2,128,4,128]{1,3,2,0:T(8,128)(2,1)}, u32[]{:S(2)}, u32[]{:S(2)}) collective-permute-start(bf16[2,128,4,128]{1,3,2,0:T(8,128)(2,1)S(1)} %pad_maximum_fusion.1), channel_id=1, source_target_pairs={{8,0},{16,8},{24,16},{32,24},{40,32},{48,40},{56,48},{64,56},{72,6... | collective-permute-start | bytes 786440 | tf_op jit(solution)/shard_map/ppermute | solution.py:60
  25.9 26.9 %copy-start.6 = (f32[4,128,128]{2,1,0:T(8,128)}, f32[4,128,128]{2,1,0:T(8,128)S(1)}, u32[]{:S(2)}) copy-start(f32[4,128,128]{2,1,0:T(8,128)S(1)} %convolution_select_fusion.1) | copy-start | bytes 786436
  26.9 14.9 %collective-permute-start.1 = (bf16[2,128,4,128]{3,1,2,0:T(8,128)(2,1)S(1)}, bf16[2,128,4,128]{3,1,2,0:T(8,128)(2,1)S(1)}, u32[]{:S(2)}, u32[]{:S(2)}) collective-permute-start(bf16[2,128,4,128]{3,1,2,0:T(8,128)(2,1)S(1)} %collective-permute-done), channel_id=1, source_target_pairs={{0,8},{8,16},{16,24},{24,32},{32,40},{40,48},{48,56},{56,64},{64,7... | collective-permute-start | bytes 786440 | tf_op jit(solution)/shard_map/ppermute | solution.py:60
  39.5 9.3 %collective-permute-start.5 = (bf16[2,128,4,128]{1,3,2,0:T(8,128)(2,1)}, bf16[2,128,4,128]{1,3,2,0:T(8,128)(2,1)}, u32[]{:S(2)}, u32[]{:S(2)}) collective-permute-start(bf16[2,128,4,128]{1,3,2,0:T(8,128)(2,1)} %collective-permute-done.4), channel_id=1, source_target_pairs={{8,0},{16,8},{24,16},{32,24},{40,32},{48,40},{56,48},{64,56},{72,6... | collective-permute-start | bytes 786440 | tf_op jit(solution)/shard_map/ppermute | solution.py:60
  41.8 36.1 %copy-start.17 = (bf16[2,128,4,128]{3,1,2,0:T(8,128)(2,1)}, bf16[2,128,4,128]{3,1,2,0:T(8,128)(2,1)S(1)}, u32[]{:S(2)}) copy-start(bf16[2,128,4,128]{3,1,2,0:T(8,128)(2,1)S(1)} %collective-permute-done.1) | copy-start | bytes 786436
  41.8 27.8 %collective-permute-start.2 = (bf16[2,128,4,128]{3,1,2,0:T(8,128)(2,1)S(1)}, bf16[2,128,4,128]{3,1,2,0:T(8,128)(2,1)}, u32[]{:S(2)}, u32[]{:S(2)}) collective-permute-start(bf16[2,128,4,128]{3,1,2,0:T(8,128)(2,1)S(1)} %collective-permute-done.1), channel_id=1, source_target_pairs={{0,8},{8,16},{16,24},{24,32},{32,40},{40,48},{48,56},{56,64},{64,7... | collective-permute-start | bytes 786440 | tf_op jit(solution)/shard_map/ppermute | solution.py:60
  48.9 22.7 %collective-permute-start.6 = (bf16[2,128,4,128]{1,3,2,0:T(8,128)(2,1)}, bf16[2,128,4,128]{1,3,2,0:T(8,128)(2,1)}, u32[]{:S(2)}, u32[]{:S(2)}) collective-permute-start(bf16[2,128,4,128]{1,3,2,0:T(8,128)(2,1)} %collective-permute-done.5), channel_id=1, source_target_pairs={{8,0},{16,8},{24,16},{32,24},{40,32},{48,40},{56,48},{64,56},{72,6... | collective-permute-start | bytes 786440 | tf_op jit(solution)/shard_map/ppermute | solution.py:60
  52.8 24.8 %all-to-all-start.1 = ((f32[8,1,5462]{2,1,0:T(1,128)}), f32[8,1,5462]{2,1,0:T(1,128)S(1)}, u32[]{:S(2)}, u32[]{:S(2)}) async-start(f32[8,1,5462]{2,1,0:T(1,128)} %broadcast_in_dim.42), calls=%async_computation.1 | async-start | bytes 352256 | tf_op jit(solution)/shard_map/all_to_all | solution.py:40
  69.6 13.1 %collective-permute-start.3 = (bf16[2,128,4,128]{3,1,2,0:T(8,128)(2,1)}, bf16[2,128,4,128]{3,1,2,0:T(8,128)(2,1)}, u32[]{:S(2)}, u32[]{:S(2)}) collective-permute-start(bf16[2,128,4,128]{3,1,2,0:T(8,128)(2,1)} %collective-permute-done.2), channel_id=1, source_target_pairs={{0,8},{8,16},{16,24},{24,32},{32,40},{40,48},{48,56},{56,64},{64,7... | collective-permute-start | bytes 786440 | tf_op jit(solution)/shard_map/ppermute | solution.py:60
  71.6 20.5 %collective-permute-start.7 = (bf16[2,128,4,128]{1,3,2,0:T(8,128)(2,1)}, bf16[2,128,4,128]{1,3,2,0:T(8,128)(2,1)}, u32[]{:S(2)}, u32[]{:S(2)}) collective-permute-start(bf16[2,128,4,128]{1,3,2,0:T(8,128)(2,1)} %collective-permute-done.6), channel_id=1, source_target_pairs={{8,0},{16,8},{24,16},{32,24},{40,32},{48,40},{56,48},{64,56},{72,6... | collective-permute-start | bytes 786440 | tf_op jit(solution)/shard_map/ppermute | solution.py:60
  79.1 24.6 %all-to-all-start.2 = ((f32[12,1,5462]{2,1,0:T(1,128)}), f32[12,1,5462]{2,1,0:T(1,128)S(1)}, u32[]{:S(2)}, u32[]{:S(2)}) async-start(f32[12,1,5462]{2,1,0:T(1,128)} %copy.193), calls=%async_computation.2 | async-start | bytes 528384 | tf_op jit(solution)/shard_map/all_to_all | solution.py:47
  86.3 8.4 %collective-permute-start.8 = (f32[2,4,128]{2,1,0:T(4,128)S(1)}, f32[2,4,128]{2,1,0:T(4,128)S(1)}, u32[]{:S(2)}, u32[]{:S(2)}) collective-permute-start(f32[2,4,128]{2,1,0:T(4,128)S(1)} %pad_maximum_fusion.2), channel_id=1, source_target_pairs={{8,0},{16,8},{24,16},{32,24},{40,32},{48,40},{56,48},{64,56},{72,6... | collective-permute-start | bytes 12296 | tf_op jit(solution)/shard_map/ppermute | solution.py:60
  87.6 7.6 %collective-permute-start.9 = (f32[2,4,128]{2,1,0:T(4,128)S(1)}, f32[2,4,128]{2,1,0:T(4,128)S(1)}, u32[]{:S(2)}, u32[]{:S(2)}) collective-permute-start(f32[2,4,128]{2,1,0:T(4,128)S(1)} %pad_maximum_fusion.2), channel_id=1, source_target_pairs={{16,0},{24,8},{32,16},{40,24},{48,32},{56,40},{64,48},{72,56},{80,... | collective-permute-start | bytes 12296 | tf_op jit(solution)/shard_map/ppermute | solution.py:60
  88.9 9.1 %collective-permute-start.10 = (f32[2,4,128]{2,1,0:T(4,128)S(1)}, f32[2,4,128]{2,1,0:T(4,128)S(1)}, u32[]{:S(2)}, u32[]{:S(2)}) collective-permute-start(f32[2,4,128]{2,1,0:T(4,128)S(1)} %pad_maximum_fusion.2), channel_id=1, source_target_pairs={{24,0},{32,8},{40,16},{48,24},{56,32},{64,40},{72,48},{80,56},{88,... | collective-permute-start | bytes 12296 | tf_op jit(solution)/shard_map/ppermute | solution.py:60
  90.2 12.4 %collective-permute-start.11 = (f32[2,4,128]{2,1,0:T(4,128)S(1)}, f32[2,4,128]{2,1,0:T(4,128)S(1)}, u32[]{:S(2)}, u32[]{:S(2)}) collective-permute-start(f32[2,4,128]{2,1,0:T(4,128)S(1)} %pad_maximum_fusion.2), channel_id=1, source_target_pairs={{32,0},{40,8},{48,16},{56,24},{64,32},{72,40},{80,48},{88,56},{96,... | collective-permute-start | bytes 12296 | tf_op jit(solution)/shard_map/ppermute | solution.py:60
  106.3 8.0 %all-to-all-start.3 = ((f32[8,2,128]{2,1,0:T(2,128)}), f32[8,2,128]{2,1,0:T(2,128)S(1)}, u32[]{:S(2)}, u32[]{:S(2)}) async-start(f32[8,2,128]{2,1,0:T(2,128)} %broadcast_in_dim.43), calls=%async_computation.3 | async-start | bytes 16384 | tf_op jit(solution)/shard_map/all_to_all | solution.py:54
  114.4 14.2 %copy-start.9 = (bf16[128,512]{0,1:T(8,128)(2,1)S(1)}, bf16[128,512]{0,1:T(8,128)(2,1)}, u32[]{:S(2)}) copy-start(bf16[128,512]{0,1:T(8,128)(2,1)} %copy-done.8) | copy-start | bytes 393220
  114.4 14.2 %copy-start.24 = (f32[4,640]{1,0:T(4,128)S(1)}, f32[4,640]{1,0:T(4,128)}, u32[]{:S(2)}) copy-start(f32[4,640]{1,0:T(4,128)} %copy-done.23) | copy-start | bytes 30724
  117.5 27.0 %all-to-all-start.4 = ((f32[12,1,5462]{2,1,0:T(1,128)}), f32[12,1,5462]{2,1,0:T(1,128)S(1)}, u32[]{:S(2)}, u32[]{:S(2)}) async-start(f32[12,1,5462]{2,1,0:T(1,128)} %all_to_all.51), calls=%async_computation.4 | async-start | bytes 528384 | tf_op jit(solution)/shard_map/all_to_all | solution.py:35
  133.6 24.1 %copy-start.11 = (bf16[128,512]{1,0:T(8,128)(2,1)S(1)}, bf16[128,512]{1,0:T(8,128)(2,1)}, u32[]{:S(2)}) copy-start(bf16[128,512]{1,0:T(8,128)(2,1)} %param.9) | copy-start | bytes 393220
  135.3 23.4 %copy-start.13 = (bf16[128,512]{0,1:T(8,128)(2,1)S(1)}, bf16[128,512]{0,1:T(8,128)(2,1)}, u32[]{:S(2)}) copy-start(bf16[128,512]{0,1:T(8,128)(2,1)} %copy-done.12) | copy-start | bytes 393220
  145.4 21.9 %all-to-all-start.5 = ((f32[8,1,5462]{2,1,0:T(1,128)}), f32[8,1,5462]{2,1,0:T(1,128)S(1)}, u32[]{:S(2)}, u32[]{:S(2)}) async-start(f32[8,1,5462]{2,1,0:T(1,128)} %broadcast_in_dim.50), calls=%async_computation.5 | async-start | bytes 352256 | tf_op jit(solution)/shard_map/all_to_all | solution.py:40
  168.8 18.1 %all-to-all-start.6 = ((f32[12,1,5462]{2,1,0:T(1,128)}), f32[12,1,5462]{2,1,0:T(1,128)S(1)}, u32[]{:S(2)}, u32[]{:S(2)}) async-start(f32[12,1,5462]{2,1,0:T(1,128)} %copy.217), calls=%async_computation.6 | async-start | bytes 528384 | tf_op jit(solution)/shard_map/all_to_all | solution.py:47
  174.0 14.9 %copy-start.16 = (bf16[128,512]{1,0:T(8,128)(2,1)S(1)}, bf16[128,512]{1,0:T(8,128)(2,1)}, u32[]{:S(2)}) copy-start(bf16[128,512]{1,0:T(8,128)(2,1)} %param.8) | copy-start | bytes 393220
  (13 other events, 72.8 us)

commit v4 on v3

--- a/solution.py
+++ b/solution.py
@@ -29,10 +29,12 @@
     return jnp.pad(vector, (0, per * count - vector.shape[0])).reshape(count, per)
 
 
-def scan_states(state, outer, inner, reverse):
+def scan_states(state, outer, inner, reverse, tied=None):
     flat = state.reshape(-1)
     pieces = padded_pieces(flat, lax.axis_size(inner))
     gathered = lax.all_to_all(pieces, inner, 0, 0, tiled=True)
+    if tied is not None:
+        gathered, tied = lax.optimization_barrier((gathered, tied))
     within = exclusive_sum(gathered, reverse)
     group_total = jnp.sum(gathered, axis=0)
     groups = lax.axis_size(outer)
@@ -45,7 +47,8 @@
         "j,jf->f", chosen.astype(jnp.float32), gathered_totals, precision=PRECISE
     )
     returned = lax.all_to_all(within + across[None, :], inner, 0, 0, tiled=True)
-    return returned.reshape(-1)[: flat.shape[0]].reshape(state.shape)
+    result = returned.reshape(-1)[: flat.shape[0]].reshape(state.shape)
+    return result if tied is None else (result, tied)
 
 
 def head_sum(values, axis):
@@ -160,11 +163,11 @@
 
     earlier_keys, earlier_values = [], []
     later_queries, later_upstreams = [], []
-    key_pair = jnp.stack([win_key, win_value])
-    row_pair = jnp.stack([win_query, cotangent])
-    for _ in range(span):
-        key_pair = passed_along(key_pair, CTX, 1)
-        row_pair = passed_along(row_pair, CTX, -1)
+    own_keys = jnp.stack([win_key, win_value])
+    own_rows = jnp.stack([win_query, cotangent])
+    for distance in range(1, span + 1):
+        key_pair = passed_along(own_keys, CTX, distance)
+        row_pair = passed_along(own_rows, CTX, -distance)
         earlier_keys.insert(0, key_pair[0])
         earlier_values.insert(0, key_pair[1])
         later_queries.append(row_pair[0])
@@ -190,21 +193,22 @@
     query_state = jnp.einsum(
         "thd,the->hde", lin_query, lin_dout, preferred_element_type=jnp.float32
     )
-    suffix = scan_states(query_state, CTX[0], CTX[1], True)
-    grad_q, grad_k, grad_v = linear_backward(
-        lin_query, lin_key, lin_value, lin_dout, lin_scores, prefix, suffix
-    )
-
     key_ext = jnp.concatenate(earlier_keys + [win_key], axis=0)
     value_ext = jnp.concatenate(earlier_values + [win_value], axis=0)
     win_out, win_dq, log_total, row_dot = query_head(
         win_query, key_ext, value_ext, cotangent, first_pos
     )
 
+    suffix, own_stats = scan_states(
+        query_state, CTX[0], CTX[1], True, tied=jnp.stack([log_total, row_dot])
+    )
+    grad_q, grad_k, grad_v = linear_backward(
+        lin_query, lin_key, lin_value, lin_dout, lin_scores, prefix, suffix
+    )
+
     later_totals, later_dots = [], []
-    stat_pair = jnp.stack([log_total, row_dot])
     for distance in range(1, span + 1):
-        stat_pair = passed_along(jnp.stack([log_total, row_dot]), CTX, -distance)
+        stat_pair = passed_along(own_stats, CTX, -distance)
         later_totals.append(stat_pair[0])
         later_dots.append(stat_pair[1])
     query_ext = jnp.concatenate([win_query] + later_queries, axis=0)

time: 192 us -> 225 us (1.17)
  waiting for transfers between devices: 52.4 us -> 85 us
  starting transfers between devices: 91.1 us -> 81.7 us
  matrix products: 13.6 us -> 19.2 us
  other arithmetic: 3.21 us -> 8.16 us
    all_to_all x2, starting transfers between devices: 25.3 us -> 7.72 us  [scan_states(): gathered = lax.all_to_all(pieces, inner, 0, 0, tiled=True)]
    all_to_all x2, waiting for transfers between devices: 9.13 us -> 25.3 us  [scan_states(): gathered = lax.all_to_all(pieces, inner, 0, 0, tiled=True)]
    ppermute x12, starting transfers between devices: 26.5 us -> 36.6 us  [passed_along(): return lax.ppermute(block, axis, route)]
    ppermute x12, waiting for transfers between devices: 17.8 us -> 26.3 us  [passed_along(): return lax.ppermute(block, axis, route)]
    all_to_all x2, starting transfers between devices: 27.4 us -> 22.5 us  [scan_states(): gathered_totals = lax.all_to_all(copies, outer, 0, 0, tiled=True)]
    all_to_all x2, waiting for transfers between devices: 11.2 us -> 16.1 us  [scan_states(): gathered_totals = lax.all_to_all(copies, outer, 0, 0, tiled=True)]
    all_to_all x2, starting transfers between devices: 7.09 us -> 10 us  [scan_states(): returned = lax.all_to_all(within + across[None, :], inner, 0, 0, tiled=True)]
    all_to_all x2, waiting for transfers between devices: 12.9 us -> 15.4 us  [scan_states(): returned = lax.all_to_all(within + across[None, :], inner, 0, 0, tiled=True)]
  transfers between devices with their start and end apart: 19 -> 19, of which waited for: 10 -> 10; matrix products, arithmetic and copies ran while one was open for 15% -> 18% of each run, Pallas kernels for 0% -> 0%
where the time goes in v4:
time: 225 us; the launch traced here: 222 us
  waiting for transfers between devices  85 us (38%)
  starting transfers between devices  81.7 us (36%)
  local copies, waits for them, and re-layouts  26.7 us (12%)
  matrix products  19.2 us (9%)
  other arithmetic  8.16 us (4%)
    ppermute x12, starting transfers between devices, passed_along(): return lax.ppermute(block, axis, route)  36.6 us
    ppermute x12, waiting for transfers between devices, passed_along(): return lax.ppermute(block, axis, route)  26.3 us
    all_to_all x2, waiting for transfers between devices, scan_states(): gathered = lax.all_to_all(pieces, inner, 0, 0, tiled=True)  25.3 us
    all_to_all x2, starting transfers between devices, scan_states(): gathered_totals = lax.all_to_all(copies, outer, 0, 0, tiled=True)  22.5 us
    unnamed x86, local copies, waits for them, and re-layouts  16.7 us
    all_to_all x2, waiting for transfers between devices, scan_states(): gathered_totals = lax.all_to_all(copies, outer, 0, 0, tiled=True)  16.1 us
    all_to_all x2, waiting for transfers between devices, scan_states(): returned = lax.all_to_all(within + across[None, :], inner, 0, 0, tiled=True)  15.4 us
    all_to_all x2, starting transfers between devices, scan_states(): returned = lax.all_to_all(within + across[None, :], inner, 0, 0, tiled=True)  10 us
  transfers between devices with their start and end apart: 19, of which 10 were waited for; matrix products, arithmetic and copies ran while one was open for 18% of the time, Pallas kernels for 0%

profile of v4, /device:TPU:6, one launch (start us, length us, event | category | flops | bytes accessed | tf_op | source)
XLA Modules:
  0.0 222.3 jit_solution(2373109464105873463)
XLA Ops:
  3.1 11.1 %collective-permute-start = (bf16[2,128,4,128]{3,1,2,0:T(8,128)(2,1)S(1)}, bf16[2,128,4,128]{3,1,2,0:T(8,128)(2,1)S(1)}, u32[]{:S(2)}, u32[]{:S(2)}) collective-permute-start(bf16[2,128,4,128]{3,1,2,0:T(8,128)(2,1)S(1)} %pad_maximum_fusion), channel_id=1, source_target_pairs={{0,32},{8,40},{16,48},{24,56},{32,64},{40,72},{48,80},{56,88},{64,... | collective-permute-start | bytes 786440 | tf_op jit(solution)/shard_map/ppermute | solution.py:63
  14.2 7.6 %collective-permute-start.1 = (bf16[2,128,4,128]{3,1,2,0:T(8,128)(2,1)S(1)}, bf16[2,128,4,128]{3,1,2,0:T(8,128)(2,1)S(1)}, u32[]{:S(2)}, u32[]{:S(2)}) collective-permute-start(bf16[2,128,4,128]{3,1,2,0:T(8,128)(2,1)S(1)} %pad_maximum_fusion), channel_id=1, source_target_pairs={{0,24},{8,32},{16,40},{24,48},{32,56},{40,64},{48,72},{56,80},{64,... | collective-permute-start | bytes 786440 | tf_op jit(solution)/shard_map/ppermute | solution.py:63
  21.8 4.3 %collective-permute-start.2 = (bf16[2,128,4,128]{3,1,2,0:T(8,128)(2,1)S(1)}, bf16[2,128,4,128]{3,1,2,0:T(8,128)(2,1)S(1)}, u32[]{:S(2)}, u32[]{:S(2)}) collective-permute-start(bf16[2,128,4,128]{3,1,2,0:T(8,128)(2,1)S(1)} %pad_maximum_fusion), channel_id=1, source_target_pairs={{0,16},{8,24},{16,32},{24,40},{32,48},{40,56},{48,64},{56,72},{64,... | collective-permute-start | bytes 786440 | tf_op jit(solution)/shard_map/ppermute | solution.py:63
  26.1 3.4 %collective-permute-start.3 = (bf16[2,128,4,128]{3,1,2,0:T(8,128)(2,1)S(1)}, bf16[2,128,4,128]{3,1,2,0:T(8,128)(2,1)S(1)}, u32[]{:S(2)}, u32[]{:S(2)}) collective-permute-start(bf16[2,128,4,128]{3,1,2,0:T(8,128)(2,1)S(1)} %pad_maximum_fusion), channel_id=1, source_target_pairs={{0,8},{8,16},{16,24},{24,32},{32,40},{40,48},{48,56},{56,64},{64,7... | collective-permute-start | bytes 786440 | tf_op jit(solution)/shard_map/ppermute | solution.py:63
  31.0 4.2 %all-to-all-start = ((f32[12,1,5462]{2,1,0:T(1,128)}), f32[12,1,5462]{2,1,0:T(1,128)}, u32[]{:S(2)}, u32[]{:S(2)}) async-start(f32[12,1,5462]{2,1,0:T(1,128)} %all_to_all.43), calls=%async_computation | async-start | bytes 528384 | tf_op jit(solution)/shard_map/all_to_all | solution.py:35
  44.2 12.0 %collective-permute-done.1 = bf16[2,128,4,128]{3,1,2,0:T(8,128)(2,1)S(1)} collective-permute-done((bf16[2,128,4,128]{3,1,2,0:T(8,128)(2,1)S(1)}, bf16[2,128,4,128]{3,1,2,0:T(8,128)(2,1)S(1)}, u32[]{:S(2)}, u32[]{:S(2)}) %collective-permute-start.1) | collective-permute-done | bytes 262176 | tf_op jit(solution)/shard_map/ppermute | solution.py:63
  57.5 4.7 %collective-permute-done.2 = bf16[2,128,4,128]{3,1,2,0:T(8,128)(2,1)S(1)} collective-permute-done((bf16[2,128,4,128]{3,1,2,0:T(8,128)(2,1)S(1)}, bf16[2,128,4,128]{3,1,2,0:T(8,128)(2,1)S(1)}, u32[]{:S(2)}, u32[]{:S(2)}) %collective-permute-start.2) | collective-permute-done | bytes 262176 | tf_op jit(solution)/shard_map/ppermute | solution.py:63
  63.5 9.7 %collective-permute-done.3 = bf16[2,128,4,128]{3,1,2,0:T(8,128)(2,1)S(1)} collective-permute-done((bf16[2,128,4,128]{3,1,2,0:T(8,128)(2,1)S(1)}, bf16[2,128,4,128]{3,1,2,0:T(8,128)(2,1)S(1)}, u32[]{:S(2)}, u32[]{:S(2)}) %collective-permute-start.3) | collective-permute-done | bytes 262176 | tf_op jit(solution)/shard_map/ppermute | solution.py:63
  75.3 1.7 fusion.52
  77.0 11.5 %all-to-all-done = f32[12,1,5462]{2,1,0:T(1,128)} async-done(((f32[12,1,5462]{2,1,0:T(1,128)}), f32[12,1,5462]{2,1,0:T(1,128)}, u32[]{:S(2)}, u32[]{:S(2)}) %all-to-all-start) | async-done | bytes 262208 | tf_op jit(solution)/shard_map/all_to_all | solution.py:35
  88.5 1.7 reduce_sum.63
  90.2 1.5 broadcast_in_dim.46
  91.7 7.1 %all-to-all-start.1 = ((f32[8,1,5462]{2,1,0:T(1,128)}), f32[8,1,5462]{2,1,0:T(1,128)}, u32[]{:S(2)}, u32[]{:S(2)}) async-start(f32[8,1,5462]{2,1,0:T(1,128)} %broadcast_in_dim.46), calls=%async_computation.1 | async-start | bytes 352256 | tf_op jit(solution)/shard_map/all_to_all | solution.py:42
  98.8 1.7 fusion.51
  101.8 6.7 %all-to-all-done.1 = f32[8,1,5462]{2,1,0:T(1,128)} async-done(((f32[8,1,5462]{2,1,0:T(1,128)}), f32[8,1,5462]{2,1,0:T(1,128)}, u32[]{:S(2)}, u32[]{:S(2)}) %all-to-all-start.1) | async-done | bytes 174816 | tf_op jit(solution)/shard_map/all_to_all | solution.py:42
  111.9 4.2 %all-to-all-start.2 = ((f32[12,1,5462]{2,1,0:T(1,128)}), f32[12,1,5462]{2,1,0:T(1,128)}, u32[]{:S(2)}, u32[]{:S(2)}) async-start(f32[12,1,5462]{2,1,0:T(1,128)} %copy.193), calls=%async_computation.2 | async-start | bytes 528384 | tf_op jit(solution)/shard_map/all_to_all | solution.py:49
  116.1 1.7 fusion.50
  117.9 1.7 fusion.49
  119.6 1.9 convolution_convert_fusion.1
  121.5 8.7 %all-to-all-done.2 = f32[12,1,5462]{2,1,0:T(1,128)} async-done(((f32[12,1,5462]{2,1,0:T(1,128)}), f32[12,1,5462]{2,1,0:T(1,128)}, u32[]{:S(2)}, u32[]{:S(2)}) %all-to-all-start.2) | async-done | bytes 262208 | tf_op jit(solution)/shard_map/all_to_all | solution.py:49
  130.2 1.6 reduce.2
  133.1 4.8 %all-to-all-start.3 = ((f32[8,2,128]{2,1,0:T(2,128)}), f32[8,2,128]{2,1,0:T(2,128)S(1)}, u32[]{:S(2)}, u32[]{:S(2)}) async-start(f32[8,2,128]{2,1,0:T(2,128)} %broadcast_in_dim.47), calls=%async_computation.3 | async-start | bytes 16384 | tf_op jit(solution)/shard_map/all_to_all | solution.py:57
  139.2 1.9 all-to-all-done.3
  144.5 3.5 %all-to-all-start.4 = ((f32[12,1,5462]{2,1,0:T(1,128)}), f32[12,1,5462]{2,1,0:T(1,128)S(1)}, u32[]{:S(2)}, u32[]{:S(2)}) async-start(f32[12,1,5462]{2,1,0:T(1,128)} %all_to_all.51), calls=%async_computation.4 | async-start | bytes 528384 | tf_op jit(solution)/shard_map/all_to_all | solution.py:35
  149.1 1.9 fusion.15
  151.5 13.8 %all-to-all-done.4 = f32[12,1,5462]{2,1,0:T(1,128)S(1)} async-done(((f32[12,1,5462]{2,1,0:T(1,128)}), f32[12,1,5462]{2,1,0:T(1,128)S(1)}, u32[]{:S(2)}, u32[]{:S(2)}) %all-to-all-start.4) | async-done | bytes 262208 | tf_op jit(solution)/shard_map/all_to_all | solution.py:35
  173.2 15.4 %all-to-all-start.5 = ((f32[8,1,5462]{2,1,0:T(1,128)}), f32[8,1,5462]{2,1,0:T(1,128)S(1)}, u32[]{:S(2)}, u32[]{:S(2)}) async-start(f32[8,1,5462]{2,1,0:T(1,128)} %broadcast_in_dim.50), calls=%async_computation.5 | async-start | bytes 352256 | tf_op jit(solution)/shard_map/all_to_all | solution.py:42
  188.8 9.5 %all-to-all-done.5 = f32[8,1,5462]{2,1,0:T(1,128)S(1)} async-done(((f32[8,1,5462]{2,1,0:T(1,128)}), f32[8,1,5462]{2,1,0:T(1,128)S(1)}, u32[]{:S(2)}, u32[]{:S(2)}) %all-to-all-start.5) | async-done | bytes 174816 | tf_op jit(solution)/shard_map/all_to_all | solution.py:42
  199.7 5.9 %all-to-all-start.6 = ((f32[12,1,5462]{2,1,0:T(1,128)}), f32[12,1,5462]{2,1,0:T(1,128)S(1)}, u32[]{:S(2)}, u32[]{:S(2)}) async-start(f32[12,1,5462]{2,1,0:T(1,128)} %copy.218), calls=%async_computation.6 | async-start | bytes 528384 | tf_op jit(solution)/shard_map/all_to_all | solution.py:49
  205.6 1.7 fusion.6
  207.4 2.1 fusion.19
  212.4 6.7 %all-to-all-done.6 = f32[12,1,5462]{2,1,0:T(1,128)S(1)} async-done(((f32[12,1,5462]{2,1,0:T(1,128)}), f32[12,1,5462]{2,1,0:T(1,128)S(1)}, u32[]{:S(2)}, u32[]{:S(2)}) %all-to-all-start.6) | async-done | bytes 262208 | tf_op jit(solution)/shard_map/all_to_all | solution.py:49
  (161 shorter events, 45.1 us)
Async XLA Ops:
  0.6 37.7 %copy-start = (bf16[128,512]{1,0:T(8,128)(2,1)S(1)}, bf16[128,512]{1,0:T(8,128)(2,1)}, u32[]{:S(2)}) copy-start(bf16[128,512]{1,0:T(8,128)(2,1)} %param.7) | copy-start | bytes 393220
  0.6 28.9 %copy-start.13 = (bf16[128,512]{1,0:T(8,128)(2,1)S(1)}, bf16[128,512]{1,0:T(8,128)(2,1)}, u32[]{:S(2)}) copy-start(bf16[128,512]{1,0:T(8,128)(2,1)} %param.8) | copy-start | bytes 393220
  0.7 29.0 %copy-start.7 = (bf16[128,512]{1,0:T(8,128)(2,1)S(1)}, bf16[128,512]{1,0:T(8,128)(2,1)}, u32[]{:S(2)}) copy-start(bf16[128,512]{1,0:T(8,128)(2,1)} %param.9) | copy-start | bytes 393220
  1.7 39.1 %copy-start.5 = (bf16[128,512]{0,1:T(8,128)(2,1)}, bf16[128,512]{0,1:T(8,128)(2,1)S(1)}, u32[]{:S(2)}) copy-start(bf16[128,512]{0,1:T(8,128)(2,1)S(1)} %copy.199) | copy-start | bytes 393220
  2.9 38.1 %copy-start.9 = (bf16[128,512]{0,1:T(8,128)(2,1)}, bf16[128,512]{0,1:T(8,128)(2,1)S(1)}, u32[]{:S(2)}) copy-start(bf16[128,512]{0,1:T(8,128)(2,1)S(1)} %copy.198) | copy-start | bytes 393220
  3.1 32.1 %copy-start.20 = (bf16[128,512]{1,0:T(8,128)(2,1)S(1)}, bf16[128,512]{1,0:T(8,128)(2,1)}, u32[]{:S(2)}) copy-start(bf16[128,512]{1,0:T(8,128)(2,1)} %param.10) | copy-start | bytes 393220
  3.1 32.2 %copy-start.21 = (bf16[128,512]{1,0:T(8,128)(2,1)S(1)}, bf16[128,512]{1,0:T(8,128)(2,1)}, u32[]{:S(2)}) copy-start(bf16[128,512]{1,0:T(8,128)(2,1)} %param.13) | copy-start | bytes 393220
  3.1 38.0 %collective-permute-start = (bf16[2,128,4,128]{3,1,2,0:T(8,128)(2,1)S(1)}, bf16[2,128,4,128]{3,1,2,0:T(8,128)(2,1)S(1)}, u32[]{:S(2)}, u32[]{:S(2)}) collective-permute-start(bf16[2,128,4,128]{3,1,2,0:T(8,128)(2,1)S(1)} %pad_maximum_fusion), channel_id=1, source_target_pairs={{0,32},{8,40},{16,48},{24,56},{32,64},{40,72},{48,80},{56,88},{64,... | collective-permute-start | bytes 786440 | tf_op jit(solution)/shard_map/ppermute | solution.py:63
  14.2 41.9 %collective-permute-start.1 = (bf16[2,128,4,128]{3,1,2,0:T(8,128)(2,1)S(1)}, bf16[2,128,4,128]{3,1,2,0:T(8,128)(2,1)S(1)}, u32[]{:S(2)}, u32[]{:S(2)}) collective-permute-start(bf16[2,128,4,128]{3,1,2,0:T(8,128)(2,1)S(1)} %pad_maximum_fusion), channel_id=1, source_target_pairs={{0,24},{8,32},{16,40},{24,48},{32,56},{40,64},{48,72},{56,80},{64,... | collective-permute-start | bytes 786440 | tf_op jit(solution)/shard_map/ppermute | solution.py:63
  21.8 40.3 %collective-permute-start.2 = (bf16[2,128,4,128]{3,1,2,0:T(8,128)(2,1)S(1)}, bf16[2,128,4,128]{3,1,2,0:T(8,128)(2,1)S(1)}, u32[]{:S(2)}, u32[]{:S(2)}) collective-permute-start(bf16[2,128,4,128]{3,1,2,0:T(8,128)(2,1)S(1)} %pad_maximum_fusion), channel_id=1, source_target_pairs={{0,16},{8,24},{16,32},{24,40},{32,48},{40,56},{48,64},{56,72},{64,... | collective-permute-start | bytes 786440 | tf_op jit(solution)/shard_map/ppermute | solution.py:63
  26.1 47.0 %collective-permute-start.3 = (bf16[2,128,4,128]{3,1,2,0:T(8,128)(2,1)S(1)}, bf16[2,128,4,128]{3,1,2,0:T(8,128)(2,1)S(1)}, u32[]{:S(2)}, u32[]{:S(2)}) collective-permute-start(bf16[2,128,4,128]{3,1,2,0:T(8,128)(2,1)S(1)} %pad_maximum_fusion), channel_id=1, source_target_pairs={{0,8},{8,16},{16,24},{24,32},{32,40},{40,48},{48,56},{56,64},{64,7... | collective-permute-start | bytes 786440 | tf_op jit(solution)/shard_map/ppermute | solution.py:63
  31.0 57.5 %all-to-all-start = ((f32[12,1,5462]{2,1,0:T(1,128)}), f32[12,1,5462]{2,1,0:T(1,128)}, u32[]{:S(2)}, u32[]{:S(2)}) async-start(f32[12,1,5462]{2,1,0:T(1,128)} %all_to_all.43), calls=%async_computation | async-start | bytes 528384 | tf_op jit(solution)/shard_map/all_to_all | solution.py:35
  36.2 39.1 %collective-permute-start.4 = (bf16[2,128,4,128]{1,3,2,0:T(8,128)(2,1)}, bf16[2,128,4,128]{1,3,2,0:T(8,128)(2,1)}, u32[]{:S(2)}, u32[]{:S(2)}) collective-permute-start(bf16[2,128,4,128]{1,3,2,0:T(8,128)(2,1)} %pad_maximum_fusion.1), channel_id=1, source_target_pairs={{8,0},{16,8},{24,16},{32,24},{40,32},{48,40},{56,48},{64,56},{72,6... | collective-permute-start | bytes 786440 | tf_op jit(solution)/shard_map/ppermute | solution.py:63
  38.5 24.9 %copy-start.3 = (f32[4,128,128]{2,1,0:T(8,128)}, f32[4,128,128]{2,1,0:T(8,128)S(1)}, u32[]{:S(2)}) copy-start(f32[4,128,128]{2,1,0:T(8,128)S(1)} %convolution_select_fusion.1) | copy-start | bytes 786436
  41.9 56.9 %collective-permute-start.5 = (bf16[2,128,4,128]{1,3,2,0:T(8,128)(2,1)}, bf16[2,128,4,128]{1,3,2,0:T(8,128)(2,1)}, u32[]{:S(2)}, u32[]{:S(2)}) collective-permute-start(bf16[2,128,4,128]{1,3,2,0:T(8,128)(2,1)} %pad_maximum_fusion.1), channel_id=1, source_target_pairs={{16,0},{24,8},{32,16},{40,24},{48,32},{56,40},{64,48},{72,56},{80,... | collective-permute-start | bytes 786440 | tf_op jit(solution)/shard_map/ppermute | solution.py:63
  56.1 60.0 %collective-permute-start.6 = (bf16[2,128,4,128]{1,3,2,0:T(8,128)(2,1)}, bf16[2,128,4,128]{1,3,2,0:T(8,128)(2,1)}, u32[]{:S(2)}, u32[]{:S(2)}) collective-permute-start(bf16[2,128,4,128]{1,3,2,0:T(8,128)(2,1)} %pad_maximum_fusion.1), channel_id=1, source_target_pairs={{24,0},{32,8},{40,16},{48,24},{56,32},{64,40},{72,48},{80,56},{88,... | collective-permute-start | bytes 786440 | tf_op jit(solution)/shard_map/ppermute | solution.py:63
  62.1 55.7 %collective-permute-start.7 = (bf16[2,128,4,128]{1,3,2,0:T(8,128)(2,1)}, bf16[2,128,4,128]{1,3,2,0:T(8,128)(2,1)}, u32[]{:S(2)}, u32[]{:S(2)}) collective-permute-start(bf16[2,128,4,128]{1,3,2,0:T(8,128)(2,1)} %pad_maximum_fusion.1), channel_id=1, source_target_pairs={{32,0},{40,8},{48,16},{56,24},{64,32},{72,40},{80,48},{88,56},{96,... | collective-permute-start | bytes 786440 | tf_op jit(solution)/shard_map/ppermute | solution.py:63
  91.7 16.8 %all-to-all-start.1 = ((f32[8,1,5462]{2,1,0:T(1,128)}), f32[8,1,5462]{2,1,0:T(1,128)}, u32[]{:S(2)}, u32[]{:S(2)}) async-start(f32[8,1,5462]{2,1,0:T(1,128)} %broadcast_in_dim.46), calls=%async_computation.1 | async-start | bytes 352256 | tf_op jit(solution)/shard_map/all_to_all | solution.py:42
  111.9 18.3 %all-to-all-start.2 = ((f32[12,1,5462]{2,1,0:T(1,128)}), f32[12,1,5462]{2,1,0:T(1,128)}, u32[]{:S(2)}, u32[]{:S(2)}) async-start(f32[12,1,5462]{2,1,0:T(1,128)} %copy.193), calls=%async_computation.2 | async-start | bytes 528384 | tf_op jit(solution)/shard_map/all_to_all | solution.py:49
  121.5 16.9 %copy-start.18 = (bf16[4,128,128]{2,1,0:T(8,128)(2,1)S(1)}, bf16[4,128,128]{2,1,0:T(8,128)(2,1)}, u32[]{:S(2)}) copy-start(bf16[4,128,128]{2,1,0:T(8,128)(2,1)} %convolution_convert_fusion.1) | copy-start | bytes 393220
  133.1 8.0 %all-to-all-start.3 = ((f32[8,2,128]{2,1,0:T(2,128)}), f32[8,2,128]{2,1,0:T(2,128)S(1)}, u32[]{:S(2)}, u32[]{:S(2)}) async-start(f32[8,2,128]{2,1,0:T(2,128)} %broadcast_in_dim.47), calls=%async_computation.3 | async-start | bytes 16384 | tf_op jit(solution)/shard_map/all_to_all | solution.py:57
  144.5 20.8 %all-to-all-start.4 = ((f32[12,1,5462]{2,1,0:T(1,128)}), f32[12,1,5462]{2,1,0:T(1,128)S(1)}, u32[]{:S(2)}, u32[]{:S(2)}) async-start(f32[12,1,5462]{2,1,0:T(1,128)} %all_to_all.51), calls=%async_computation.4 | async-start | bytes 528384 | tf_op jit(solution)/shard_map/all_to_all | solution.py:35
  151.5 37.2 %copy-start.26 = (f32[4,640]{1,0:T(4,128)S(1)}, f32[4,640]{1,0:T(4,128)}, u32[]{:S(2)}) copy-start(f32[4,640]{1,0:T(4,128)} %constant_dynamic-update-slice_fusion.13) | copy-start | bytes 30724
  151.5 37.2 %copy-start.30 = (f32[4,640]{1,0:T(4,128)S(1)}, f32[4,640]{1,0:T(4,128)}, u32[]{:S(2)}) copy-start(f32[4,640]{1,0:T(4,128)} %get-tuple-element.48) | copy-start | bytes 30724
  165.4 23.3 %collective-permute-start.8 = (f32[2,4,128]{2,1,0:T(4,128)S(1)}, f32[2,4,128]{2,1,0:T(4,128)S(1)}, u32[]{:S(2)}, u32[]{:S(2)}) collective-permute-start(f32[2,4,128]{2,1,0:T(4,128)S(1)} %copy-done.27), channel_id=1, source_target_pairs={{8,0},{16,8},{24,16},{32,24},{40,32},{48,40},{56,48},{64,56},{72,6... | collective-permute-start | bytes 12296 | tf_op jit(solution)/shard_map/ppermute | solution.py:63
  168.5 20.2 %collective-permute-start.9 = (f32[2,4,128]{2,1,0:T(4,128)S(1)}, f32[2,4,128]{2,1,0:T(4,128)S(1)}, u32[]{:S(2)}, u32[]{:S(2)}) collective-permute-start(f32[2,4,128]{2,1,0:T(4,128)S(1)} %copy-done.27), channel_id=1, source_target_pairs={{16,0},{24,8},{32,16},{40,24},{48,32},{56,40},{64,48},{72,56},{80,... | collective-permute-start | bytes 12296 | tf_op jit(solution)/shard_map/ppermute | solution.py:63
  169.8 18.9 %collective-permute-start.10 = (f32[2,4,128]{2,1,0:T(4,128)S(1)}, f32[2,4,128]{2,1,0:T(4,128)S(1)}, u32[]{:S(2)}, u32[]{:S(2)}) collective-permute-start(f32[2,4,128]{2,1,0:T(4,128)S(1)} %copy-done.27), channel_id=1, source_target_pairs={{24,0},{32,8},{40,16},{48,24},{56,32},{64,40},{72,48},{80,56},{88,... | collective-permute-start | bytes 12296 | tf_op jit(solution)/shard_map/ppermute | solution.py:63
  171.1 17.6 %collective-permute-start.11 = (f32[2,4,128]{2,1,0:T(4,128)S(1)}, f32[2,4,128]{2,1,0:T(4,128)S(1)}, u32[]{:S(2)}, u32[]{:S(2)}) collective-permute-start(f32[2,4,128]{2,1,0:T(4,128)S(1)} %copy-done.27), channel_id=1, source_target_pairs={{32,0},{40,8},{48,16},{56,24},{64,32},{72,40},{80,48},{88,56},{96,... | collective-permute-start | bytes 12296 | tf_op jit(solution)/shard_map/ppermute | solution.py:63
  172.4 33.2 %copy-start.10 = (bf16[128,512]{0,1:T(8,128)(2,1)S(1)}, bf16[128,512]{0,1:T(8,128)(2,1)}, u32[]{:S(2)}) copy-start(bf16[128,512]{0,1:T(8,128)(2,1)} %copy-done.9) | copy-start | bytes 393220
  172.5 33.2 %copy-start.22 = (pred[640,128]{1,0:T(8,128)(4,1)S(1)}, pred[640,128]{1,0:T(8,128)(4,1)}, u32[]{:S(2)}) copy-start(pred[640,128]{1,0:T(8,128)(4,1)} %compare_and_fusion) | copy-start | bytes 245764
  173.2 25.0 %all-to-all-start.5 = ((f32[8,1,5462]{2,1,0:T(1,128)}), f32[8,1,5462]{2,1,0:T(1,128)S(1)}, u32[]{:S(2)}, u32[]{:S(2)}) async-start(f32[8,1,5462]{2,1,0:T(1,128)} %broadcast_in_dim.50), calls=%async_computation.5 | async-start | bytes 352256 | tf_op jit(solution)/shard_map/all_to_all | solution.py:42
  199.7 19.4 %all-to-all-start.6 = ((f32[12,1,5462]{2,1,0:T(1,128)}), f32[12,1,5462]{2,1,0:T(1,128)S(1)}, u32[]{:S(2)}, u32[]{:S(2)}) async-start(f32[12,1,5462]{2,1,0:T(1,128)} %copy.218), calls=%async_computation.6 | async-start | bytes 528384 | tf_op jit(solution)/shard_map/all_to_all | solution.py:49
  (18 other events, 143.7 us)

commit v5 on v4

--- a/solution.py
+++ b/solution.py
@@ -163,11 +163,11 @@
 
     earlier_keys, earlier_values = [], []
     later_queries, later_upstreams = [], []
-    own_keys = jnp.stack([win_key, win_value])
-    own_rows = jnp.stack([win_query, cotangent])
-    for distance in range(1, span + 1):
-        key_pair = passed_along(own_keys, CTX, distance)
-        row_pair = passed_along(own_rows, CTX, -distance)
+    key_pair = jnp.stack([win_key, win_value])
+    row_pair = jnp.stack([win_query, cotangent])
+    for _ in range(span):
+        key_pair = passed_along(key_pair, CTX, 1)
+        row_pair = passed_along(row_pair, CTX, -1)
         earlier_keys.insert(0, key_pair[0])
         earlier_values.insert(0, key_pair[1])
         later_queries.append(row_pair[0])

time: 225 us -> 202 us (0.90)
  waiting for transfers between devices: 85 us -> 50 us
  starting transfers between devices: 81.7 us -> 92.1 us
  local copies, waits for them, and re-layouts: 26.7 us -> 30.4 us
  other arithmetic: 8.16 us -> 5.68 us
    ppermute x12, waiting for transfers between devices: 26.3 us -> 8.42 us  [passed_along(): return lax.ppermute(block, axis, route)]
    all_to_all x2, waiting for transfers between devices: 25.3 us -> 12.3 us  [scan_states(): gathered = lax.all_to_all(pieces, inner, 0, 0, tiled=True)]
    all_to_all x2, starting transfers between devices: 7.72 us -> 18.4 us  [scan_states(): gathered = lax.all_to_all(pieces, inner, 0, 0, tiled=True)]
    all_to_all x2, starting transfers between devices: 22.5 us -> 32.3 us  [scan_states(): gathered_totals = lax.all_to_all(copies, outer, 0, 0, tiled=True)]
    ppermute x12, starting transfers between devices: 36.6 us -> 27.2 us  [passed_along(): return lax.ppermute(block, axis, route)]
    unnamed x86 -> x83, local copies, waits for them, and re-layouts: 16.7 us -> 17 us
  transfers between devices with their start and end apart: 19 -> 19, of which waited for: 10 -> 8; matrix products, arithmetic and copies ran while one was open for 18% -> 17% of each run, Pallas kernels for 0% -> 0%
where the time goes in v5:
time: 202 us; the launch traced here: 200 us
  starting transfers between devices  92.1 us (46%)
  waiting for transfers between devices  50 us (25%)
  local copies, waits for them, and re-layouts  30.4 us (15%)
  matrix products  19.8 us (10%)
  other arithmetic  5.68 us (3%)
    all_to_all x2, starting transfers between devices, scan_states(): gathered_totals = lax.all_to_all(copies, outer, 0, 0, tiled=True)  32.3 us
    ppermute x12, starting transfers between devices, passed_along(): return lax.ppermute(block, axis, route)  27.2 us
    all_to_all x2, starting transfers between devices, scan_states(): gathered = lax.all_to_all(pieces, inner, 0, 0, tiled=True)  18.4 us
    unnamed x83, local copies, waits for them, and re-layouts  17 us
    all_to_all x2, waiting for transfers between devices, scan_states(): returned = lax.all_to_all(within + across[None, :], inner, 0, 0, tiled=True)  14.3 us
    all_to_all x2, waiting for transfers between devices, scan_states(): gathered_totals = lax.all_to_all(copies, outer, 0, 0, tiled=True)  13.9 us
    all_to_all x2, waiting for transfers between devices, scan_states(): gathered = lax.all_to_all(pieces, inner, 0, 0, tiled=True)  12.3 us
    all_to_all x2, starting transfers between devices, scan_states(): returned = lax.all_to_all(within + across[None, :], inner, 0, 0, tiled=True)  9.39 us
  transfers between devices with their start and end apart: 19, of which 8 were waited for; matrix products, arithmetic and copies ran while one was open for 17% of the time, Pallas kernels for 0%

profile of v5, /device:TPU:6, one launch (start us, length us, event | category | flops | bytes accessed | tf_op | source)
XLA Modules:
  0.0 199.5 jit_solution(12462257827561935194)
XLA Ops:
  3.8 4.4 %collective-permute-start = (bf16[2,128,4,128]{3,1,2,0:T(8,128)(2,1)}, bf16[2,128,4,128]{3,1,2,0:T(8,128)(2,1)S(1)}, u32[]{:S(2)}, u32[]{:S(2)}) collective-permute-start(bf16[2,128,4,128]{3,1,2,0:T(8,128)(2,1)} %pad_maximum_fusion), channel_id=1, source_target_pairs={{0,8},{8,16},{16,24},{24,32},{32,40},{40,48},{48,56},{56,64},{64,7... | collective-permute-start | bytes 786440 | tf_op jit(solution)/shard_map/ppermute | solution.py:63
  9.7 14.2 %all-to-all-start = ((f32[12,1,5462]{2,1,0:T(1,128)}), f32[12,1,5462]{2,1,0:T(1,128)S(1)}, u32[]{:S(2)}, u32[]{:S(2)}) async-start(f32[12,1,5462]{2,1,0:T(1,128)} %all_to_all.43), calls=%async_computation | async-start | bytes 528384 | tf_op jit(solution)/shard_map/all_to_all | solution.py:35
  27.6 5.3 %collective-permute-start.1 = (bf16[2,128,4,128]{3,1,2,0:T(8,128)(2,1)S(1)}, bf16[2,128,4,128]{3,1,2,0:T(8,128)(2,1)}, u32[]{:S(2)}, u32[]{:S(2)}) collective-permute-start(bf16[2,128,4,128]{3,1,2,0:T(8,128)(2,1)S(1)} %collective-permute-done), channel_id=1, source_target_pairs={{0,8},{8,16},{16,24},{24,32},{32,40},{40,48},{48,56},{56,64},{64,7... | collective-permute-start | bytes 786440 | tf_op jit(solution)/shard_map/ppermute | solution.py:63
  32.9 7.3 %collective-permute-done.4 = bf16[2,128,4,128]{1,3,2,0:T(8,128)(2,1)} collective-permute-done((bf16[2,128,4,128]{1,3,2,0:T(8,128)(2,1)}, bf16[2,128,4,128]{1,3,2,0:T(8,128)(2,1)}, u32[]{:S(2)}, u32[]{:S(2)}) %collective-permute-start.4) | collective-permute-done | bytes 262176 | tf_op jit(solution)/shard_map/ppermute | solution.py:63
  43.1 5.3 %collective-permute-start.2 = (bf16[2,128,4,128]{3,1,2,0:T(8,128)(2,1)}, bf16[2,128,4,128]{3,1,2,0:T(8,128)(2,1)}, u32[]{:S(2)}, u32[]{:S(2)}) collective-permute-start(bf16[2,128,4,128]{3,1,2,0:T(8,128)(2,1)} %collective-permute-done.1), channel_id=1, source_target_pairs={{0,8},{8,16},{16,24},{24,32},{32,40},{40,48},{48,56},{56,64},{64,7... | collective-permute-start | bytes 786440 | tf_op jit(solution)/shard_map/ppermute | solution.py:63
  52.8 15.2 %all-to-all-start.1 = ((f32[8,1,5462]{2,1,0:T(1,128)}), f32[8,1,5462]{2,1,0:T(1,128)S(1)}, u32[]{:S(2)}, u32[]{:S(2)}) async-start(f32[8,1,5462]{2,1,0:T(1,128)} %broadcast_in_dim.46), calls=%async_computation.1 | async-start | bytes 352256 | tf_op jit(solution)/shard_map/all_to_all | solution.py:42
  69.0 2.0 %collective-permute-start.3 = (bf16[2,128,4,128]{3,1,2,0:T(8,128)(2,1)}, bf16[2,128,4,128]{3,1,2,0:T(8,128)(2,1)}, u32[]{:S(2)}, u32[]{:S(2)}) collective-permute-start(bf16[2,128,4,128]{3,1,2,0:T(8,128)(2,1)} %collective-permute-done.2), channel_id=1, source_target_pairs={{0,8},{8,16},{16,24},{24,32},{32,40},{40,48},{48,56},{56,64},{64,7... | collective-permute-start | bytes 786440 | tf_op jit(solution)/shard_map/ppermute | solution.py:63
  71.0 1.3 collective-permute-start.7
  73.3 4.5 %all-to-all-done.1 = f32[8,1,5462]{2,1,0:T(1,128)S(1)} async-done(((f32[8,1,5462]{2,1,0:T(1,128)}), f32[8,1,5462]{2,1,0:T(1,128)S(1)}, u32[]{:S(2)}, u32[]{:S(2)}) %all-to-all-start.1) | async-done | bytes 174816 | tf_op jit(solution)/shard_map/all_to_all | solution.py:42
  79.4 3.5 %all-to-all-start.2 = ((f32[12,1,5462]{2,1,0:T(1,128)}), f32[12,1,5462]{2,1,0:T(1,128)S(1)}, u32[]{:S(2)}, u32[]{:S(2)}) async-start(f32[12,1,5462]{2,1,0:T(1,128)} %copy.193), calls=%async_computation.2 | async-start | bytes 528384 | tf_op jit(solution)/shard_map/all_to_all | solution.py:49
  88.1 1.7 fusion.49
  91.1 6.2 %all-to-all-done.2 = f32[12,1,5462]{2,1,0:T(1,128)S(1)} async-done(((f32[12,1,5462]{2,1,0:T(1,128)}), f32[12,1,5462]{2,1,0:T(1,128)S(1)}, u32[]{:S(2)}, u32[]{:S(2)}) %all-to-all-start.2) | async-done | bytes 262208 | tf_op jit(solution)/shard_map/all_to_all | solution.py:49
  98.1 1.4 multiply_reduce_fusion.1
  100.1 4.8 %all-to-all-start.3 = ((f32[8,2,128]{2,1,0:T(2,128)}), f32[8,2,128]{2,1,0:T(2,128)S(1)}, u32[]{:S(2)}, u32[]{:S(2)}) async-start(f32[8,2,128]{2,1,0:T(2,128)} %broadcast_in_dim.47), calls=%async_computation.3 | async-start | bytes 16384 | tf_op jit(solution)/shard_map/all_to_all | solution.py:57
  105.5 1.7 copy.234
  110.8 2.0 %convolution_bitcast_fusion.4 = f32[128,4,128]{0,2,1:T(8,128)} fusion(f32[4,128,128]{2,1,0:T(8,128)S(1)} %convolution_select_fusion, bf16[128,4,128]{0,2,1:T(8,128)(2,1)} %bitcast.300), kind=kOutput, calls=%fused_computation.27 | convolution fusion | flops 100663296 | bytes 655360 | tf_op jit(solution)/shard_map/hts,shd->thd/dot_general | solution.py:87
  112.8 1.8 copy.216
  114.6 1.7 pad.8
  116.3 2.0 %all_to_all.51 = f32[12,1,5462]{2,1,0:T(1,128)} reshape(f32[65544]{0:T(1024)} %pad.8) | data formatting | bytes 524352 | tf_op jit(solution)/shard_map/all_to_all | solution.py:35
  118.3 4.2 %all-to-all-start.4 = ((f32[12,1,5462]{2,1,0:T(1,128)}), f32[12,1,5462]{2,1,0:T(1,128)}, u32[]{:S(2)}, u32[]{:S(2)}) async-start(f32[12,1,5462]{2,1,0:T(1,128)} %all_to_all.51), calls=%async_computation.4 | async-start | bytes 528384 | tf_op jit(solution)/shard_map/all_to_all | solution.py:35
  122.5 2.0 convolution_bitcast_fusion.2
  124.5 1.9 fusion.15
  127.5 12.3 %all-to-all-done.4 = f32[12,1,5462]{2,1,0:T(1,128)} async-done(((f32[12,1,5462]{2,1,0:T(1,128)}), f32[12,1,5462]{2,1,0:T(1,128)}, u32[]{:S(2)}, u32[]{:S(2)}) %all-to-all-start.4) | async-done | bytes 262208 | tf_op jit(solution)/shard_map/all_to_all | solution.py:35
  140.8 1.3 collective-permute-start.8
  145.3 1.3 collective-permute-start.10
  146.6 1.3 collective-permute-start.11
  148.7 17.1 %all-to-all-start.5 = ((f32[8,1,5462]{2,1,0:T(1,128)}), f32[8,1,5462]{2,1,0:T(1,128)S(1)}, u32[]{:S(2)}, u32[]{:S(2)}) async-start(f32[8,1,5462]{2,1,0:T(1,128)} %broadcast_in_dim.50), calls=%async_computation.5 | async-start | bytes 352256 | tf_op jit(solution)/shard_map/all_to_all | solution.py:42
  165.9 9.5 %all-to-all-done.5 = f32[8,1,5462]{2,1,0:T(1,128)S(1)} async-done(((f32[8,1,5462]{2,1,0:T(1,128)}), f32[8,1,5462]{2,1,0:T(1,128)S(1)}, u32[]{:S(2)}, u32[]{:S(2)}) %all-to-all-start.5) | async-done | bytes 174816 | tf_op jit(solution)/shard_map/all_to_all | solution.py:42
  176.9 5.8 %all-to-all-start.6 = ((f32[12,1,5462]{2,1,0:T(1,128)}), f32[12,1,5462]{2,1,0:T(1,128)S(1)}, u32[]{:S(2)}, u32[]{:S(2)}) async-start(f32[12,1,5462]{2,1,0:T(1,128)} %copy.218), calls=%async_computation.6 | async-start | bytes 528384 | tf_op jit(solution)/shard_map/all_to_all | solution.py:49
  182.8 1.7 fusion.6
  184.5 1.9 fusion.19
  188.3 8.0 %all-to-all-done.6 = f32[12,1,5462]{2,1,0:T(1,128)S(1)} async-done(((f32[12,1,5462]{2,1,0:T(1,128)}), f32[12,1,5462]{2,1,0:T(1,128)S(1)}, u32[]{:S(2)}, u32[]{:S(2)}) %all-to-all-start.6) | async-done | bytes 262208 | tf_op jit(solution)/shard_map/all_to_all | solution.py:49
  (158 shorter events, 43.6 us)
Async XLA Ops:
  0.6 25.7 %copy-start = (bf16[128,512]{1,0:T(8,128)(2,1)S(1)}, bf16[128,512]{1,0:T(8,128)(2,1)}, u32[]{:S(2)}) copy-start(bf16[128,512]{1,0:T(8,128)(2,1)} %param.7) | copy-start | bytes 393220
  1.7 40.0 %copy-start.4 = (bf16[128,512]{0,1:T(8,128)(2,1)}, bf16[128,512]{0,1:T(8,128)(2,1)S(1)}, u32[]{:S(2)}) copy-start(bf16[128,512]{0,1:T(8,128)(2,1)S(1)} %copy.199) | copy-start | bytes 393220
  2.9 38.9 %copy-start.8 = (bf16[128,512]{0,1:T(8,128)(2,1)}, bf16[128,512]{0,1:T(8,128)(2,1)S(1)}, u32[]{:S(2)}) copy-start(bf16[128,512]{0,1:T(8,128)(2,1)S(1)} %copy.198) | copy-start | bytes 393220
  3.8 20.1 %copy-start.19 = (bf16[128,512]{1,0:T(8,128)(2,1)S(1)}, bf16[128,512]{1,0:T(8,128)(2,1)}, u32[]{:S(2)}) copy-start(bf16[128,512]{1,0:T(8,128)(2,1)} %param.10) | copy-start | bytes 393220
  3.8 20.2 %copy-start.20 = (bf16[128,512]{1,0:T(8,128)(2,1)S(1)}, bf16[128,512]{1,0:T(8,128)(2,1)}, u32[]{:S(2)}) copy-start(bf16[128,512]{1,0:T(8,128)(2,1)} %param.13) | copy-start | bytes 393220
  3.8 23.8 %collective-permute-start = (bf16[2,128,4,128]{3,1,2,0:T(8,128)(2,1)}, bf16[2,128,4,128]{3,1,2,0:T(8,128)(2,1)S(1)}, u32[]{:S(2)}, u32[]{:S(2)}) collective-permute-start(bf16[2,128,4,128]{3,1,2,0:T(8,128)(2,1)} %pad_maximum_fusion), channel_id=1, source_target_pairs={{0,8},{8,16},{16,24},{24,32},{32,40},{40,48},{48,56},{56,64},{64,7... | collective-permute-start | bytes 786440 | tf_op jit(solution)/shard_map/ppermute | solution.py:63
  8.4 17.8 %copy-start.10 = (bf16[128,512]{0,1:T(8,128)(2,1)}, bf16[128,512]{0,1:T(8,128)(2,1)S(1)}, u32[]{:S(2)}) copy-start(bf16[128,512]{0,1:T(8,128)(2,1)S(1)} %copy.314) | copy-start | bytes 393220
  9.7 42.2 %all-to-all-start = ((f32[12,1,5462]{2,1,0:T(1,128)}), f32[12,1,5462]{2,1,0:T(1,128)S(1)}, u32[]{:S(2)}, u32[]{:S(2)}) async-start(f32[12,1,5462]{2,1,0:T(1,128)} %all_to_all.43), calls=%async_computation | async-start | bytes 528384 | tf_op jit(solution)/shard_map/all_to_all | solution.py:35
  24.9 15.2 %collective-permute-start.4 = (bf16[2,128,4,128]{1,3,2,0:T(8,128)(2,1)}, bf16[2,128,4,128]{1,3,2,0:T(8,128)(2,1)}, u32[]{:S(2)}, u32[]{:S(2)}) collective-permute-start(bf16[2,128,4,128]{1,3,2,0:T(8,128)(2,1)} %pad_maximum_fusion.1), channel_id=1, source_target_pairs={{8,0},{16,8},{24,16},{32,24},{40,32},{48,40},{56,48},{64,56},{72,6... | collective-permute-start | bytes 786440 | tf_op jit(solution)/shard_map/ppermute | solution.py:63
  26.6 26.2 %copy-start.1 = (f32[4,128,128]{2,1,0:T(8,128)}, f32[4,128,128]{2,1,0:T(8,128)S(1)}, u32[]{:S(2)}) copy-start(f32[4,128,128]{2,1,0:T(8,128)S(1)} %convolution_select_fusion.1) | copy-start | bytes 786436
  27.6 25.2 %copy-start.17 = (bf16[2,128,4,128]{3,1,2,0:T(8,128)(2,1)}, bf16[2,128,4,128]{3,1,2,0:T(8,128)(2,1)S(1)}, u32[]{:S(2)}) copy-start(bf16[2,128,4,128]{3,1,2,0:T(8,128)(2,1)S(1)} %collective-permute-done) | copy-start | bytes 786436
  27.6 15.5 %collective-permute-start.1 = (bf16[2,128,4,128]{3,1,2,0:T(8,128)(2,1)S(1)}, bf16[2,128,4,128]{3,1,2,0:T(8,128)(2,1)}, u32[]{:S(2)}, u32[]{:S(2)}) collective-permute-start(bf16[2,128,4,128]{3,1,2,0:T(8,128)(2,1)S(1)} %collective-permute-done), channel_id=1, source_target_pairs={{0,8},{8,16},{16,24},{24,32},{32,40},{40,48},{48,56},{56,64},{64,7... | collective-permute-start | bytes 786440 | tf_op jit(solution)/shard_map/ppermute | solution.py:63
  40.2 9.3 %collective-permute-start.5 = (bf16[2,128,4,128]{1,3,2,0:T(8,128)(2,1)}, bf16[2,128,4,128]{1,3,2,0:T(8,128)(2,1)}, u32[]{:S(2)}, u32[]{:S(2)}) collective-permute-start(bf16[2,128,4,128]{1,3,2,0:T(8,128)(2,1)} %collective-permute-done.4), channel_id=1, source_target_pairs={{8,0},{16,8},{24,16},{32,24},{40,32},{48,40},{56,48},{64,56},{72,6... | collective-permute-start | bytes 786440 | tf_op jit(solution)/shard_map/ppermute | solution.py:63
  43.1 25.9 %collective-permute-start.2 = (bf16[2,128,4,128]{3,1,2,0:T(8,128)(2,1)}, bf16[2,128,4,128]{3,1,2,0:T(8,128)(2,1)}, u32[]{:S(2)}, u32[]{:S(2)}) collective-permute-start(bf16[2,128,4,128]{3,1,2,0:T(8,128)(2,1)} %collective-permute-done.1), channel_id=1, source_target_pairs={{0,8},{8,16},{16,24},{24,32},{32,40},{40,48},{48,56},{56,64},{64,7... | collective-permute-start | bytes 786440 | tf_op jit(solution)/shard_map/ppermute | solution.py:63
  49.5 21.5 %collective-permute-start.6 = (bf16[2,128,4,128]{1,3,2,0:T(8,128)(2,1)}, bf16[2,128,4,128]{1,3,2,0:T(8,128)(2,1)}, u32[]{:S(2)}, u32[]{:S(2)}) collective-permute-start(bf16[2,128,4,128]{1,3,2,0:T(8,128)(2,1)} %collective-permute-done.5), channel_id=1, source_target_pairs={{8,0},{16,8},{24,16},{32,24},{40,32},{48,40},{56,48},{64,56},{72,6... | collective-permute-start | bytes 786440 | tf_op jit(solution)/shard_map/ppermute | solution.py:63
  52.8 25.0 %all-to-all-start.1 = ((f32[8,1,5462]{2,1,0:T(1,128)}), f32[8,1,5462]{2,1,0:T(1,128)S(1)}, u32[]{:S(2)}, u32[]{:S(2)}) async-start(f32[8,1,5462]{2,1,0:T(1,128)} %broadcast_in_dim.46), calls=%async_computation.1 | async-start | bytes 352256 | tf_op jit(solution)/shard_map/all_to_all | solution.py:42
  69.0 13.9 %collective-permute-start.3 = (bf16[2,128,4,128]{3,1,2,0:T(8,128)(2,1)}, bf16[2,128,4,128]{3,1,2,0:T(8,128)(2,1)}, u32[]{:S(2)}, u32[]{:S(2)}) collective-permute-start(bf16[2,128,4,128]{3,1,2,0:T(8,128)(2,1)} %collective-permute-done.2), channel_id=1, source_target_pairs={{0,8},{8,16},{16,24},{24,32},{32,40},{40,48},{48,56},{56,64},{64,7... | collective-permute-start | bytes 786440 | tf_op jit(solution)/shard_map/ppermute | solution.py:63
  71.0 17.1 %collective-permute-start.7 = (bf16[2,128,4,128]{1,3,2,0:T(8,128)(2,1)}, bf16[2,128,4,128]{1,3,2,0:T(8,128)(2,1)}, u32[]{:S(2)}, u32[]{:S(2)}) collective-permute-start(bf16[2,128,4,128]{1,3,2,0:T(8,128)(2,1)} %collective-permute-done.6), channel_id=1, source_target_pairs={{8,0},{16,8},{24,16},{32,24},{40,32},{48,40},{56,48},{64,56},{72,6... | collective-permute-start | bytes 786440 | tf_op jit(solution)/shard_map/ppermute | solution.py:63
  79.4 17.9 %all-to-all-start.2 = ((f32[12,1,5462]{2,1,0:T(1,128)}), f32[12,1,5462]{2,1,0:T(1,128)S(1)}, u32[]{:S(2)}, u32[]{:S(2)}) async-start(f32[12,1,5462]{2,1,0:T(1,128)} %copy.193), calls=%async_computation.2 | async-start | bytes 528384 | tf_op jit(solution)/shard_map/all_to_all | solution.py:49
  100.1 8.0 %all-to-all-start.3 = ((f32[8,2,128]{2,1,0:T(2,128)}), f32[8,2,128]{2,1,0:T(2,128)S(1)}, u32[]{:S(2)}, u32[]{:S(2)}) async-start(f32[8,2,128]{2,1,0:T(2,128)} %broadcast_in_dim.47), calls=%async_computation.3 | async-start | bytes 16384 | tf_op jit(solution)/shard_map/all_to_all | solution.py:57
  118.3 21.5 %all-to-all-start.4 = ((f32[12,1,5462]{2,1,0:T(1,128)}), f32[12,1,5462]{2,1,0:T(1,128)}, u32[]{:S(2)}, u32[]{:S(2)}) async-start(f32[12,1,5462]{2,1,0:T(1,128)} %all_to_all.51), calls=%async_computation.4 | async-start | bytes 528384 | tf_op jit(solution)/shard_map/all_to_all | solution.py:35
  126.3 15.8 %copy-start.2 = (f32[4,128,128]{2,1,0:T(8,128)S(1)}, f32[4,128,128]{2,1,0:T(8,128)}, u32[]{:S(2)}) copy-start(f32[4,128,128]{2,1,0:T(8,128)} %copy-done.1) | copy-start | bytes 786436
  127.5 38.3 %copy-start.24 = (f32[4,640]{1,0:T(4,128)S(1)}, f32[4,640]{1,0:T(4,128)}, u32[]{:S(2)}) copy-start(f32[4,640]{1,0:T(4,128)} %constant_dynamic-update-slice_fusion.13) | copy-start | bytes 30724
  127.5 38.3 %copy-start.28 = (f32[4,640]{1,0:T(4,128)S(1)}, f32[4,640]{1,0:T(4,128)}, u32[]{:S(2)}) copy-start(f32[4,640]{1,0:T(4,128)} %get-tuple-element.48) | copy-start | bytes 30724
  140.8 25.0 %collective-permute-start.8 = (f32[2,4,128]{2,1,0:T(4,128)S(1)}, f32[2,4,128]{2,1,0:T(4,128)S(1)}, u32[]{:S(2)}, u32[]{:S(2)}) collective-permute-start(f32[2,4,128]{2,1,0:T(4,128)S(1)} %copy-done.25), channel_id=1, source_target_pairs={{8,0},{16,8},{24,16},{32,24},{40,32},{48,40},{56,48},{64,56},{72,6... | collective-permute-start | bytes 12296 | tf_op jit(solution)/shard_map/ppermute | solution.py:63
  144.0 21.9 %collective-permute-start.9 = (f32[2,4,128]{2,1,0:T(4,128)S(1)}, f32[2,4,128]{2,1,0:T(4,128)S(1)}, u32[]{:S(2)}, u32[]{:S(2)}) collective-permute-start(f32[2,4,128]{2,1,0:T(4,128)S(1)} %copy-done.25), channel_id=1, source_target_pairs={{16,0},{24,8},{32,16},{40,24},{48,32},{56,40},{64,48},{72,56},{80,... | collective-permute-start | bytes 12296 | tf_op jit(solution)/shard_map/ppermute | solution.py:63
  145.3 20.6 %collective-permute-start.10 = (f32[2,4,128]{2,1,0:T(4,128)S(1)}, f32[2,4,128]{2,1,0:T(4,128)S(1)}, u32[]{:S(2)}, u32[]{:S(2)}) collective-permute-start(f32[2,4,128]{2,1,0:T(4,128)S(1)} %copy-done.25), channel_id=1, source_target_pairs={{24,0},{32,8},{40,16},{48,24},{56,32},{64,40},{72,48},{80,56},{88,... | collective-permute-start | bytes 12296 | tf_op jit(solution)/shard_map/ppermute | solution.py:63
  146.6 19.3 %collective-permute-start.11 = (f32[2,4,128]{2,1,0:T(4,128)S(1)}, f32[2,4,128]{2,1,0:T(4,128)S(1)}, u32[]{:S(2)}, u32[]{:S(2)}) collective-permute-start(f32[2,4,128]{2,1,0:T(4,128)S(1)} %copy-done.25), channel_id=1, source_target_pairs={{32,0},{40,8},{48,16},{56,24},{64,32},{72,40},{80,48},{88,56},{96,... | collective-permute-start | bytes 12296 | tf_op jit(solution)/shard_map/ppermute | solution.py:63
  147.9 34.8 %copy-start.9 = (bf16[128,512]{0,1:T(8,128)(2,1)S(1)}, bf16[128,512]{0,1:T(8,128)(2,1)}, u32[]{:S(2)}) copy-start(bf16[128,512]{0,1:T(8,128)(2,1)} %copy-done.8) | copy-start | bytes 393220
  147.9 34.8 %copy-start.21 = (pred[640,128]{1,0:T(8,128)(4,1)S(1)}, pred[640,128]{1,0:T(8,128)(4,1)}, u32[]{:S(2)}) copy-start(pred[640,128]{1,0:T(8,128)(4,1)} %compare_and_fusion) | copy-start | bytes 245764
  148.7 26.7 %all-to-all-start.5 = ((f32[8,1,5462]{2,1,0:T(1,128)}), f32[8,1,5462]{2,1,0:T(1,128)S(1)}, u32[]{:S(2)}, u32[]{:S(2)}) async-start(f32[8,1,5462]{2,1,0:T(1,128)} %broadcast_in_dim.50), calls=%async_computation.5 | async-start | bytes 352256 | tf_op jit(solution)/shard_map/all_to_all | solution.py:42
  176.9 19.4 %all-to-all-start.6 = ((f32[12,1,5462]{2,1,0:T(1,128)}), f32[12,1,5462]{2,1,0:T(1,128)S(1)}, u32[]{:S(2)}, u32[]{:S(2)}) async-start(f32[12,1,5462]{2,1,0:T(1,128)} %copy.218), calls=%async_computation.6 | async-start | bytes 528384 | tf_op jit(solution)/shard_map/all_to_all | solution.py:49
  (16 other events, 136.0 us)

commit v6 on v3

--- a/solution.py
+++ b/solution.py
@@ -1,8 +1,11 @@
 import math
+from functools import partial
 
 import jax
 import jax.numpy as jnp
 from jax import lax
+from jax.experimental import pallas as pl
+from jax.experimental.pallas import tpu as pltpu
 from jax.sharding import PartitionSpec as P
 
 HD = 128
@@ -12,6 +15,7 @@
 
 PRECISE = lax.Precision.HIGHEST
 NORM_EPS = 1e-05
+INTERPRET = False
 
 
 def exclusive_sum(gathered, reverse):
@@ -142,6 +146,62 @@
     return (key_grad, value_grad)
 
 
+def key_side_kernel(pos_ref, query_ref, upstream_ref, totals_ref, dots_ref, keys_ref, values_ref,
+                    key_grad_ref, value_grad_ref, *, window, total_rows, score_scale):
+    first_pos = pos_ref[0]
+    query = query_ref[...]
+    upstream = upstream_ref[...]
+    keys = keys_ref[...]
+    values = values_ref[...]
+    contract_last = (((1,), (1,)), ((), ()))
+    scores = lax.dot_general(keys, query, contract_last, preferred_element_type=jnp.float32) * score_scale
+    row_count, ext_count = scores.shape
+    key_pos = first_pos + lax.broadcasted_iota(jnp.int32, (row_count, ext_count), 0)
+    query_pos = first_pos + lax.broadcasted_iota(jnp.int32, (row_count, ext_count), 1)
+    allowed = (query_pos < total_rows) & (key_pos <= query_pos) & (key_pos > query_pos - window)
+    probs = jnp.where(allowed, jnp.exp(scores - totals_ref[0]), 0.0)
+    weights_low = probs.astype(jnp.bfloat16)
+    dprobs = lax.dot_general(values, upstream, contract_last, preferred_element_type=jnp.float32)
+    dscores = (probs * (dprobs - dots_ref[0]) * score_scale).astype(jnp.bfloat16)
+    key_grad_ref[...] = jnp.dot(dscores, query, preferred_element_type=jnp.float32)
+    value_grad_ref[...] = jnp.dot(weights_low, upstream, preferred_element_type=jnp.float32)
+
+
+def key_side(query, upstream, totals, dots, keys, values, first_pos, total_rows):
+    ext_count = query.shape[0]
+    row_count = keys.shape[0]
+    head_count = keys.shape[1] // HD
+    body = partial(
+        key_side_kernel,
+        window=ext_count - row_count,
+        total_rows=total_rows,
+        score_scale=1.0 / math.sqrt(HD),
+    )
+    ext_spec = pl.BlockSpec((ext_count, HD), lambda h, pos: (0, h))
+    stat_spec = pl.BlockSpec((1, 1, ext_count), lambda h, pos: (h, 0, 0))
+    row_spec = pl.BlockSpec((row_count, HD), lambda h, pos: (0, h))
+    grad = jax.ShapeDtypeStruct(keys.shape, jnp.float32)
+    return pl.pallas_call(
+        body,
+        grid_spec=pltpu.PrefetchScalarGridSpec(
+            num_scalar_prefetch=1,
+            grid=(head_count,),
+            in_specs=[ext_spec, ext_spec, stat_spec, stat_spec, row_spec, row_spec],
+            out_specs=[row_spec, row_spec],
+        ),
+        out_shape=[grad, grad],
+        interpret=INTERPRET,
+    )(
+        jnp.reshape(first_pos, (1,)).astype(jnp.int32),
+        query,
+        upstream,
+        totals.reshape(head_count, 1, ext_count),
+        dots.reshape(head_count, 1, ext_count),
+        keys,
+        values,
+    )
+
+
 CTX = ("cy", "cz")
 
 
@@ -211,8 +271,15 @@
     upstream_ext = jnp.concatenate([cotangent] + later_upstreams, axis=0)
     total_ext = jnp.concatenate([log_total] + later_totals, axis=1)
     dot_ext = jnp.concatenate([row_dot] + later_dots, axis=1)
-    win_dk, win_dv = key_head(
-        query_ext, upstream_ext, total_ext, dot_ext, win_key, win_value, first_pos, total_rows
+    win_dk, win_dv = key_side(
+        query_ext.reshape(-1, head_count * HD),
+        upstream_ext.reshape(-1, head_count * HD),
+        total_ext,
+        dot_ext,
+        win_k,
+        win_v,
+        first_pos,
+        total_rows,
     )
     mixed = (lin_out * inv_rms[:, None, None] + win_out).astype(jnp.bfloat16).reshape(flat)
     return (
@@ -221,8 +288,8 @@
         grad_k.astype(jnp.bfloat16).reshape(flat),
         grad_v.astype(jnp.bfloat16).reshape(flat),
         win_dq.astype(jnp.bfloat16).reshape(flat),
-        win_dk.astype(jnp.bfloat16).reshape(flat),
-        win_dv.astype(jnp.bfloat16).reshape(flat),
+        win_dk.astype(jnp.bfloat16),
+        win_dv.astype(jnp.bfloat16),
     )
 
 

time: 192 us -> 196 us (1.021)
  waiting for transfers between devices: 52.4 us -> 43.4 us
  local copies, waits for them, and re-layouts: 28.2 us -> 33.6 us
  Pallas kernels: 0 us -> 4.38 us
  matrix products: 13.6 us -> 10.2 us
  starting transfers between devices: 91.1 us -> 94.3 us
  other arithmetic: 3.21 us -> 6.3 us
    all_to_all x2, waiting for transfers between devices: 9.13 us -> 1.96 us  [scan_states(): gathered = lax.all_to_all(pieces, inner, 0, 0, tiled=True)]
    ppermute x12, waiting for transfers between devices: 17.8 us -> 12.2 us  [passed_along(): return lax.ppermute(block, axis, route)]
    all_to_all x2, starting transfers between devices: 7.09 us -> 12.4 us  [scan_states(): returned = lax.all_to_all(within + across[None, :], inner, 0, 0, tiled=True)]
    dot_general x3 -> x0, matrix products: 5.24 us -> none  [the longest x1 2.06 us: key_head(): jnp.einsum('hts,thd->shd', dscores, query, preferred_element_type=jnp.flo...]
    pallas_call x0 -> x1, Pallas kernels: none -> 4.38 us  [key_side(): pl.pallas_call(body, grid_spec=pltpu.PrefetchScalarGridSpec(num_scalar_pr...]
    convert_element_type x0 -> x2, other arithmetic: none -> 3.24 us  [the longest x1 1.62 us: shards(): win_dv.astype(jnp.bfloat16)]
    reshape x0 -> x2, local copies, waits for them, and re-layouts: none -> 2.62 us  [the longest x1 1.31 us: key_side(): totals.reshape(head_count, 1, ext_count)]
    all_to_all x2, waiting for transfers between devices: 12.9 us -> 15.4 us  [scan_states(): returned = lax.all_to_all(within + across[None, :], inner, 0, 0, tiled=True)]
  transfers between devices with their start and end apart: 19 -> 19, of which waited for: 10 -> 9; matrix products, arithmetic and copies ran while one was open for 15% -> 20% of each run, Pallas kernels for 0% -> 2%
where the time goes in v6:
time: 196 us; the launch traced here: 194 us
  starting transfers between devices  94.3 us (48%)
  waiting for transfers between devices  43.4 us (22%)
  local copies, waits for them, and re-layouts  33.6 us (17%)
  matrix products  10.2 us (5%)
  other arithmetic  6.3 us (3%)
  Pallas kernels  4.38 us (2%)
    all_to_all x2, starting transfers between devices, scan_states(): gathered_totals = lax.all_to_all(copies, outer, 0, 0, tiled=True)  25.8 us
    ppermute x12, starting transfers between devices, passed_along(): return lax.ppermute(block, axis, route)  25.7 us
    all_to_all x2, starting transfers between devices, scan_states(): gathered = lax.all_to_all(pieces, inner, 0, 0, tiled=True)  25.7 us
    unnamed x50, local copies, waits for them, and re-layouts  15.9 us
    all_to_all x2, waiting for transfers between devices, scan_states(): returned = lax.all_to_all(within + across[None, :], inner, 0, 0, tiled=True)  15.4 us
    all_to_all x2, starting transfers between devices, scan_states(): returned = lax.all_to_all(within + across[None, :], inner, 0, 0, tiled=True)  12.4 us
    ppermute x12, waiting for transfers between devices, passed_along(): return lax.ppermute(block, axis, route)  12.2 us
    all_to_all x2, waiting for transfers between devices, scan_states(): gathered_totals = lax.all_to_all(copies, outer, 0, 0, tiled=True)  12 us
  transfers between devices with their start and end apart: 19, of which 9 were waited for; matrix products, arithmetic and copies ran while one was open for 20% of the time, Pallas kernels for 2%

profile of v6, /device:TPU:6, one launch (start us, length us, event | category | flops | bytes accessed | tf_op | source)
XLA Modules:
  0.0 193.6 jit_solution(10051159803635572206)
XLA Ops:
  3.1 4.4 %collective-permute-start = (bf16[2,128,4,128]{3,1,2,0:T(8,128)(2,1)S(1)}, bf16[2,128,4,128]{3,1,2,0:T(8,128)(2,1)S(1)}, u32[]{:S(2)}, u32[]{:S(2)}) collective-permute-start(bf16[2,128,4,128]{3,1,2,0:T(8,128)(2,1)S(1)} %pad_maximum_fusion), channel_id=1, source_target_pairs={{0,8},{8,16},{16,24},{24,32},{32,40},{40,48},{48,56},{56,64},{64,7... | collective-permute-start | bytes 786440 | tf_op jit(solution)/shard_map/ppermute | solution.py:64
  9.0 14.2 %all-to-all-start = ((f32[12,1,5462]{2,1,0:T(1,128)}), f32[12,1,5462]{2,1,0:T(1,128)S(1)}, u32[]{:S(2)}, u32[]{:S(2)}) async-start(f32[12,1,5462]{2,1,0:T(1,128)} %all_to_all.43), calls=%async_computation | async-start | bytes 528384 | tf_op jit(solution)/shard_map/all_to_all | solution.py:39
  23.5 1.3 collective-permute-start.4
  29.5 9.9 %collective-permute-done.4 = bf16[2,128,4,128]{3,2,1,0:T(4,128)(2,1)S(1)} collective-permute-done((bf16[2,128,4,128]{3,2,1,0:T(4,128)(2,1)S(1)}, bf16[2,128,4,128]{3,2,1,0:T(4,128)(2,1)S(1)}, u32[]{:S(2)}, u32[]{:S(2)}) %collective-permute-start.4) | collective-permute-done | bytes 262176 | tf_op jit(solution)/shard_map/ppermute | solution.py:64
  39.5 1.3 collective-permute-start.5
  42.1 4.6 %collective-permute-start.1 = (bf16[2,128,4,128]{3,1,2,0:T(8,128)(2,1)S(1)}, bf16[2,128,4,128]{3,1,2,0:T(8,128)(2,1)S(1)}, u32[]{:S(2)}, u32[]{:S(2)}) collective-permute-start(bf16[2,128,4,128]{3,1,2,0:T(8,128)(2,1)S(1)} %collective-permute-done), channel_id=1, source_target_pairs={{0,8},{8,16},{16,24},{24,32},{32,40},{40,48},{48,56},{56,64},{64,7... | collective-permute-start | bytes 786440 | tf_op jit(solution)/shard_map/ppermute | solution.py:64
  46.7 1.8 collective-permute-done.5
  48.6 1.3 collective-permute-start.6
  51.0 4.4 %collective-permute-start.2 = (bf16[2,128,4,128]{3,1,2,0:T(8,128)(2,1)S(1)}, bf16[2,128,4,128]{3,1,2,0:T(8,128)(2,1)S(1)}, u32[]{:S(2)}, u32[]{:S(2)}) collective-permute-start(bf16[2,128,4,128]{3,1,2,0:T(8,128)(2,1)S(1)} %collective-permute-done.1), channel_id=1, source_target_pairs={{0,8},{8,16},{16,24},{24,32},{32,40},{40,48},{48,56},{56,64},{64,7... | collective-permute-start | bytes 786440 | tf_op jit(solution)/shard_map/ppermute | solution.py:64
  57.0 12.5 %all-to-all-start.1 = ((f32[8,1,5462]{2,1,0:T(1,128)}), f32[8,1,5462]{2,1,0:T(1,128)S(1)}, u32[]{:S(2)}, u32[]{:S(2)}) async-start(f32[8,1,5462]{2,1,0:T(1,128)} %broadcast_in_dim.34), calls=%async_computation.1 | async-start | bytes 352256 | tf_op jit(solution)/shard_map/all_to_all | solution.py:44
  71.2 2.0 %collective-permute-start.3 = (bf16[2,128,4,128]{3,1,2,0:T(8,128)(2,1)S(1)}, bf16[2,128,4,128]{3,1,2,0:T(8,128)(2,1)}, u32[]{:S(2)}, u32[]{:S(2)}) collective-permute-start(bf16[2,128,4,128]{3,1,2,0:T(8,128)(2,1)S(1)} %collective-permute-done.2), channel_id=1, source_target_pairs={{0,8},{8,16},{16,24},{24,32},{32,40},{40,48},{48,56},{56,64},{64,7... | collective-permute-start | bytes 786440 | tf_op jit(solution)/shard_map/ppermute | solution.py:64
  75.2 4.5 %all-to-all-done.1 = f32[8,1,5462]{2,1,0:T(1,128)S(1)} async-done(((f32[8,1,5462]{2,1,0:T(1,128)}), f32[8,1,5462]{2,1,0:T(1,128)S(1)}, u32[]{:S(2)}, u32[]{:S(2)}) %all-to-all-start.1) | async-done | bytes 174816 | tf_op jit(solution)/shard_map/all_to_all | solution.py:44
  81.2 4.8 %all-to-all-start.2 = ((f32[12,1,5462]{2,1,0:T(1,128)}), f32[12,1,5462]{2,1,0:T(1,128)S(1)}, u32[]{:S(2)}, u32[]{:S(2)}) async-start(f32[12,1,5462]{2,1,0:T(1,128)} %copy.166), calls=%async_computation.2 | async-start | bytes 528384 | tf_op jit(solution)/shard_map/all_to_all | solution.py:51
  88.5 1.3 collective-permute-start.8
  89.8 1.3 collective-permute-start.9
  91.1 1.3 collective-permute-start.10
  96.9 2.9 %all-to-all-done.2 = f32[12,1,5462]{2,1,0:T(1,128)S(1)} async-done(((f32[12,1,5462]{2,1,0:T(1,128)}), f32[12,1,5462]{2,1,0:T(1,128)S(1)}, u32[]{:S(2)}, u32[]{:S(2)}) %all-to-all-start.2) | async-done | bytes 262208 | tf_op jit(solution)/shard_map/all_to_all | solution.py:51
  102.3 1.4 multiply_reduce_fusion.1
  104.3 4.8 %all-to-all-start.3 = ((f32[8,2,128]{2,1,0:T(2,128)}), f32[8,2,128]{2,1,0:T(2,128)S(1)}, u32[]{:S(2)}, u32[]{:S(2)}) async-start(f32[8,2,128]{2,1,0:T(2,128)} %broadcast_in_dim.35), calls=%async_computation.3 | async-start | bytes 16384 | tf_op jit(solution)/shard_map/all_to_all | solution.py:58
  110.4 2.0 %all-to-all-done.3 = f32[8,2,128]{2,1,0:T(2,128)S(1)} async-done(((f32[8,2,128]{2,1,0:T(2,128)}), f32[8,2,128]{2,1,0:T(2,128)S(1)}, u32[]{:S(2)}, u32[]{:S(2)}) %all-to-all-start.3) | async-done | bytes 8224 | tf_op jit(solution)/shard_map/all_to_all | solution.py:58
  116.0 11.4 %all-to-all-start.4 = ((f32[12,1,5462]{2,1,0:T(1,128)}), f32[12,1,5462]{2,1,0:T(1,128)S(1)}, u32[]{:S(2)}, u32[]{:S(2)}) async-start(f32[12,1,5462]{2,1,0:T(1,128)} %all_to_all.51), calls=%async_computation.4 | async-start | bytes 528384 | tf_op jit(solution)/shard_map/all_to_all | solution.py:39
  129.3 1.3 copy.196.totals_ref
  130.6 1.3 reshape.294.dots_ref
  131.9 4.4 %shard_map.126 = (f32[128,512]{1,0:T(8,128)}, f32[128,512]{1,0:T(8,128)}) custom-call(s32[1]{0:T(128)} %bitcast.42.pos_ref, bf16[640,512]{1,0:T(8,128)(2,1)} %get-tuple-element.82.query_ref, bf16[640,512]{1,0:T(8,128)(2,1)} %get-tuple-element.81.upstream_ref, f32[4,1,640]{2,1,0:T(1,128)} %copy.196.totals_ref, f32[4,1,640]{2,1,0:T(1,128)} %reshape.294.dots_ref, ...), custom_call_target="tpu_custom_call" | custom-call | tf_op jit(solution)/shard_map/pallas_call | solution.py:184
  136.3 1.6 convert_element_type.64
  137.9 1.6 convert_element_type.65
  139.5 1.8 fusion.11
  141.3 2.0 %all-to-all-done.4 = f32[12,1,5462]{2,1,0:T(1,128)S(1)} async-done(((f32[12,1,5462]{2,1,0:T(1,128)}), f32[12,1,5462]{2,1,0:T(1,128)S(1)}, u32[]{:S(2)}, u32[]{:S(2)}) %all-to-all-start.4) | async-done | bytes 262208 | tf_op jit(solution)/shard_map/all_to_all | solution.py:39
  144.2 13.3 %all-to-all-start.5 = ((f32[8,1,5462]{2,1,0:T(1,128)}), f32[8,1,5462]{2,1,0:T(1,128)S(1)}, u32[]{:S(2)}, u32[]{:S(2)}) async-start(f32[8,1,5462]{2,1,0:T(1,128)} %broadcast_in_dim.38), calls=%async_computation.5 | async-start | bytes 352256 | tf_op jit(solution)/shard_map/all_to_all | solution.py:44
  159.7 7.4 %all-to-all-done.5 = f32[8,1,5462]{2,1,0:T(1,128)S(1)} async-done(((f32[8,1,5462]{2,1,0:T(1,128)}), f32[8,1,5462]{2,1,0:T(1,128)S(1)}, u32[]{:S(2)}, u32[]{:S(2)}) %all-to-all-start.5) | async-done | bytes 174816 | tf_op jit(solution)/shard_map/all_to_all | solution.py:44
  168.6 7.6 %all-to-all-start.6 = ((f32[12,1,5462]{2,1,0:T(1,128)}), f32[12,1,5462]{2,1,0:T(1,128)S(1)}, u32[]{:S(2)}, u32[]{:S(2)}) async-start(f32[12,1,5462]{2,1,0:T(1,128)} %copy.189), calls=%async_computation.6 | async-start | bytes 528384 | tf_op jit(solution)/shard_map/all_to_all | solution.py:51
  177.9 12.5 %all-to-all-done.6 = f32[12,1,5462]{2,1,0:T(1,128)S(1)} async-done(((f32[12,1,5462]{2,1,0:T(1,128)}), f32[12,1,5462]{2,1,0:T(1,128)S(1)}, u32[]{:S(2)}, u32[]{:S(2)}) %all-to-all-start.6) | async-done | bytes 262208 | tf_op jit(solution)/shard_map/all_to_all | solution.py:51
  (129 shorter events, 44.1 us)
Async XLA Ops:
  0.6 24.9 %copy-start = (bf16[128,512]{1,0:T(8,128)(2,1)S(1)}, bf16[128,512]{1,0:T(8,128)(2,1)}, u32[]{:S(2)}) copy-start(bf16[128,512]{1,0:T(8,128)(2,1)} %param.7) | copy-start | bytes 393220
  0.6 6.9 %copy-start.3 = (bf16[128,512]{1,0:T(8,128)(2,1)S(1)}, bf16[128,512]{1,0:T(8,128)(2,1)}, u32[]{:S(2)}) copy-start(bf16[128,512]{1,0:T(8,128)(2,1)} %param.8) | copy-start | bytes 393220
  0.7 7.0 %copy-start.1 = (bf16[128,512]{1,0:T(8,128)(2,1)S(1)}, bf16[128,512]{1,0:T(8,128)(2,1)}, u32[]{:S(2)}) copy-start(bf16[128,512]{1,0:T(8,128)(2,1)} %param.9) | copy-start | bytes 393220
  3.1 20.1 %copy-start.2 = (bf16[128,512]{1,0:T(8,128)(2,1)S(1)}, bf16[128,512]{1,0:T(8,128)(2,1)}, u32[]{:S(2)}) copy-start(bf16[128,512]{1,0:T(8,128)(2,1)} %param.13) | copy-start | bytes 393220
  3.1 20.2 %copy-start.6 = (bf16[128,512]{1,0:T(8,128)(2,1)S(1)}, bf16[128,512]{1,0:T(8,128)(2,1)}, u32[]{:S(2)}) copy-start(bf16[128,512]{1,0:T(8,128)(2,1)} %param.10) | copy-start | bytes 393220
  3.1 39.0 %collective-permute-start = (bf16[2,128,4,128]{3,1,2,0:T(8,128)(2,1)S(1)}, bf16[2,128,4,128]{3,1,2,0:T(8,128)(2,1)S(1)}, u32[]{:S(2)}, u32[]{:S(2)}) collective-permute-start(bf16[2,128,4,128]{3,1,2,0:T(8,128)(2,1)S(1)} %pad_maximum_fusion), channel_id=1, source_target_pairs={{0,8},{8,16},{16,24},{24,32},{32,40},{40,48},{48,56},{56,64},{64,7... | collective-permute-start | bytes 786440 | tf_op jit(solution)/shard_map/ppermute | solution.py:64
  9.0 47.1 %all-to-all-start = ((f32[12,1,5462]{2,1,0:T(1,128)}), f32[12,1,5462]{2,1,0:T(1,128)S(1)}, u32[]{:S(2)}, u32[]{:S(2)}) async-start(f32[12,1,5462]{2,1,0:T(1,128)} %all_to_all.43), calls=%async_computation | async-start | bytes 528384 | tf_op jit(solution)/shard_map/all_to_all | solution.py:39
  23.5 15.9 %collective-permute-start.4 = (bf16[2,128,4,128]{3,2,1,0:T(4,128)(2,1)S(1)}, bf16[2,128,4,128]{3,2,1,0:T(4,128)(2,1)S(1)}, u32[]{:S(2)}, u32[]{:S(2)}) collective-permute-start(bf16[2,128,4,128]{3,2,1,0:T(4,128)(2,1)S(1)} %pad_maximum_fusion.1), channel_id=1, source_target_pairs={{8,0},{16,8},{24,16},{32,24},{40,32},{48,40},{56,48},{64,56},{72,6... | collective-permute-start | bytes 786440 | tf_op jit(solution)/shard_map/ppermute | solution.py:64
  24.9 14.6 %copy-start.8 = (pred[128,128]{1,0:T(8,128)(4,1)}, pred[128,128]{1,0:T(8,128)(4,1)S(1)}, u32[]{:S(2)}) copy-start(pred[128,128]{1,0:T(8,128)(4,1)S(1)} %iota_compare_fusion) | copy-start | bytes 49156
  39.5 9.0 %collective-permute-start.5 = (bf16[2,128,4,128]{3,2,1,0:T(4,128)(2,1)S(1)}, bf16[2,128,4,128]{3,2,1,0:T(4,128)(2,1)S(1)}, u32[]{:S(2)}, u32[]{:S(2)}) collective-permute-start(bf16[2,128,4,128]{3,2,1,0:T(4,128)(2,1)S(1)} %collective-permute-done.4), channel_id=1, source_target_pairs={{8,0},{16,8},{24,16},{32,24},{40,32},{48,40},{56,48},{64,56},{72,6... | collective-permute-start | bytes 786440 | tf_op jit(solution)/shard_map/ppermute | solution.py:64
  42.1 8.9 %collective-permute-start.1 = (bf16[2,128,4,128]{3,1,2,0:T(8,128)(2,1)S(1)}, bf16[2,128,4,128]{3,1,2,0:T(8,128)(2,1)S(1)}, u32[]{:S(2)}, u32[]{:S(2)}) collective-permute-start(bf16[2,128,4,128]{3,1,2,0:T(8,128)(2,1)S(1)} %collective-permute-done), channel_id=1, source_target_pairs={{0,8},{8,16},{16,24},{24,32},{32,40},{40,48},{48,56},{56,64},{64,7... | collective-permute-start | bytes 786440 | tf_op jit(solution)/shard_map/ppermute | solution.py:64
  48.6 20.9 %collective-permute-start.6 = (bf16[2,128,4,128]{3,2,1,0:T(4,128)(2,1)S(1)}, bf16[2,128,4,128]{3,2,1,0:T(4,128)(2,1)}, u32[]{:S(2)}, u32[]{:S(2)}) collective-permute-start(bf16[2,128,4,128]{3,2,1,0:T(4,128)(2,1)S(1)} %collective-permute-done.5), channel_id=1, source_target_pairs={{8,0},{16,8},{24,16},{32,24},{40,32},{48,40},{56,48},{64,56},{72,6... | collective-permute-start | bytes 786440 | tf_op jit(solution)/shard_map/ppermute | solution.py:64
  51.0 20.2 %collective-permute-start.2 = (bf16[2,128,4,128]{3,1,2,0:T(8,128)(2,1)S(1)}, bf16[2,128,4,128]{3,1,2,0:T(8,128)(2,1)S(1)}, u32[]{:S(2)}, u32[]{:S(2)}) collective-permute-start(bf16[2,128,4,128]{3,1,2,0:T(8,128)(2,1)S(1)} %collective-permute-done.1), channel_id=1, source_target_pairs={{0,8},{8,16},{16,24},{24,32},{32,40},{40,48},{48,56},{56,64},{64,7... | collective-permute-start | bytes 786440 | tf_op jit(solution)/shard_map/ppermute | solution.py:64
  57.0 22.7 %all-to-all-start.1 = ((f32[8,1,5462]{2,1,0:T(1,128)}), f32[8,1,5462]{2,1,0:T(1,128)S(1)}, u32[]{:S(2)}, u32[]{:S(2)}) async-start(f32[8,1,5462]{2,1,0:T(1,128)} %broadcast_in_dim.34), calls=%async_computation.1 | async-start | bytes 352256 | tf_op jit(solution)/shard_map/all_to_all | solution.py:44
  71.2 14.8 %collective-permute-start.3 = (bf16[2,128,4,128]{3,1,2,0:T(8,128)(2,1)S(1)}, bf16[2,128,4,128]{3,1,2,0:T(8,128)(2,1)}, u32[]{:S(2)}, u32[]{:S(2)}) collective-permute-start(bf16[2,128,4,128]{3,1,2,0:T(8,128)(2,1)S(1)} %collective-permute-done.2), channel_id=1, source_target_pairs={{0,8},{8,16},{16,24},{24,32},{32,40},{40,48},{48,56},{56,64},{64,7... | collective-permute-start | bytes 786440 | tf_op jit(solution)/shard_map/ppermute | solution.py:64
  73.9 19.9 %collective-permute-start.7 = (bf16[2,128,4,128]{3,2,1,0:T(4,128)(2,1)}, bf16[2,128,4,128]{3,2,1,0:T(4,128)(2,1)}, u32[]{:S(2)}, u32[]{:S(2)}) collective-permute-start(bf16[2,128,4,128]{3,2,1,0:T(4,128)(2,1)} %collective-permute-done.6), channel_id=1, source_target_pairs={{8,0},{16,8},{24,16},{32,24},{40,32},{48,40},{56,48},{64,56},{72,6... | collective-permute-start | bytes 786440 | tf_op jit(solution)/shard_map/ppermute | solution.py:64
  81.2 18.6 %all-to-all-start.2 = ((f32[12,1,5462]{2,1,0:T(1,128)}), f32[12,1,5462]{2,1,0:T(1,128)S(1)}, u32[]{:S(2)}, u32[]{:S(2)}) async-start(f32[12,1,5462]{2,1,0:T(1,128)} %copy.166), calls=%async_computation.2 | async-start | bytes 528384 | tf_op jit(solution)/shard_map/all_to_all | solution.py:51
  86.0 1.2 copy-start.9
  87.3 0.9 copy-start.7
  88.5 8.4 %collective-permute-start.8 = (f32[2,4,128]{2,1,0:T(4,128)S(1)}, f32[2,4,128]{2,1,0:T(4,128)S(1)}, u32[]{:S(2)}, u32[]{:S(2)}) collective-permute-start(f32[2,4,128]{2,1,0:T(4,128)S(1)} %pad_maximum_fusion.2), channel_id=1, source_target_pairs={{8,0},{16,8},{24,16},{32,24},{40,32},{48,40},{56,48},{64,56},{72,6... | collective-permute-start | bytes 12296 | tf_op jit(solution)/shard_map/ppermute | solution.py:64
  89.8 19.3 %collective-permute-start.9 = (f32[2,4,128]{2,1,0:T(4,128)S(1)}, f32[2,4,128]{2,1,0:T(4,128)}, u32[]{:S(2)}, u32[]{:S(2)}) collective-permute-start(f32[2,4,128]{2,1,0:T(4,128)S(1)} %pad_maximum_fusion.2), channel_id=1, source_target_pairs={{16,0},{24,8},{32,16},{40,24},{48,32},{56,40},{64,48},{72,56},{80,... | collective-permute-start | bytes 12296 | tf_op jit(solution)/shard_map/ppermute | solution.py:64
  91.1 36.3 %collective-permute-start.10 = (f32[2,4,128]{2,1,0:T(4,128)S(1)}, f32[2,4,128]{2,1,0:T(4,128)}, u32[]{:S(2)}, u32[]{:S(2)}) collective-permute-start(f32[2,4,128]{2,1,0:T(4,128)S(1)} %pad_maximum_fusion.2), channel_id=1, source_target_pairs={{24,0},{32,8},{40,16},{48,24},{56,32},{64,40},{72,48},{80,56},{88,... | collective-permute-start | bytes 12296 | tf_op jit(solution)/shard_map/ppermute | solution.py:64
  92.4 36.3 %collective-permute-start.11 = (f32[2,4,128]{2,1,0:T(4,128)S(1)}, f32[2,4,128]{2,1,0:T(4,128)S(1)}, u32[]{:S(2)}, u32[]{:S(2)}) collective-permute-start(f32[2,4,128]{2,1,0:T(4,128)S(1)} %pad_maximum_fusion.2), channel_id=1, source_target_pairs={{32,0},{40,8},{48,16},{56,24},{64,32},{72,40},{80,48},{88,56},{96,... | collective-permute-start | bytes 12296 | tf_op jit(solution)/shard_map/ppermute | solution.py:64
  96.9 5.4 %copy-start.10 = (f32[4,640]{1,0:T(4,128)}, f32[4,640]{1,0:T(4,128)S(1)}, u32[]{:S(2)}) copy-start(f32[4,640]{1,0:T(4,128)S(1)} %get-tuple-element.72) | copy-start | bytes 30724
  96.9 5.4 %copy-start.11 = (f32[4,640]{1,0:T(4,128)}, f32[4,640]{1,0:T(4,128)S(1)}, u32[]{:S(2)}) copy-start(f32[4,640]{1,0:T(4,128)S(1)} %get-tuple-element.73) | copy-start | bytes 30724
  104.3 8.0 %all-to-all-start.3 = ((f32[8,2,128]{2,1,0:T(2,128)}), f32[8,2,128]{2,1,0:T(2,128)S(1)}, u32[]{:S(2)}, u32[]{:S(2)}) async-start(f32[8,2,128]{2,1,0:T(2,128)} %broadcast_in_dim.35), calls=%async_computation.3 | async-start | bytes 16384 | tf_op jit(solution)/shard_map/all_to_all | solution.py:58
  112.4 0.5 copy-start.12
  116.0 27.3 %all-to-all-start.4 = ((f32[12,1,5462]{2,1,0:T(1,128)}), f32[12,1,5462]{2,1,0:T(1,128)S(1)}, u32[]{:S(2)}, u32[]{:S(2)}) async-start(f32[12,1,5462]{2,1,0:T(1,128)} %all_to_all.51), calls=%async_computation.4 | async-start | bytes 528384 | tf_op jit(solution)/shard_map/all_to_all | solution.py:39
  141.3 17.2 %copy-start.5 = (bf16[128,4,128]{0,2,1:T(8,128)(2,1)S(1)}, bf16[128,4,128]{0,2,1:T(8,128)(2,1)}, u32[]{:S(2)}) copy-start(bf16[128,4,128]{0,2,1:T(8,128)(2,1)} %fusion.11) | copy-start | bytes 393220
  144.2 22.9 %all-to-all-start.5 = ((f32[8,1,5462]{2,1,0:T(1,128)}), f32[8,1,5462]{2,1,0:T(1,128)S(1)}, u32[]{:S(2)}, u32[]{:S(2)}) async-start(f32[8,1,5462]{2,1,0:T(1,128)} %broadcast_in_dim.38), calls=%async_computation.5 | async-start | bytes 352256 | tf_op jit(solution)/shard_map/all_to_all | solution.py:44
  168.6 21.8 %all-to-all-start.6 = ((f32[12,1,5462]{2,1,0:T(1,128)}), f32[12,1,5462]{2,1,0:T(1,128)S(1)}, u32[]{:S(2)}, u32[]{:S(2)}) async-start(f32[12,1,5462]{2,1,0:T(1,128)} %copy.189), calls=%async_computation.6 | async-start | bytes 528384 | tf_op jit(solution)/shard_map/all_to_all | solution.py:51
  177.9 14.5 %copy-start.4 = (bf16[128,512]{1,0:T(8,128)(2,1)S(1)}, bf16[128,512]{1,0:T(8,128)(2,1)}, u32[]{:S(2)}) copy-start(bf16[128,512]{1,0:T(8,128)(2,1)} %param.8) | copy-start | bytes 393220

commit v7 on v3

--- a/solution.py
+++ b/solution.py
@@ -48,6 +48,14 @@
     return returned.reshape(-1)[: flat.shape[0]].reshape(state.shape)
 
 
+def scan_flat(state, axis, reverse):
+    flat = state.reshape(-1)
+    pieces = padded_pieces(flat, lax.axis_size(axis[0]) * lax.axis_size(axis[1]))
+    gathered = lax.all_to_all(pieces, axis, 0, 0, tiled=True)
+    returned = lax.all_to_all(exclusive_sum(gathered, reverse), axis, 0, 0, tiled=True)
+    return returned.reshape(-1)[: flat.shape[0]].reshape(state.shape)
+
+
 def head_sum(values, axis):
     count = lax.axis_size(axis)
     copies = jnp.broadcast_to(values[None], (count,) + values.shape)
@@ -190,7 +198,7 @@
     query_state = jnp.einsum(
         "thd,the->hde", lin_query, lin_dout, preferred_element_type=jnp.float32
     )
-    suffix = scan_states(query_state, CTX[0], CTX[1], True)
+    suffix = scan_flat(query_state, CTX, True)
     grad_q, grad_k, grad_v = linear_backward(
         lin_query, lin_key, lin_value, lin_dout, lin_scores, prefix, suffix
     )

time: 192 us -> 203 us (1.057)
  other arithmetic: 3.21 us -> 7.85 us
  matrix products: 13.6 us -> 16.5 us
    all_to_all x0 -> x2, waiting for transfers between devices: none -> 32.4 us  [the longest x1 16.8 us: scan_flat(): lax.all_to_all(exclusive_sum(gathered, reverse), axis, 0, 0, tiled=True)]
    all_to_all x0 -> x2, starting transfers between devices: none -> 26.4 us  [the longest x1 20.1 us: scan_flat(): gathered = lax.all_to_all(pieces, axis, 0, 0, tiled=True)]
    all_to_all x2 -> x1, waiting for transfers between devices: 12.9 us -> 0.01 us  [scan_states(): returned = lax.all_to_all(within + across[None, :], inner, 0, 0, tiled=True)]
    all_to_all x2 -> x1, starting transfers between devices: 27.4 us -> 15.2 us  [scan_states(): gathered_totals = lax.all_to_all(copies, outer, 0, 0, tiled=True)]
    all_to_all x2 -> x1, starting transfers between devices: 25.3 us -> 14.2 us  [scan_states(): gathered = lax.all_to_all(pieces, inner, 0, 0, tiled=True)]
    all_to_all x2 -> x1, waiting for transfers between devices: 9.13 us -> 0.01 us  [scan_states(): gathered = lax.all_to_all(pieces, inner, 0, 0, tiled=True)]
    all_to_all x2 -> x1, waiting for transfers between devices: 11.2 us -> 4.51 us  [scan_states(): gathered_totals = lax.all_to_all(copies, outer, 0, 0, tiled=True)]
    all_to_all x2 -> x1, starting transfers between devices: 7.09 us -> 4.19 us  [scan_states(): returned = lax.all_to_all(within + across[None, :], inner, 0, 0, tiled=True)]
  transfers between devices with their start and end apart: 19 -> 18, of which waited for: 10 -> 8; matrix products, arithmetic and copies ran while one was open for 15% -> 15% of each run, Pallas kernels for 0% -> 0%
where the time goes in v7:
time: 203 us; the launch traced here: 201 us
  starting transfers between devices  91.9 us (45%)
  waiting for transfers between devices  53.6 us (26%)
  local copies, waits for them, and re-layouts  29.7 us (15%)
  matrix products  16.5 us (8%)
  other arithmetic  7.85 us (4%)
    ppermute x12, starting transfers between devices, passed_along(): return lax.ppermute(block, axis, route)  27.2 us
    all_to_all x1, starting transfers between devices, scan_flat(): gathered = lax.all_to_all(pieces, axis, 0, 0, tiled=True)  20.1 us
    unnamed x72, local copies, waits for them, and re-layouts  17.4 us
    all_to_all x1, waiting for transfers between devices, scan_flat(): lax.all_to_all(exclusive_sum(gathered, reverse), axis, 0, 0, tiled=True)  16.8 us
    ppermute x12, waiting for transfers between devices, passed_along(): return lax.ppermute(block, axis, route)  16.7 us
    all_to_all x1, waiting for transfers between devices, scan_flat(): gathered = lax.all_to_all(pieces, axis, 0, 0, tiled=True)  15.6 us
    all_to_all x1, starting transfers between devices, scan_states(): gathered_totals = lax.all_to_all(copies, outer, 0, 0, tiled=True)  15.2 us
    all_to_all x1, starting transfers between devices, scan_states(): gathered = lax.all_to_all(pieces, inner, 0, 0, tiled=True)  14.2 us
  transfers between devices with their start and end apart: 18, of which 8 were waited for; matrix products, arithmetic and copies ran while one was open for 15% of the time, Pallas kernels for 0%

profile of v7, /device:TPU:6, one launch (start us, length us, event | category | flops | bytes accessed | tf_op | source)
XLA Modules:
  0.0 200.9 jit_solution(14242249280071579431)
XLA Ops:
  3.8 4.4 %collective-permute-start = (bf16[2,128,4,128]{3,1,2,0:T(8,128)(2,1)}, bf16[2,128,4,128]{3,1,2,0:T(8,128)(2,1)S(1)}, u32[]{:S(2)}, u32[]{:S(2)}) collective-permute-start(bf16[2,128,4,128]{3,1,2,0:T(8,128)(2,1)} %pad_maximum_fusion), channel_id=1, source_target_pairs={{0,8},{8,16},{16,24},{24,32},{32,40},{40,48},{48,56},{56,64},{64,7... | collective-permute-start | bytes 786440 | tf_op jit(solution)/shard_map/ppermute | solution.py:68
  9.7 14.2 %all-to-all-start = ((f32[12,1,5462]{2,1,0:T(1,128)}), f32[12,1,5462]{2,1,0:T(1,128)S(1)}, u32[]{:S(2)}, u32[]{:S(2)}) async-start(f32[12,1,5462]{2,1,0:T(1,128)} %all_to_all.37), calls=%async_computation | async-start | bytes 528384 | tf_op jit(solution)/shard_map/all_to_all | solution.py:35
  24.9 1.3 collective-permute-start.4
  27.6 5.3 %collective-permute-start.1 = (bf16[2,128,4,128]{3,1,2,0:T(8,128)(2,1)S(1)}, bf16[2,128,4,128]{3,1,2,0:T(8,128)(2,1)}, u32[]{:S(2)}, u32[]{:S(2)}) collective-permute-start(bf16[2,128,4,128]{3,1,2,0:T(8,128)(2,1)S(1)} %collective-permute-done), channel_id=1, source_target_pairs={{0,8},{8,16},{16,24},{24,32},{32,40},{40,48},{48,56},{56,64},{64,7... | collective-permute-start | bytes 786440 | tf_op jit(solution)/shard_map/ppermute | solution.py:68
  32.8 7.3 %collective-permute-done.4 = bf16[2,128,4,128]{1,3,2,0:T(8,128)(2,1)} collective-permute-done((bf16[2,128,4,128]{1,3,2,0:T(8,128)(2,1)}, bf16[2,128,4,128]{1,3,2,0:T(8,128)(2,1)}, u32[]{:S(2)}, u32[]{:S(2)}) %collective-permute-start.4) | collective-permute-done | bytes 262176 | tf_op jit(solution)/shard_map/ppermute | solution.py:68
  40.2 1.3 collective-permute-start.5
  43.2 5.2 %collective-permute-start.2 = (bf16[2,128,4,128]{3,1,2,0:T(8,128)(2,1)}, bf16[2,128,4,128]{3,1,2,0:T(8,128)(2,1)}, u32[]{:S(2)}, u32[]{:S(2)}) collective-permute-start(bf16[2,128,4,128]{3,1,2,0:T(8,128)(2,1)} %collective-permute-done.1), channel_id=1, source_target_pairs={{0,8},{8,16},{16,24},{24,32},{32,40},{40,48},{48,56},{56,64},{64,7... | collective-permute-start | bytes 786440 | tf_op jit(solution)/shard_map/ppermute | solution.py:68
  49.5 1.3 collective-permute-start.6
  52.8 15.2 %all-to-all-start.1 = ((f32[8,1,5462]{2,1,0:T(1,128)}), f32[8,1,5462]{2,1,0:T(1,128)S(1)}, u32[]{:S(2)}, u32[]{:S(2)}) async-start(f32[8,1,5462]{2,1,0:T(1,128)} %broadcast_in_dim.44), calls=%async_computation.1 | async-start | bytes 352256 | tf_op jit(solution)/shard_map/all_to_all | solution.py:40
  69.0 2.0 collective-permute-start.3
  71.0 1.3 collective-permute-start.7
  73.3 4.5 %all-to-all-done.1 = f32[8,1,5462]{2,1,0:T(1,128)S(1)} async-done(((f32[8,1,5462]{2,1,0:T(1,128)}), f32[8,1,5462]{2,1,0:T(1,128)S(1)}, u32[]{:S(2)}, u32[]{:S(2)}) %all-to-all-start.1) | async-done | bytes 174816 | tf_op jit(solution)/shard_map/all_to_all | solution.py:40
  79.4 4.2 %all-to-all-start.2 = ((f32[12,1,5462]{2,1,0:T(1,128)}), f32[12,1,5462]{2,1,0:T(1,128)}, u32[]{:S(2)}, u32[]{:S(2)}) async-start(f32[12,1,5462]{2,1,0:T(1,128)} %copy.193), calls=%async_computation.2 | async-start | bytes 528384 | tf_op jit(solution)/shard_map/all_to_all | solution.py:47
  88.1 1.3 collective-permute-start.8
  89.4 1.3 collective-permute-start.9
  90.7 1.3 collective-permute-start.10
  92.0 1.3 collective-permute-start.11
  96.8 3.0 %collective-permute-done.10 = f32[2,4,128]{2,1,0:T(4,128)S(1)} collective-permute-done((f32[2,4,128]{2,1,0:T(4,128)S(1)}, f32[2,4,128]{2,1,0:T(4,128)S(1)}, u32[]{:S(2)}, u32[]{:S(2)}) %collective-permute-start.10) | collective-permute-done | bytes 4128 | tf_op jit(solution)/shard_map/ppermute | solution.py:68
  99.8 4.4 %collective-permute-done.11 = f32[2,4,128]{2,1,0:T(4,128)S(1)} collective-permute-done((f32[2,4,128]{2,1,0:T(4,128)S(1)}, f32[2,4,128]{2,1,0:T(4,128)S(1)}, u32[]{:S(2)}, u32[]{:S(2)}) %collective-permute-start.11) | collective-permute-done | bytes 4128 | tf_op jit(solution)/shard_map/ppermute | solution.py:68
  104.8 1.8 fusion.5
  106.6 2.3 %reduce.2 = f32[12,5462]{1,0:T(8,128)} reduce(f32[12,1,5462]{2,1,0:T(1,128)} %all-to-all-done.2, f32[]{:T(128)} %constant.50), dimensions={1}, to_apply=%all_to_all.43.reduce_sub_computation | reduce | bytes 524356 | tf_op jit(solution)/shard_map/all_to_all | solution.py:47
  108.9 1.9 reshape.332
  112.5 2.1 %multiply_reduce_fusion.1 = (f32[128]{0:T(128)S(1)}, f32[128]{0:T(128)S(1)}, f32[128,4,128]{0,2,1:T(8,128)}) fusion(bf16[128,512]{0,1:T(8,128)(2,1)S(1)} %copy.196, f32[128,4,128]{0,2,1:T(8,128)} %convolution_bitcast_fusion.7, f32[4,128,128]{2,1,0:T(8,128)S(1)} %bitcast.278, bf16[128,512]{1,0:T(8,128)(2,1)S(1)} %copy-done), kind=kOutput, calls=%fused_computation.64 | convolution fusion | flops 101056256 | bytes 1049600 | tf_op jit(solution)/shard_map/thd,hde->the/dot_general | solution.py:81
  115.1 4.8 %all-to-all-start.3 = ((f32[8,2,128]{2,1,0:T(2,128)}), f32[8,2,128]{2,1,0:T(2,128)}, u32[]{:S(2)}, u32[]{:S(2)}) async-start(f32[8,2,128]{2,1,0:T(2,128)} %broadcast_in_dim.45), calls=%async_computation.3 | async-start | bytes 16384 | tf_op jit(solution)/shard_map/all_to_all | solution.py:62
  119.9 2.6 %fusion.18 = bf16[4,128,128]{2,1,0:T(8,128)(2,1)} fusion(bf16[640,4,128]{0,2,1:T(8,128)(2,1)} %copy-done.17, f32[4,640,128]{2,1,0:T(8,128)S(1)} %fusion.5, bf16[640,4,128]{0,2,1:T(8,128)(2,1)S(1)} %get-tuple-element.46, bf16[128,4,128]{0,2,1:T(8,128)(2,1)} %bitcast.284, f32[4,640]{1,0:T(4,128)} %copy-done.21), kind=kOutput, calls=%fused_computation.41 | convolution fusion | flops 169148416 | bytes 2893824 | tf_op jit(solution)/shard_map/hts,thd->shd/dot_general | solution.py:148
  122.5 1.7 copy.235
  129.6 20.1 %all-to-all-start.4 = ((f32[96,1,683]{2,1,0:T(1,128)}), f32[96,1,683]{2,1,0:T(1,128)}, u32[]{:S(2)}, u32[]{:S(2)}) async-start(f32[96,1,683]{2,1,0:T(1,128)} %all_to_all.45), calls=%async_computation.4 | async-start | bytes 589824 | tf_op jit(solution)/shard_map/all_to_all | solution.py:54
  149.8 1.5 convolution_convert_fusion
  152.3 1.6 fusion.17
  153.9 15.6 %all-to-all-done.4 = f32[96,1,683]{2,1,0:T(1,128)} async-done(((f32[96,1,683]{2,1,0:T(1,128)}), f32[96,1,683]{2,1,0:T(1,128)}, u32[]{:S(2)}, u32[]{:S(2)}) %all-to-all-start.4) | async-done | bytes 262304 | tf_op jit(solution)/shard_map/all_to_all | solution.py:54
  171.7 6.2 %all-to-all-start.5 = ((f32[96,1,683]{2,1,0:T(1,128)}), f32[96,1,683]{2,1,0:T(1,128)S(1)}, u32[]{:S(2)}, u32[]{:S(2)}) async-start(f32[96,1,683]{2,1,0:T(1,128)} %copy.217), calls=%async_computation.5 | async-start | bytes 589824 | tf_op jit(solution)/shard_map/all_to_all | solution.py:55
  180.8 16.8 %all-to-all-done.5 = f32[96,1,683]{2,1,0:T(1,128)S(1)} async-done(((f32[96,1,683]{2,1,0:T(1,128)}), f32[96,1,683]{2,1,0:T(1,128)S(1)}, u32[]{:S(2)}, u32[]{:S(2)}) %all-to-all-start.5) | async-done | bytes 262304 | tf_op jit(solution)/shard_map/all_to_all | solution.py:55
  (142 shorter events, 40.7 us)
Async XLA Ops:
  0.6 25.7 %copy-start = (bf16[128,512]{1,0:T(8,128)(2,1)S(1)}, bf16[128,512]{1,0:T(8,128)(2,1)}, u32[]{:S(2)}) copy-start(bf16[128,512]{1,0:T(8,128)(2,1)} %param.7) | copy-start | bytes 393220
  0.7 7.7 %copy-start.9 = (bf16[128,512]{1,0:T(8,128)(2,1)S(1)}, bf16[128,512]{1,0:T(8,128)(2,1)}, u32[]{:S(2)}) copy-start(bf16[128,512]{1,0:T(8,128)(2,1)} %param.9) | copy-start | bytes 393220
  1.8 40.0 %copy-start.8 = (bf16[128,512]{0,1:T(8,128)(2,1)}, bf16[128,512]{0,1:T(8,128)(2,1)S(1)}, u32[]{:S(2)}) copy-start(bf16[128,512]{0,1:T(8,128)(2,1)S(1)} %copy.199) | copy-start | bytes 393220
  2.9 38.9 %copy-start.14 = (bf16[128,512]{0,1:T(8,128)(2,1)}, bf16[128,512]{0,1:T(8,128)(2,1)S(1)}, u32[]{:S(2)}) copy-start(bf16[128,512]{0,1:T(8,128)(2,1)S(1)} %copy.198) | copy-start | bytes 393220
  3.8 20.1 %copy-start.18 = (bf16[128,512]{1,0:T(8,128)(2,1)S(1)}, bf16[128,512]{1,0:T(8,128)(2,1)}, u32[]{:S(2)}) copy-start(bf16[128,512]{1,0:T(8,128)(2,1)} %param.10) | copy-start | bytes 393220
  3.8 20.3 %copy-start.19 = (bf16[128,512]{1,0:T(8,128)(2,1)S(1)}, bf16[128,512]{1,0:T(8,128)(2,1)}, u32[]{:S(2)}) copy-start(bf16[128,512]{1,0:T(8,128)(2,1)} %param.13) | copy-start | bytes 393220
  3.8 23.8 %collective-permute-start = (bf16[2,128,4,128]{3,1,2,0:T(8,128)(2,1)}, bf16[2,128,4,128]{3,1,2,0:T(8,128)(2,1)S(1)}, u32[]{:S(2)}, u32[]{:S(2)}) collective-permute-start(bf16[2,128,4,128]{3,1,2,0:T(8,128)(2,1)} %pad_maximum_fusion), channel_id=1, source_target_pairs={{0,8},{8,16},{16,24},{24,32},{32,40},{40,48},{48,56},{56,64},{64,7... | collective-permute-start | bytes 786440 | tf_op jit(solution)/shard_map/ppermute | solution.py:68
  8.4 15.6 %copy-start.12 = (bf16[128,512]{0,1:T(8,128)(2,1)}, bf16[128,512]{0,1:T(8,128)(2,1)S(1)}, u32[]{:S(2)}) copy-start(bf16[128,512]{0,1:T(8,128)(2,1)S(1)} %copy.312) | copy-start | bytes 393220
  9.7 42.2 %all-to-all-start = ((f32[12,1,5462]{2,1,0:T(1,128)}), f32[12,1,5462]{2,1,0:T(1,128)S(1)}, u32[]{:S(2)}, u32[]{:S(2)}) async-start(f32[12,1,5462]{2,1,0:T(1,128)} %all_to_all.37), calls=%async_computation | async-start | bytes 528384 | tf_op jit(solution)/shard_map/all_to_all | solution.py:35
  24.9 15.2 %collective-permute-start.4 = (bf16[2,128,4,128]{1,3,2,0:T(8,128)(2,1)}, bf16[2,128,4,128]{1,3,2,0:T(8,128)(2,1)}, u32[]{:S(2)}, u32[]{:S(2)}) collective-permute-start(bf16[2,128,4,128]{1,3,2,0:T(8,128)(2,1)} %pad_maximum_fusion.1), channel_id=1, source_target_pairs={{8,0},{16,8},{24,16},{32,24},{40,32},{48,40},{56,48},{64,56},{72,6... | collective-permute-start | bytes 786440 | tf_op jit(solution)/shard_map/ppermute | solution.py:68
  26.6 26.2 %copy-start.6 = (f32[4,128,128]{2,1,0:T(8,128)}, f32[4,128,128]{2,1,0:T(8,128)S(1)}, u32[]{:S(2)}) copy-start(f32[4,128,128]{2,1,0:T(8,128)S(1)} %convolution_select_fusion.1) | copy-start | bytes 786436
  27.6 15.6 %collective-permute-start.1 = (bf16[2,128,4,128]{3,1,2,0:T(8,128)(2,1)S(1)}, bf16[2,128,4,128]{3,1,2,0:T(8,128)(2,1)}, u32[]{:S(2)}, u32[]{:S(2)}) collective-permute-start(bf16[2,128,4,128]{3,1,2,0:T(8,128)(2,1)S(1)} %collective-permute-done), channel_id=1, source_target_pairs={{0,8},{8,16},{16,24},{24,32},{32,40},{40,48},{48,56},{56,64},{64,7... | collective-permute-start | bytes 786440 | tf_op jit(solution)/shard_map/ppermute | solution.py:68
  40.2 9.3 %collective-permute-start.5 = (bf16[2,128,4,128]{1,3,2,0:T(8,128)(2,1)}, bf16[2,128,4,128]{1,3,2,0:T(8,128)(2,1)}, u32[]{:S(2)}, u32[]{:S(2)}) collective-permute-start(bf16[2,128,4,128]{1,3,2,0:T(8,128)(2,1)} %collective-permute-done.4), channel_id=1, source_target_pairs={{8,0},{16,8},{24,16},{32,24},{40,32},{48,40},{56,48},{64,56},{72,6... | collective-permute-start | bytes 786440 | tf_op jit(solution)/shard_map/ppermute | solution.py:68
  43.2 25.8 %collective-permute-start.2 = (bf16[2,128,4,128]{3,1,2,0:T(8,128)(2,1)}, bf16[2,128,4,128]{3,1,2,0:T(8,128)(2,1)}, u32[]{:S(2)}, u32[]{:S(2)}) collective-permute-start(bf16[2,128,4,128]{3,1,2,0:T(8,128)(2,1)} %collective-permute-done.1), channel_id=1, source_target_pairs={{0,8},{8,16},{16,24},{24,32},{32,40},{40,48},{48,56},{56,64},{64,7... | collective-permute-start | bytes 786440 | tf_op jit(solution)/shard_map/ppermute | solution.py:68
  49.5 21.5 %collective-permute-start.6 = (bf16[2,128,4,128]{1,3,2,0:T(8,128)(2,1)}, bf16[2,128,4,128]{1,3,2,0:T(8,128)(2,1)}, u32[]{:S(2)}, u32[]{:S(2)}) collective-permute-start(bf16[2,128,4,128]{1,3,2,0:T(8,128)(2,1)} %collective-permute-done.5), channel_id=1, source_target_pairs={{8,0},{16,8},{24,16},{32,24},{40,32},{48,40},{56,48},{64,56},{72,6... | collective-permute-start | bytes 786440 | tf_op jit(solution)/shard_map/ppermute | solution.py:68
  52.8 25.0 %all-to-all-start.1 = ((f32[8,1,5462]{2,1,0:T(1,128)}), f32[8,1,5462]{2,1,0:T(1,128)S(1)}, u32[]{:S(2)}, u32[]{:S(2)}) async-start(f32[8,1,5462]{2,1,0:T(1,128)} %broadcast_in_dim.44), calls=%async_computation.1 | async-start | bytes 352256 | tf_op jit(solution)/shard_map/all_to_all | solution.py:40
  69.0 14.6 %collective-permute-start.3 = (bf16[2,128,4,128]{3,1,2,0:T(8,128)(2,1)}, bf16[2,128,4,128]{3,1,2,0:T(8,128)(2,1)}, u32[]{:S(2)}, u32[]{:S(2)}) collective-permute-start(bf16[2,128,4,128]{3,1,2,0:T(8,128)(2,1)} %collective-permute-done.2), channel_id=1, source_target_pairs={{0,8},{8,16},{16,24},{24,32},{32,40},{40,48},{48,56},{56,64},{64,7... | collective-permute-start | bytes 786440 | tf_op jit(solution)/shard_map/ppermute | solution.py:68
  71.0 22.9 %collective-permute-start.7 = (bf16[2,128,4,128]{1,3,2,0:T(8,128)(2,1)}, bf16[2,128,4,128]{1,3,2,0:T(8,128)(2,1)}, u32[]{:S(2)}, u32[]{:S(2)}) collective-permute-start(bf16[2,128,4,128]{1,3,2,0:T(8,128)(2,1)} %collective-permute-done.6), channel_id=1, source_target_pairs={{8,0},{16,8},{24,16},{32,24},{40,32},{48,40},{56,48},{64,56},{72,6... | collective-permute-start | bytes 786440 | tf_op jit(solution)/shard_map/ppermute | solution.py:68
  79.4 27.2 %all-to-all-start.2 = ((f32[12,1,5462]{2,1,0:T(1,128)}), f32[12,1,5462]{2,1,0:T(1,128)}, u32[]{:S(2)}, u32[]{:S(2)}) async-start(f32[12,1,5462]{2,1,0:T(1,128)} %copy.193), calls=%async_computation.2 | async-start | bytes 528384 | tf_op jit(solution)/shard_map/all_to_all | solution.py:47
  88.1 7.8 %collective-permute-start.8 = (f32[2,4,128]{2,1,0:T(4,128)S(1)}, f32[2,4,128]{2,1,0:T(4,128)S(1)}, u32[]{:S(2)}, u32[]{:S(2)}) collective-permute-start(f32[2,4,128]{2,1,0:T(4,128)S(1)} %pad_maximum_fusion.2), channel_id=1, source_target_pairs={{8,0},{16,8},{24,16},{32,24},{40,32},{48,40},{56,48},{64,56},{72,6... | collective-permute-start | bytes 12296 | tf_op jit(solution)/shard_map/ppermute | solution.py:68
  89.4 7.4 %collective-permute-start.9 = (f32[2,4,128]{2,1,0:T(4,128)S(1)}, f32[2,4,128]{2,1,0:T(4,128)S(1)}, u32[]{:S(2)}, u32[]{:S(2)}) collective-permute-start(f32[2,4,128]{2,1,0:T(4,128)S(1)} %pad_maximum_fusion.2), channel_id=1, source_target_pairs={{16,0},{24,8},{32,16},{40,24},{48,32},{56,40},{64,48},{72,56},{80,... | collective-permute-start | bytes 12296 | tf_op jit(solution)/shard_map/ppermute | solution.py:68
  90.7 9.1 %collective-permute-start.10 = (f32[2,4,128]{2,1,0:T(4,128)S(1)}, f32[2,4,128]{2,1,0:T(4,128)S(1)}, u32[]{:S(2)}, u32[]{:S(2)}) collective-permute-start(f32[2,4,128]{2,1,0:T(4,128)S(1)} %pad_maximum_fusion.2), channel_id=1, source_target_pairs={{24,0},{32,8},{40,16},{48,24},{56,32},{64,40},{72,48},{80,56},{88,... | collective-permute-start | bytes 12296 | tf_op jit(solution)/shard_map/ppermute | solution.py:68
  92.0 12.2 %collective-permute-start.11 = (f32[2,4,128]{2,1,0:T(4,128)S(1)}, f32[2,4,128]{2,1,0:T(4,128)S(1)}, u32[]{:S(2)}, u32[]{:S(2)}) collective-permute-start(f32[2,4,128]{2,1,0:T(4,128)S(1)} %pad_maximum_fusion.2), channel_id=1, source_target_pairs={{32,0},{40,8},{48,16},{56,24},{64,32},{72,40},{80,48},{88,56},{96,... | collective-permute-start | bytes 12296 | tf_op jit(solution)/shard_map/ppermute | solution.py:68
  94.9 9.3 %copy-start.17 = (bf16[640,4,128]{0,2,1:T(8,128)(2,1)}, bf16[640,4,128]{0,2,1:T(8,128)(2,1)S(1)}, u32[]{:S(2)}) copy-start(bf16[640,4,128]{0,2,1:T(8,128)(2,1)S(1)} %get-tuple-element.47) | copy-start | bytes 1966084
  95.0 25.0 %copy-start.1 = (bf16[640,4,128]{0,2,1:T(8,128)(2,1)}, bf16[640,4,128]{0,2,1:T(8,128)(2,1)S(1)}, u32[]{:S(2)}) copy-start(bf16[640,4,128]{0,2,1:T(8,128)(2,1)S(1)} %get-tuple-element.46) | copy-start | bytes 1966084
  115.1 9.0 %all-to-all-start.3 = ((f32[8,2,128]{2,1,0:T(2,128)}), f32[8,2,128]{2,1,0:T(2,128)}, u32[]{:S(2)}, u32[]{:S(2)}) async-start(f32[8,2,128]{2,1,0:T(2,128)} %broadcast_in_dim.45), calls=%async_computation.3 | async-start | bytes 16384 | tf_op jit(solution)/shard_map/all_to_all | solution.py:62
  129.6 39.8 %all-to-all-start.4 = ((f32[96,1,683]{2,1,0:T(1,128)}), f32[96,1,683]{2,1,0:T(1,128)}, u32[]{:S(2)}, u32[]{:S(2)}) async-start(f32[96,1,683]{2,1,0:T(1,128)} %all_to_all.45), calls=%async_computation.4 | async-start | bytes 589824 | tf_op jit(solution)/shard_map/all_to_all | solution.py:54
  153.8 24.1 %copy-start.13 = (bf16[128,512]{0,1:T(8,128)(2,1)S(1)}, bf16[128,512]{0,1:T(8,128)(2,1)}, u32[]{:S(2)}) copy-start(bf16[128,512]{0,1:T(8,128)(2,1)} %copy-done.12) | copy-start | bytes 393220
  153.9 25.3 %copy-start.4 = (f32[65536]{0:T(1024)S(1)}, f32[65536]{0:T(1024)}, u32[]{:S(2)}) copy-start(f32[65536]{0:T(1024)} %copy-done.3) | copy-start | bytes 786436
  171.7 25.9 %all-to-all-start.5 = ((f32[96,1,683]{2,1,0:T(1,128)}), f32[96,1,683]{2,1,0:T(1,128)S(1)}, u32[]{:S(2)}, u32[]{:S(2)}) async-start(f32[96,1,683]{2,1,0:T(1,128)} %copy.217), calls=%async_computation.5 | async-start | bytes 589824 | tf_op jit(solution)/shard_map/all_to_all | solution.py:55
  180.5 18.1 %copy-start.11 = (bf16[128,512]{1,0:T(8,128)(2,1)S(1)}, bf16[128,512]{1,0:T(8,128)(2,1)}, u32[]{:S(2)}) copy-start(bf16[128,512]{1,0:T(8,128)(2,1)} %param.9) | copy-start | bytes 393220
  180.8 18.9 %copy-start.16 = (bf16[128,512]{1,0:T(8,128)(2,1)S(1)}, bf16[128,512]{1,0:T(8,128)(2,1)}, u32[]{:S(2)}) copy-start(bf16[128,512]{1,0:T(8,128)(2,1)} %param.8) | copy-start | bytes 393220
  (10 other events, 24.2 us)
